TPU v7x, 128 devices: a whole 4x4x4 slice. The times are simulated.
128 devices in a mesh: pipe: 2 (over x_lo), ctx: 16 (over x_hi, z, core), tp: 4 (over y).
Axes of the slice: x: 4 (x_hi: 2, x_lo: 2; x = x_hi * 2 + x_lo), y: 4, z: 4, core: 2. Of those that a mesh axis runs over, the one named last changes fastest.
Arguments:
- value_input: bfloat16 [2, 2048, 16384], P('pipe', 'ctx', 'tp'), may hold values from -6 to 6
- state_input: bfloat16 [2, 2048, 4096], P('pipe', 'ctx', 'tp'), may hold values from -6 to 6
- step_raw: bfloat16 [2, 2048, 256], P('pipe', 'ctx', 'tp'), may hold values from -4 to 11
- upstream: bfloat16 [2, 2048, 16384], P('pipe', 'ctx', 'tp'), may hold values from -6 to 6
- step_bias: float32 [256], P('tp'), may hold values from -6.9 to -2.3
- decay_log: float32 [256], P('tp'), may hold values from 0 to 2.77
- skip_gain: float32 [256], P('tp'), may hold values from 0.5 to 2
- value_kernel: float32 [4, 16384], P(None, 'tp'), may hold values from -0.5 to 0.5
- value_offset: float32 [16384], P('tp'), may hold values from -0.5 to 0.5
- state_kernel: float32 [4, 4096], P(None, 'tp'), may hold values from -0.5 to 0.5
- state_offset: float32 [4096], P('tp'), may hold values from -0.5 to 0.5
Outputs:
- value_grad: bfloat16 [2, 2048, 16384], P('pipe', 'ctx', 'tp')
- state_grad: bfloat16 [2, 2048, 4096], P('pipe', 'ctx', 'tp')
- step_grad: bfloat16 [2, 2048, 256], P('pipe', 'ctx', 'tp')
All inputs are finite; a program needn't handle non-finite values.
Results may differ from a plain program's by a relative error of at most 0.011.
Values may be sent and summed in bfloat16 or wider, within the bound.
No kernel may reach another device: no remote copies, remote signals or barrier semaphores. Data moves between devices by JAX's collectives and lax.ppermute only.
A program may use at most 128 MiB of HBM per device.

v0:
```python
import functools

import jax
import jax.numpy as jnp
from jax import lax
from jax.experimental import pallas as pl
from jax.experimental.pallas import tpu as pltpu
from jax.sharding import PartitionSpec as P

HEAD_DIM = 64
STATE = 256
CONV = 4
CORES = 2
RING = 4
HALVES = 2
f32 = jnp.float32
bf16 = jnp.bfloat16
HIGH = lax.Precision.HIGHEST

TOK = 128
ROWS = TOK * CORES
HEADS = 32
WIDE = HEADS * HEAD_DIM
PART = WIDE // RING
TAIL = 16


def nn(a, b, precision=None):
    return lax.dot_general(
        a, b, (((1,), (0,)), ((), ())), precision=precision, preferred_element_type=f32
    )


def nt(a, b):
    return lax.dot_general(a, b, (((1,), (1,)), ((), ())), preferred_element_type=f32)


def iota(shape, axis):
    return lax.broadcasted_iota(jnp.int32, shape, axis)


def split3(x):
    high = x.astype(bf16).astype(f32)
    rest = x - high
    mid = rest.astype(bf16).astype(f32)
    low = rest - mid
    part = iota(x.shape, 1) // HEADS
    picked = jnp.where(part == 0, high, jnp.where(part == 1, mid, jnp.where(part == 2, low, 0.0)))
    return picked.astype(bf16)


def spread(width, start=0):
    rows = iota((128, width), 0) % HEADS
    cols = (iota((128, width), 1) + start) // HEAD_DIM
    return jnp.where(rows == cols, 1.0, 0.0).astype(bf16)


def head_sum(x, ones):
    high = x.astype(bf16)
    low = (x - high.astype(f32)).astype(bf16)
    return nt(high, ones) + nt(low, ones)


def softplus(x):
    u = jnp.exp(-jnp.abs(x))
    small = u * (1.0 - u * (0.5 - u * (1.0 / 3.0 - u * 0.25)))
    return jnp.maximum(x, 0.0) + jnp.where(u < 0.01, small, jnp.log(1.0 + u))


def sigmoid(x):
    return 1.0 / (1.0 + jnp.exp(-x))


def first_kernel(
    ids, v_own, v_in, s_own, s_in, r_own, r_in, halo_a, halo_b, bias, rate_log,
    v_tap, v_off, s_tap, s_off,
    m0, m1, m2, m3, x_out, xs_out, sx_out, bc_out, sbc_out, delta_out, within_out, sig_out,
    buf, sbuf, raw, wide,
):
    core, ring = ids[0], ids[1]
    mine = pl.multiple_of(core * TOK, TOK)
    other = pl.multiple_of((1 - core) * TOK, TOK)
    raw[pl.ds(mine, TOK), :] = r_own[...].astype(f32)
    raw[pl.ds(other, TOK), :] = r_in[...].astype(f32)
    pre = raw[...] + bias[...]
    delta = softplus(pre)
    rate = -jnp.exp(rate_log[...])
    lower = jnp.where(iota((ROWS, ROWS), 0) >= iota((ROWS, ROWS), 1), 1.0, 0.0).astype(f32)
    within = nn(lower, delta * rate, HIGH)
    delta_out[...] = delta
    within_out[...] = within
    sig_out[...] = sigmoid(pre)
    total = within[ROWS - 1 : ROWS, :]
    scale = split3(delta * jnp.exp(total - within))
    wide[...] = nn(scale, spread(WIDE))

    buf[pl.ds(pl.multiple_of(8 + mine, 8), TOK), :] = v_own[...].astype(f32)
    buf[pl.ds(pl.multiple_of(8 + other, 8), TOK), :] = v_in[...].astype(f32)
    sbuf[pl.ds(pl.multiple_of(8 + mine, 8), TOK), :] = s_own[...].astype(f32)
    sbuf[pl.ds(pl.multiple_of(8 + other, 8), TOK), :] = s_in[...].astype(f32)
    halo = halo_a[...].astype(f32) + halo_b[...].astype(f32)
    buf[0:8, :] = halo[8:16, :WIDE]
    sbuf[0:8, :] = halo[8:16, WIDE:]

    def conv(source, tap, off, cols):
        acc = off[:, cols] + tap[0:1, cols] * source[5 : 5 + ROWS, cols]
        for j in range(1, CONV):
            acc = acc + tap[j : j + 1, cols] * source[5 + j : 5 + j + ROWS, cols]
        sig = sigmoid(acc)
        return acc * sig, sig * (1.0 + acc * (1.0 - sig))

    def state_block(b, carry):
        cols = pl.ds(pl.multiple_of(b * 128, 128), 128)
        post, slope = conv(sbuf, s_tap, s_off, cols)
        bc_out[:, cols] = post.astype(bf16)
        sbc_out[:, cols] = slope.astype(bf16)
        return carry

    lax.fori_loop(0, 4, state_block, 0)

    def value_block(b, carry):
        cols = pl.ds(pl.multiple_of(b * 128, 128), 128)
        post, slope = conv(buf, v_tap, v_off, cols)
        post = post.astype(bf16)
        x_out[:, cols] = post
        sx_out[:, cols] = slope.astype(bf16)
        xs_out[:, cols] = (post.astype(f32) * wide[:, cols]).astype(bf16)
        return carry

    lax.fori_loop(0, 16, value_block, 0)

    write_t = bc_out[:, :STATE].astype(f32).T.astype(bf16)
    total_parts = split3(jnp.broadcast_to(total, (8, 128)))
    for slot, out in enumerate((m0, m1, m2, m3)):
        start = pl.multiple_of(((ring + slot) % RING) * PART, PART)
        out[0:STATE, :] = nn(write_t, xs_out[:, pl.ds(start, PART)]).astype(bf16)
        full = nn(total_parts, spread(PART, start))[0:1, :]
        high = full.astype(bf16).astype(f32)
        mid = (full - high).astype(bf16).astype(f32)
        low = full - high - mid
        row = iota((TAIL, PART), 0)
        out[STATE : STATE + TAIL, :] = jnp.where(
            row == 0, high, jnp.where(row == 1, mid, jnp.where(row == 2, low, 0.0))
        ).astype(bf16)


def ring_totals(parts):
    out = []
    for part in parts:
        rows = part[STATE : STATE + TAIL, :].astype(f32)
        out.append(rows[0:1] + rows[1:2] + rows[2:3])
    return out


def between(totals, places, low, high):
    out = jnp.zeros_like(totals[0])
    for total, place in zip(totals, places):
        inside = jnp.logical_and(place > low, place < high)
        out = out + total * jnp.where(inside, 1.0, 0.0)
    return out


def edge_kernel(back, ids, m0, m1, m2, m3, d0, d1, d2, d3, out):
    ring = ids[1]
    places = [(ring + RING - s) % RING for s in range(RING)]
    totals = ring_totals((m0, m1, m2, m3))
    acc = jnp.zeros((STATE, PART), f32)
    for src, place in zip((d0, d1, d2, d3), places):
        if back:
            weight = jnp.exp(between(totals, places, -1, place))
        else:
            weight = jnp.exp(between(totals, places, place, RING))
        acc = acc + weight * src[0:STATE, :].astype(f32)
    out[...] = acc.astype(bf16)


def scan_kernel(back, ids, m0, m1, m2, m3, d0, d1, d2, d3, edge, o0, o1, o2, o3):
    ring = ids[1]
    places = [(ring + RING - s) % RING for s in range(RING)]
    totals = ring_totals((m0, m1, m2, m3))
    for out, here in zip((o0, o1, o2, o3), places):
        if back:
            weight = jnp.exp(between(totals, places, here, RING))
        else:
            weight = jnp.exp(between(totals, places, -1, here))
        acc = weight * edge[...].astype(f32)
        for src, place in zip((d0, d1, d2, d3), places):
            if back:
                gap = between(totals, places, here, place)
                live = place > here
            else:
                gap = between(totals, places, place, here)
                live = place < here
            weight = jnp.exp(gap) * jnp.where(live, 1.0, 0.0)
            acc = acc + weight * src[0:STATE, :].astype(f32)
        out[...] = acc.astype(bf16)


def second_kernel(ids, g_own, g_in, bc, within, d0, d1, d2, d3, dy_out, dye_out, wide):
    core, ring = ids[0], ids[1]
    mine = pl.multiple_of(core * TOK, TOK)
    other = pl.multiple_of((1 - core) * TOK, TOK)
    dy_out[pl.ds(mine, TOK), :] = g_own[...]
    dy_out[pl.ds(other, TOK), :] = g_in[...]
    wide[...] = nn(split3(jnp.exp(within[...])), spread(WIDE))
    read_t = bc[:, STATE:].astype(f32).T.astype(bf16)

    def block(b, carry):
        cols = pl.ds(pl.multiple_of(b * 128, 128), 128)
        dye_out[:, cols] = (dy_out[:, cols].astype(f32) * wide[:, cols]).astype(bf16)
        return carry

    lax.fori_loop(0, 16, block, 0)
    for slot, out in enumerate((d0, d1, d2, d3)):
        start = pl.multiple_of(((ring + slot) % RING) * PART, PART)
        out[...] = nn(read_t, dye_out[:, pl.ds(start, PART)]).astype(bf16)


def inner_kernel(
    x, dy, bc, delta, within, u_out, dbc_out, diff_out, wide, within_t, row_sum, bcs, dbcs
):
    half = ROWS // 2
    wide[...] = nn(split3(delta[...]), spread(WIDE))
    within_t[...] = within[...].T
    write, read = bc[:, :STATE], bc[:, STATE:]
    bcs[...] = nt(write, read)
    dbcs[...] = jnp.zeros_like(dbcs)
    diff_out[...] = jnp.zeros_like(diff_out)
    keep = iota((half, half), 1) >= iota((half, half), 0)
    lanes = iota((ROWS, 128), 1)
    first = lanes < HEAD_DIM

    def pair(b, carry):
        cols = pl.ds(pl.multiple_of(b * 128, 128), 128)
        xd = (x[:, cols].astype(f32) * wide[:, cols]).astype(bf16)
        grad = dy[:, cols]
        zero = jnp.zeros_like(grad)
        top = jnp.zeros((half, 128), f32)
        bot = jnp.zeros((half, 128), f32)
        col_total = jnp.zeros((ROWS, 128), f32)
        for e in range(2):
            h = 2 * b + e
            g = jnp.where(first, grad, zero) if e == 0 else jnp.where(first, zero, grad)
            wq = within_t[pl.ds(h, 1), :]
            ws = jnp.sum(jnp.where(lanes == h, within[...], 0.0), axis=1, keepdims=True)
            diff00 = jnp.where(keep, wq[:, :half] - ws[:half], -jnp.inf)
            diff01 = wq[:, half:] - ws[:half]
            diff11 = jnp.where(keep, wq[:, half:] - ws[half:], -jnp.inf)
            dm0 = nt(xd[:half], g)
            dm11 = nt(xd[half:], g[half:])
            sums = []
            rows0 = jnp.zeros((1, half), f32)
            rows1 = jnp.zeros((1, half), f32)
            products = []
            for dif, dm, r, c in (
                (diff00, dm0[:, :half], 0, 0),
                (diff01, dm0[:, half:], 0, 1),
                (diff11, dm11, 1, 1),
            ):
                rs, cs = pl.ds(r * half, half), pl.ds(c * half, half)
                decay = jnp.exp(dif)
                m = decay * bcs[rs, cs]
                p = dm * m
                dbcs[rs, cs] = dbcs[rs, cs] + dm * decay
                total = jnp.sum(p, axis=0, keepdims=True)
                if c == 0:
                    rows0 = rows0 + total
                else:
                    rows1 = rows1 + total
                sums.append(jnp.sum(p, axis=1, keepdims=True))
                products.append(m.astype(bf16))
            row_sum[pl.ds(h, 1), :] = jnp.concatenate([rows0, rows1], axis=1)
            top = top + nn(products[0], g[:half]) + nn(products[1], g[half:])
            bot = bot + nn(products[2], g[half:])
            col = jnp.concatenate([sums[0] + sums[1], sums[2]], axis=0)
            col_total = col_total + jnp.where(lanes % HEADS == h, col, 0.0)
        u_out[:half, cols] = top
        u_out[half:, cols] = bot
        diff_out[...] = diff_out[...] - col_total
        return carry

    for t in range(1, 4):
        row_sum[t * HEADS : (t + 1) * HEADS, :] = jnp.zeros((HEADS, ROWS), f32)
    lax.fori_loop(0, 16, pair, 0)
    for t in range(1, 4):
        row_sum[t * HEADS : (t + 1) * HEADS, :] = row_sum[0:HEADS, :]
    diff_out[...] = diff_out[...] + row_sum[...].T
    grad = dbcs[...]
    dbc_out[:, :STATE] = nn(grad.astype(bf16), read)
    dbc_out[:, STATE:] = nn(grad.T.astype(bf16), write)


def carry_kernel(ids, c0, c1, c2, c3, bc, dye, dbc, outer_out, dread_out, carried_out):
    ring = ids[1]
    for slot, src in enumerate((c0, c1, c2, c3)):
        start = pl.multiple_of(((ring + slot) % RING) * PART, PART)
        carried_out[:, pl.ds(start, PART)] = src[...]
    read = bc[:, STATE:]
    dread_out[...] = dbc[:, STATE:] + nt(dye[...], carried_out[...])
    outer = jnp.zeros((ROWS, 128), f32)
    for b in range(4):
        cols = slice(b * PART, (b + 1) * PART)
        part = nn(read, carried_out[:, cols]) * dye[:, cols].astype(f32)
        outer = outer + head_sum(part, spread(PART, b * PART))
    outer_out[...] = outer


def last_kernel(
    ids, g0, g1, g2, g3, carried, bc, x, xs, dy, u_in, sx, sbc, delta, within, sig, diff, outer,
    dread, dbc, rate_log, skip, v_tap, s_tap,
    vg_own, vg_out, sg_own, sg_out, st_own, st_out, head_out,
    gbuf, ebuf, sbuf, dbuf, back, sback,
):
    core, ring = ids[0], ids[1]
    mine = pl.multiple_of(core * TOK, TOK)
    other = pl.multiple_of((1 - core) * TOK, TOK)
    for slot, src in enumerate((g0, g1, g2, g3)):
        start = pl.multiple_of(((ring + slot) % RING) * PART, PART)
        gbuf[:, pl.ds(start, PART)] = src[...]
    write = bc[:, :STATE]
    w = within[...]
    dlt = delta[...]
    total = w[ROWS - 1 : ROWS, :]
    tail_parts = split3(jnp.exp(total - w))
    delta_parts = split3(dlt)
    rsum = jnp.zeros((ROWS, 128), f32)
    vsum = jnp.zeros((ROWS, 128), f32)
    tsum = jnp.zeros((8, 128), f32)
    ebuf[ROWS : ROWS + 8, :] = jnp.zeros((8, WIDE), f32)
    sbuf[ROWS : ROWS + 8, :] = jnp.zeros((8, 2 * STATE), f32)
    for b in range(4):
        cols = slice(b * PART, (b + 1) * PART)
        ones = spread(PART, b * PART)
        grad = gbuf[:, cols]
        through = nn(write, grad)
        rsum = rsum + head_sum(xs[:, cols].astype(f32) * through, ones)
        u = u_in[:, cols] + nn(tail_parts, ones) * through
        vsum = vsum + head_sum(x[:, cols].astype(f32) * u, ones)
        dx = nn(delta_parts, ones) * u + skip[:, cols] * dy[:, cols].astype(f32)
        ebuf[0:ROWS, cols] = dx * sx[:, cols].astype(f32)
        both = jnp.sum(
            grad.astype(f32) * carried[:, cols].astype(f32), axis=0, keepdims=True
        )
        tsum = tsum + head_sum(jnp.broadcast_to(both, (8, PART)), ones)
    dtotal = tsum[0:1, :] * jnp.exp(total)
    ra, rb = iota((ROWS, ROWS), 0), iota((ROWS, ROWS), 1)
    later = jnp.where(rb >= ra, 1.0, 0.0).astype(f32)
    earlier = jnp.where(rb < ra, 1.0, 0.0).astype(f32)
    da = nn(later, diff[...] + outer[...], HIGH) + nn(earlier, rsum, HIGH) + dtotal
    dbuf[...] = ((vsum - jnp.exp(rate_log[...]) * da) * sig[...])
    st_own[...] = dbuf[pl.ds(mine, TOK), :].astype(bf16)
    st_out[...] = dbuf[pl.ds(other, TOK), :].astype(bf16)

    dwrite = dbc[:, :STATE] + nt(xs[...], gbuf[...])
    sbuf[0:ROWS, :STATE] = dwrite * sbc[:, :STATE].astype(f32)
    sbuf[0:ROWS, STATE:] = dread[...] * sbc[:, STATE:].astype(f32)
    head_out[:, :WIDE] = ebuf[0:8, :]
    head_out[:, WIDE:] = sbuf[0:8, :]

    def conv(source, tap, cols):
        acc = tap[CONV - 1 : CONV, cols] * source[0:ROWS, cols]
        for shift in range(1, CONV):
            j = CONV - 1 - shift
            acc = acc + tap[j : j + 1, cols] * source[shift : shift + ROWS, cols]
        return acc

    def value_block(b, carry):
        cols = pl.ds(pl.multiple_of(b * 128, 128), 128)
        back[:, cols] = conv(ebuf, v_tap, cols).astype(bf16)
        return carry

    lax.fori_loop(0, 16, value_block, 0)

    def state_block(b, carry):
        cols = pl.ds(pl.multiple_of(b * 128, 128), 128)
        sback[:, cols] = conv(sbuf, s_tap, cols).astype(bf16)
        return carry

    lax.fori_loop(0, 4, state_block, 0)
    vg_own[...] = back[pl.ds(mine, TOK), :]
    vg_out[...] = back[pl.ds(other, TOK), :]
    sg_own[...] = sback[pl.ds(mine, TOK), :]
    sg_out[...] = sback[pl.ds(other, TOK), :]


def join_kernel(
    ids, v_own, v_in, s_own, s_in, t_own, t_in, e0, e1, v_tap, s_tap, v_out, s_out, t_out
):
    core = ids[0]

    def place(out, own, arrived, width, where):
        here = pl.multiple_of(core * width, width)
        there = pl.multiple_of((1 - core) * width, width)
        out[:, pl.ds(here, width)] = own[...]
        out[:, pl.ds(there, width)] = arrived[...]

    def patch(out, tap, edge, width, group, start):
        cols = slice(group * width, (group + 1) * width)
        rows = edge[:, start : start + width]
        row = iota((TAIL, width), 0)
        acc = out[TOK - TAIL :, cols].astype(f32)
        for shift in range(1, CONV):
            j = CONV - 1 - shift
            for k in range(shift):
                acc = acc + jnp.where(
                    row == TAIL - shift + k, tap[j : j + 1, cols] * rows[k : k + 1], 0.0
                )
        out[TOK - TAIL :, cols] = acc.astype(bf16)

    place(v_out, v_own, v_in, WIDE, core)
    place(s_out, s_own, s_in, 2 * STATE, core)
    for group, edge in enumerate((e0, e1)):
        patch(v_out, v_tap, edge, WIDE, group, 0)
        patch(s_out, s_tap, edge, 2 * STATE, group, WIDE)
    lanes = iota((TOK, HEADS), 1)
    own, arrived = t_own[:, :HEADS].astype(f32), t_in[:, :HEADS].astype(f32)
    low = jnp.where(core == 0, own, arrived)
    high = jnp.where(core == 0, arrived, own)
    t_out[...] = jnp.concatenate([low, high], axis=1).astype(bf16)


def call(kernel, ids, specs, args, outs, scratch=(), name=None):
    def full(shape):
        return pl.BlockSpec(shape, lambda i, s, n=len(shape): (0,) * n)

    in_specs = [full(a.shape) if spec is None else spec for spec, a in zip(specs, args)]
    result = pl.pallas_call(
        kernel,
        grid_spec=pltpu.PrefetchScalarGridSpec(
            num_scalar_prefetch=1,
            grid=(1,),
            in_specs=in_specs,
            out_specs=[full(o[0]) for o in outs],
            scratch_shapes=[pltpu.VMEM(*s) for s in scratch],
        ),
        out_shape=[jax.ShapeDtypeStruct(*o) for o in outs],
        compiler_params=pltpu.CompilerParams(vmem_limit_bytes=56 * 1024 * 1024),
        name=name,
    )(ids, *args)
    return result


def local(
    value_input, state_input, step_raw, upstream, step_bias, decay_log, skip_gain,
    value_kernel, value_offset, state_kernel, state_offset,
):
    count = lax.axis_size("ctx")
    index = lax.axis_index("ctx")
    core = index % CORES
    ring = (index // CORES) % RING
    ids = jnp.stack([core, ring]).astype(jnp.int32)
    chips = count // CORES

    def send(x, pairs):
        return lax.ppermute(x, "ctx", pairs)

    swap_pairs = [(i, i ^ 1) for i in range(count)]

    def around(i, shift):
        half, place, c = i // (RING * CORES), (i // CORES) % RING, i % CORES
        return (half * RING + (place + shift) % RING) * CORES + c

    def ring_send(x, shift):
        return send(x, [(i, around(i, shift)) for i in range(count)])

    def pick(x, group, width):
        return lax.dynamic_slice_in_dim(x, group * width, width, 1)

    g = upstream[0]
    g_own = lax.ppermute(pick(g, core, WIDE), "pipe", [(0, 1), (1, 0)])
    g_in = lax.ppermute(
        pick(g, 1 - core, WIDE),
        ("pipe", "ctx"),
        [(p * count + i, (1 - p) * count + (i ^ 1)) for p in range(2) for i in range(count)],
    )
    v, s, r = value_input[0], state_input[0], step_raw[0]
    v_in = send(pick(v, 1 - core, WIDE), swap_pairs)
    s_in = send(pick(s, 1 - core, 2 * STATE), swap_pairs)
    r_own = jnp.tile(pick(r, core, HEADS), (1, 4))
    r_in = send(jnp.tile(pick(r, 1 - core, HEADS), (1, 4)), swap_pairs)

    def tail(group):
        return jnp.concatenate(
            [
                v[TOK - TAIL :, group * WIDE : (group + 1) * WIDE],
                s[TOK - TAIL :, group * 2 * STATE : (group + 1) * 2 * STATE],
            ],
            axis=1,
        )

    halo_a = send(tail(1), [(k * 2 + 1, k * 2 + 3) for k in range(chips - 1)])
    halo_b = send(tail(0), [(k * 2 + 1, k * 2 + 2) for k in range(chips - 1)])

    row = lambda x: x.reshape(1, -1)
    bias = jnp.tile(row(lax.dynamic_slice_in_dim(step_bias, core * HEADS, HEADS)), (1, 4))
    rate_log = jnp.tile(row(lax.dynamic_slice_in_dim(decay_log, core * HEADS, HEADS)), (1, 4))
    skip = row(
        jnp.repeat(lax.dynamic_slice_in_dim(skip_gain, core * HEADS, HEADS), HEAD_DIM)
    )

    def group_block(rows, width):
        return pl.BlockSpec((rows, width), lambda i, ids: (0, ids[0]))

    tall = (ROWS, WIDE)
    narrow = (ROWS, 128)
    message = ((STATE + TAIL, PART), bf16)
    state_part = ((STATE, PART), bf16)
    v_spec, s_spec = group_block(CONV, WIDE), group_block(CONV, 2 * STATE)
    (m0, m1, m2, m3, x, xs, sx, bc, sbc, delta, within, sig) = call(
        first_kernel,
        ids,
        [group_block(TOK, WIDE), None, group_block(TOK, 2 * STATE)] + [None] * 7
        + [v_spec, group_block(1, WIDE), s_spec, group_block(1, 2 * STATE)],
        [v, v_in, s, s_in, r_own, r_in, halo_a, halo_b, bias, rate_log,
         value_kernel, row(value_offset), state_kernel, row(state_offset)],
        [message] * 4
        + [(tall, bf16)] * 3
        + [((ROWS, 2 * STATE), bf16)] * 2
        + [(narrow, f32)] * 3,
        [((ROWS + 8, WIDE), f32), ((ROWS + 8, 2 * STATE), f32), (narrow, f32), (tall, f32)],
        name="first",
    )

    def exchange(parts):
        return [parts[0]] + [ring_send(parts[k], k) for k in range(1, RING)]

    def exchange_back(parts):
        return [parts[0]] + [ring_send(parts[k], -k) for k in range(1, RING)]

    per_half = count // HALVES
    marks = exchange((m0, m1, m2, m3))
    edge = call(
        functools.partial(edge_kernel, False), ids, [None] * 8, marks + marks, [state_part],
        name="edge_forward",
    )[0]
    edge = send(edge, [(i, i + per_half) for i in range(per_half)])
    carried = exchange_back(
        call(
            functools.partial(scan_kernel, False), ids, [None] * 9, marks + marks + [edge],
            [state_part] * 4, name="scan_forward",
        )
    )

    d0, d1, d2, d3, dy, dye = call(
        second_kernel, ids, [None] * 4, [g_own, g_in, bc, within],
        [state_part] * 4 + [(tall, bf16)] * 2, [(tall, f32)], name="second",
    )
    grads = exchange((d0, d1, d2, d3))
    edge_back = call(
        functools.partial(edge_kernel, True), ids, [None] * 8, marks + grads, [state_part],
        name="edge_back",
    )[0]
    edge_back = send(edge_back, [(i + per_half, i) for i in range(per_half)])
    back = exchange_back(
        call(
            functools.partial(scan_kernel, True), ids, [None] * 9, marks + grads + [edge_back],
            [state_part] * 4, name="scan_back",
        )
    )

    u, dbc, diff = call(
        lambda ids, *refs: inner_kernel(*refs), ids, [None] * 5, [x, dy, bc, delta, within],
        [(tall, f32), ((ROWS, 2 * STATE), f32), (narrow, f32)],
        [(tall, f32), ((128, ROWS), f32), ((128, ROWS), f32), ((ROWS, ROWS), f32),
         ((ROWS, ROWS), f32)],
        name="inner",
    )
    outer, dread, held = call(
        carry_kernel, ids, [None] * 7, list(carried) + [bc, dye, dbc],
        [(narrow, f32), ((ROWS, STATE), f32), ((STATE, WIDE), bf16)], name="carry",
    )
    edge_shape = ((8, WIDE + 2 * STATE), f32)
    vg_own, vg_out, sg_own, sg_out, st_own, st_out, head = call(
        last_kernel,
        ids,
        [None] * 21 + [v_spec, s_spec],
        list(back)
        + [held, bc, x, xs, dy, u, sx, sbc, delta, within, sig, diff, outer, dread, dbc,
           rate_log, skip, value_kernel, state_kernel],
        [((TOK, WIDE), bf16)] * 2 + [((TOK, 2 * STATE), bf16)] * 2 + [((TOK, 128), bf16)] * 2
        + [edge_shape],
        [((STATE, WIDE), bf16), ((ROWS + 8, WIDE), f32), ((ROWS + 8, 2 * STATE), f32),
         (narrow, f32), (tall, bf16), ((ROWS, 2 * STATE), bf16)],
        name="last",
    )
    vg_in, sg_in, st_in = send(vg_out, swap_pairs), send(sg_out, swap_pairs), send(st_out, swap_pairs)
    e0 = send(head, [(k * 2, k * 2 - 1) for k in range(1, chips)])
    e1 = send(head, [(k * 2 + 1, k * 2 - 1) for k in range(1, chips)])
    value_out, state_out, step_out = call(
        join_kernel,
        ids,
        [None] * 10,
        [vg_own, vg_in, sg_own, sg_in, st_own, st_in, e0, e1, value_kernel, state_kernel],
        [((TOK, 2 * WIDE), bf16), ((TOK, 4 * STATE), bf16), ((TOK, 2 * HEADS), bf16)],
        name="join",
    )
    return value_out[None], state_out[None], step_out[None]


def solution(mesh):
    wide = P("pipe", "ctx", "tp")
    placed = (wide, wide, wide, wide, P("tp"), P("tp"), P("tp"), P(None, "tp"), P("tp"), P(None, "tp"), P("tp"))
    return jax.shard_map(
        local, mesh=mesh, in_specs=placed, out_specs=(wide, wide, wide), check_vma=False
    )
```

profile of v0, /device:TPU:15, one launch (start us, length us, event | category | flops | bytes accessed | tf_op | source)
XLA Modules:
  0.0 144.7 jit_solution(8510221962109675122)
XLA Ops:
  6.1 1.3 fusion.1
  9.0 3.5 %collective-permute-start.3 = (bf16[16,2560]{1,0:T(8,128)(2,1)}, bf16[16,2560]{1,0:T(8,128)(2,1)S(1)}, u32[]{:S(2)}, u32[]{:S(2)}) collective-permute-start(bf16[16,2560]{1,0:T(8,128)(2,1)} %pad_maximum_fusion), channel_id=1, source_target_pairs={{4,12},{12,20},{20,28},{28,36},{36,44},{44,52},{52,60},{5,13},{13,... | collective-permute-start | bytes 245768 | tf_op jit(solution)/shard_map/ppermute | solution.py:455
  18.9 4.0 %collective-permute-start.4 = (bf16[16,2560]{1,0:T(8,128)(2,1)}, bf16[16,2560]{1,0:T(8,128)(2,1)S(1)}, u32[]{:S(2)}, u32[]{:S(2)}) collective-permute-start(bf16[16,2560]{1,0:T(8,128)(2,1)} %pad_maximum_fusion.1), channel_id=1, source_target_pairs={{4,8},{12,16},{20,24},{28,32},{36,40},{44,48},{52,56},{5,9},{13,17... | collective-permute-start | bytes 245768 | tf_op jit(solution)/shard_map/ppermute | solution.py:455
  25.6 10.8 %first.1 = (bf16[272,512]{1,0:T(8,128)(2,1)}, bf16[272,512]{1,0:T(8,128)(2,1)}, bf16[272,512]{1,0:T(8,128)(2,1)}, bf16[272,512]{1,0:T(8,128)(2,1)}, bf16[256,204...) custom-call(s32[2]{0:T(128)} %pad_add_fusion.ids, ...), custom_call_target="tpu_custom_call" | custom-call | tf_op jit(solution)/shard_map/first/pallas_call | solution.py:427
  36.3 1.4 collective-permute-start.5
  37.8 2.5 %collective-permute-start.7 = (bf16[272,512]{1,0:T(8,128)(2,1)}, bf16[272,512]{1,0:T(8,128)(2,1)S(1)}, u32[]{:S(2)}, u32[]{:S(2)}) collective-permute-start(bf16[272,512]{1,0:T(8,128)(2,1)} %get-tuple-element.48), channel_id=1, source_target_pairs={{0,24},{4,28},{8,0},{12,4},{16,8},{20,12},{24,16},{28,20},{32,56},... | collective-permute-start | bytes 835592 | tf_op jit(solution)/shard_map/ppermute | solution.py:455
  41.3 4.8 %second.1 = (bf16[256,512]{1,0:T(8,128)(2,1)}, bf16[256,512]{1,0:T(8,128)(2,1)}, bf16[256,512]{1,0:T(8,128)(2,1)}, bf16[256,512]{1,0:T(8,128)(2,1)}, bf16[256,20...) custom-call(s32[2]{0:T(128)} %pad_add_fusion.ids, bf16[128,2048]{1,0:T(8,128)(2,1)} %copy-done.7, bf16[128,2048]{1,0:T(8,128)(2,1)} %copy-done.8, ...), custom_call_target="tpu_custom_call" | custom-call | tf_op jit(solution)/shard_map/second/pallas_call | solution.py:427
  46.1 2.0 %collective-permute-start.11 = (bf16[256,512]{1,0:T(8,128)(2,1)}, bf16[256,512]{1,0:T(8,128)(2,1)S(1)}, u32[]{:S(2)}, u32[]{:S(2)}) collective-permute-start(bf16[256,512]{1,0:T(8,128)(2,1)} %get-tuple-element.53), channel_id=1, source_target_pairs={{0,16},{4,20},{8,24},{12,28},{16,0},{20,4},{24,8},{28,12},{32,48},... | collective-permute-start | bytes 786440 | tf_op jit(solution)/shard_map/ppermute | solution.py:455
  50.2 3.2 %edge_forward.1 = bf16[256,512]{1,0:T(8,128)(2,1)} custom-call(s32[2]{0:T(128)} %pad_add_fusion.ids, bf16[272,512]{1,0:T(8,128)(2,1)} %get-tuple-element.45.m0.d0, bf16[272,512]{1,0:T(8,128)(2,1)} %copy-done, bf16[272,512]{1,0:T(8,128)(2,1)} %copy-done.1, bf16[272,512]{1,0:T(8,128)(2,1)} %copy-done.2, bf16[272,512]{1,0:T(8,128)(2,1)} %get-tuple-element.45.m0.d0, ...), custom_call_target="tpu_custom_call" | custom-call | tf_op jit(solution)/shard_map/edge_forward/pallas_call | solution.py:427
  56.8 3.1 %edge_back.1 = bf16[256,512]{1,0:T(8,128)(2,1)} custom-call(s32[2]{0:T(128)} %pad_add_fusion.ids, bf16[272,512]{1,0:T(8,128)(2,1)} %get-tuple-element.45.m0.d0, bf16[272,512]{1,0:T(8,128)(2,1)} %copy-done, bf16[272,512]{1,0:T(8,128)(2,1)} %copy-done.1, bf16[272,512]{1,0:T(8,128)(2,1)} %copy-done.2, bf16[256,512]{1,0:T(8,128)(2,1)} %get-tuple-element.51.d0, ...), custom_call_target="tpu_custom_call" | custom-call | tf_op jit(solution)/shard_map/edge_back/pallas_call | solution.py:427
  60.0 17.2 %collective-permute-start.13 = (bf16[256,512]{1,0:T(8,128)(2,1)}, bf16[256,512]{1,0:T(8,128)(2,1)S(1)}, u32[]{:S(2)}, u32[]{:S(2)}) collective-permute-start(bf16[256,512]{1,0:T(8,128)(2,1)} %edge_back.1), channel_id=1, source_target_pairs={{32,0},{36,4},{40,8},{44,12},{48,16},{52,20},{56,24},{60,28},{33,1... | collective-permute-start | bytes 786440 | tf_op jit(solution)/shard_map/ppermute | solution.py:455
  77.9 4.2 %scan_forward.1 = (bf16[256,512]{1,0:T(8,128)(2,1)}, bf16[256,512]{1,0:T(8,128)(2,1)}, bf16[256,512]{1,0:T(8,128)(2,1)}, bf16[256,512]{1,0:T(8,128)(2,1)}) custom-call(s32[2]{0:T(128)} %pad_add_fusion.ids, bf16[272,512]{1,0:T(8,128)(2,1)} %get-tuple-element.45.m0.d0, bf16[272,512]{1,0:T(8,128)(2,1)} %copy-done, bf16[272,512]{1,0:T(8,128)(2,1)} %copy-done.1, ...), custom_call_target="tpu_custom_call" | custom-call | tf_op jit(solution)/shard_map/scan_forward/pallas_call | solution.py:427
  82.1 3.3 %collective-permute-start.18 = (bf16[256,512]{1,0:T(8,128)(2,1)}, bf16[256,512]{1,0:T(8,128)(2,1)S(1)}, u32[]{:S(2)}, u32[]{:S(2)}) collective-permute-start(bf16[256,512]{1,0:T(8,128)(2,1)} %get-tuple-element.60), channel_id=1, source_target_pairs={{0,24},{4,28},{8,0},{12,4},{16,8},{20,12},{24,16},{28,20},{32,56},... | collective-permute-start | bytes 786440 | tf_op jit(solution)/shard_map/ppermute | solution.py:455
  86.7 4.1 %scan_back.1 = (bf16[256,512]{1,0:T(8,128)(2,1)}, bf16[256,512]{1,0:T(8,128)(2,1)}, bf16[256,512]{1,0:T(8,128)(2,1)}, bf16[256,512]{1,0:T(8,128)(2,1)}) custom-call(s32[2]{0:T(128)} %pad_add_fusion.ids, bf16[272,512]{1,0:T(8,128)(2,1)} %get-tuple-element.45.m0.d0, bf16[272,512]{1,0:T(8,128)(2,1)} %copy-done, bf16[272,512]{1,0:T(8,128)(2,1)} %copy-done.1, ...), custom_call_target="tpu_custom_call" | custom-call | tf_op jit(solution)/shard_map/scan_back/pallas_call | solution.py:427
  90.8 2.1 %collective-permute-start.14 = (bf16[256,512]{1,0:T(8,128)(2,1)}, bf16[256,512]{1,0:T(8,128)(2,1)S(1)}, u32[]{:S(2)}, u32[]{:S(2)}) collective-permute-start(bf16[256,512]{1,0:T(8,128)(2,1)} %get-tuple-element.56), channel_id=1, source_target_pairs={{0,24},{4,28},{8,0},{12,4},{16,8},{20,12},{24,16},{28,20},{32,56},... | collective-permute-start | bytes 786440 | tf_op jit(solution)/shard_map/ppermute | solution.py:455
  92.9 1.8 %collective-permute-start.15 = (bf16[256,512]{1,0:T(8,128)(2,1)}, bf16[256,512]{1,0:T(8,128)(2,1)S(1)}, u32[]{:S(2)}, u32[]{:S(2)}) collective-permute-start(bf16[256,512]{1,0:T(8,128)(2,1)} %get-tuple-element.57), channel_id=1, source_target_pairs={{0,16},{4,20},{8,24},{12,28},{16,0},{20,4},{24,8},{28,12},{32,48},... | collective-permute-start | bytes 786440 | tf_op jit(solution)/shard_map/ppermute | solution.py:455
  95.5 13.1 %inner.1 = (f32[256,2048]{1,0:T(8,128)}, f32[256,512]{1,0:T(8,128)}, f32[256,128]{1,0:T(8,128)}) custom-call(s32[2]{0:T(128)} %pad_add_fusion.ids, bf16[256,2048]{1,0:T(8,128)(2,1)} %get-tuple-element.64.refs_0_.x, bf16[256,2048]{1,0:T(8,128)(2,1)} %get-tuple-element.65.refs_1_.dy, bf16[256,512]{1,0:T(8,128)(2,1)} %get-tuple-element.49.bc.refs_2_, ...), custom_call_target="tpu_custom_call" | custom-call | tf_op jit(solution)/shard_map/inner/pallas_call | solution.py:427
  109.3 5.2 %carry.1 = (f32[256,128]{1,0:T(8,128)}, f32[256,256]{1,0:T(8,128)}, bf16[256,2048]{1,0:T(8,128)(2,1)}) custom-call(s32[2]{0:T(128)} %pad_add_fusion.ids, bf16[256,512]{1,0:T(8,128)(2,1)} %get-tuple-element.59.c0, bf16[256,512]{1,0:T(8,128)(2,1)} %copy-done.13, bf16[256,512]{1,0:T(8,128)(2,1)} %copy-done.15, bf16[256,512]{1,0:T(8,128)(2,1)} %copy-done.16, ...), custom_call_target="tpu_custom_call" | custom-call | tf_op jit(solution)/shard_map/carry/pallas_call | solution.py:427
  115.4 11.0 %last.1 = (bf16[128,2048]{1,0:T(8,128)(2,1)}, bf16[128,2048]{1,0:T(8,128)(2,1)}, bf16[128,512]{1,0:T(8,128)(2,1)}, bf16[128,512]{1,0:T(8,128)(2,1)}, bf16[128,12...) custom-call(s32[2]{0:T(128)} %pad_add_fusion.ids, bf16[256,512]{1,0:T(8,128)(2,1)} %get-tuple-element.55.g0, ...), custom_call_target="tpu_custom_call" | custom-call | tf_op jit(solution)/shard_map/last/pallas_call | solution.py:427
  126.5 5.8 %collective-permute-start.21 = (bf16[128,2048]{1,0:T(8,128)(2,1)}, bf16[128,2048]{1,0:T(8,128)(2,1)S(1)}, u32[]{:S(2)}, u32[]{:S(2)}) collective-permute-start(bf16[128,2048]{1,0:T(8,128)(2,1)} %get-tuple-element.78), channel_id=1, source_target_pairs={{0,4},{4,0},{8,12},{12,8},{16,20},{20,16},{24,28},{28,24},{32,36},... | collective-permute-start | bytes 1572872 | tf_op jit(solution)/shard_map/ppermute | solution.py:455
  133.6 2.7 %collective-permute-start.25 = (f32[8,2560]{1,0:T(8,128)}, f32[8,2560]{1,0:T(8,128)S(1)}, u32[]{:S(2)}, u32[]{:S(2)}) collective-permute-start(f32[8,2560]{1,0:T(8,128)} %get-tuple-element.83), channel_id=1, source_target_pairs={{12,4},{20,12},{28,20},{36,28},{44,36},{52,44},{60,52},{13,5},{21,... | collective-permute-start | bytes 245768 | tf_op jit(solution)/shard_map/ppermute | solution.py:455
  136.4 1.4 collective-permute-done.23.t_in
  140.0 3.2 %join.1 = (bf16[128,4096]{1,0:T(8,128)(2,1)}, bf16[128,1024]{1,0:T(8,128)(2,1)}, bf16[128,64]{1,0:T(8,128)(2,1)}) custom-call(s32[2]{0:T(128)} %pad_add_fusion.ids, bf16[128,2048]{1,0:T(8,128)(2,1)} %get-tuple-element.77.v_own, bf16[128,2048]{1,0:T(8,128)(2,1)} %copy-done.9, bf16[128,512]{1,0:T(8,128)(2,1)} %get-tuple-element.79.s_own, ...), custom_call_target="tpu_custom_call" | custom-call | tf_op jit(solution)/shard_map/join/pallas_call | solution.py:427
  143.2 1.4 %copy.17 = bf16[1,128,64]{1,2,0:T(8,128)(2,1)} copy(bf16[1,128,64]{2,1,0:T(8,128)(2,1)} %bitcast.29) | data formatting | bytes 32768
  (117 shorter events, 30.7 us)
Async XLA Ops:
  1.8 22.9 %collective-permute-start = (bf16[128,2048]{1,0:T(8,128)(2,1)S(1)}, bf16[128,2048]{1,0:T(8,128)(2,1)S(1)}, u32[]{:S(2)}, u32[]{:S(2)}) collective-permute-start(bf16[128,2048]{1,0:T(8,128)(2,1)S(1)} %dynamic-slice_bitcast_fusion.2), channel_id=1, source_target_pairs={{0,4},{4,0},{8,12},{12,8},{16,20},{20,16},{24,28},{28,24},{32,36},... | collective-permute-start | bytes 1572872 | tf_op jit(solution)/shard_map/ppermute | solution.py:455
  3.5 21.2 %collective-permute-start.1 = (bf16[128,512]{1,0:T(8,128)(2,1)S(1)}, bf16[128,512]{1,0:T(8,128)(2,1)S(1)}, u32[]{:S(2)}, u32[]{:S(2)}) collective-permute-start(bf16[128,512]{1,0:T(8,128)(2,1)S(1)} %dynamic-slice_bitcast_fusion.3), channel_id=1, source_target_pairs={{0,4},{4,0},{8,12},{12,8},{16,20},{20,16},{24,28},{28,24},{32,36},... | collective-permute-start | bytes 393224 | tf_op jit(solution)/shard_map/ppermute | solution.py:455
  5.7 7.7 %collective-permute-start.2 = (bf16[128,128]{1,0:T(8,128)(2,1)}, bf16[128,128]{1,0:T(8,128)(2,1)}, u32[]{:S(2)}, u32[]{:S(2)}) collective-permute-start(bf16[128,128]{1,0:T(8,128)(2,1)} %copy.15), channel_id=1, source_target_pairs={{0,4},{4,0},{8,12},{12,8},{16,20},{20,16},{24,28},{28,24},{32,36},... | collective-permute-start | bytes 98312 | tf_op jit(solution)/shard_map/ppermute | solution.py:455
  9.0 9.9 %collective-permute-start.3 = (bf16[16,2560]{1,0:T(8,128)(2,1)}, bf16[16,2560]{1,0:T(8,128)(2,1)S(1)}, u32[]{:S(2)}, u32[]{:S(2)}) collective-permute-start(bf16[16,2560]{1,0:T(8,128)(2,1)} %pad_maximum_fusion), channel_id=1, source_target_pairs={{4,12},{12,20},{20,28},{28,36},{36,44},{44,52},{52,60},{5,13},{13,... | collective-permute-start | bytes 245768 | tf_op jit(solution)/shard_map/ppermute | solution.py:455
  12.7 27.6 %collective-permute-start.8 = (bf16[128,2048]{1,0:T(8,128)(2,1)S(1)}, bf16[128,2048]{1,0:T(8,128)(2,1)S(1)}, u32[]{:S(2)}, u32[]{:S(2)}) collective-permute-start(bf16[128,2048]{1,0:T(8,128)(2,1)S(1)} %get-tuple-element.94), channel_id=1, source_target_pairs={{0,64},{64,0},{1,65},{65,1},{2,66},{66,2},{3,67},{67,3},{4,68},{68... | collective-permute-start | bytes 1572872 | tf_op jit(solution)/shard_map/ppermute | solution.py:470
  13.3 26.9 %collective-permute-start.9 = (bf16[128,2048]{1,0:T(8,128)(2,1)S(1)}, bf16[128,2048]{1,0:T(8,128)(2,1)S(1)}, u32[]{:S(2)}, u32[]{:S(2)}) collective-permute-start(bf16[128,2048]{1,0:T(8,128)(2,1)S(1)} %get-tuple-element.93), channel_id=1, source_target_pairs={{0,68},{4,64},{8,76},{12,72},{16,84},{20,80},{24,92},{28,88},{32,1... | collective-permute-start | bytes 1572872 | tf_op jit(solution)/shard_map/ppermute | solution.py:471
  18.9 5.8 %collective-permute-start.4 = (bf16[16,2560]{1,0:T(8,128)(2,1)}, bf16[16,2560]{1,0:T(8,128)(2,1)S(1)}, u32[]{:S(2)}, u32[]{:S(2)}) collective-permute-start(bf16[16,2560]{1,0:T(8,128)(2,1)} %pad_maximum_fusion.1), channel_id=1, source_target_pairs={{4,8},{12,16},{20,24},{28,32},{36,40},{44,48},{52,56},{5,9},{13,17... | collective-permute-start | bytes 245768 | tf_op jit(solution)/shard_map/ppermute | solution.py:455
  36.3 11.7 %collective-permute-start.5 = (bf16[272,512]{1,0:T(8,128)(2,1)}, bf16[272,512]{1,0:T(8,128)(2,1)S(1)}, u32[]{:S(2)}, u32[]{:S(2)}) collective-permute-start(bf16[272,512]{1,0:T(8,128)(2,1)} %get-tuple-element.46), channel_id=1, source_target_pairs={{0,8},{4,12},{8,16},{12,20},{16,24},{20,28},{24,0},{28,4},{32,40},... | collective-permute-start | bytes 835592 | tf_op jit(solution)/shard_map/ppermute | solution.py:455
  37.8 11.6 %collective-permute-start.6 = (bf16[272,512]{1,0:T(8,128)(2,1)}, bf16[272,512]{1,0:T(8,128)(2,1)S(1)}, u32[]{:S(2)}, u32[]{:S(2)}) collective-permute-start(bf16[272,512]{1,0:T(8,128)(2,1)} %get-tuple-element.47), channel_id=1, source_target_pairs={{0,16},{4,20},{8,24},{12,28},{16,0},{20,4},{24,8},{28,12},{32,48},... | collective-permute-start | bytes 835592 | tf_op jit(solution)/shard_map/ppermute | solution.py:455
  37.8 11.6 %collective-permute-start.7 = (bf16[272,512]{1,0:T(8,128)(2,1)}, bf16[272,512]{1,0:T(8,128)(2,1)S(1)}, u32[]{:S(2)}, u32[]{:S(2)}) collective-permute-start(bf16[272,512]{1,0:T(8,128)(2,1)} %get-tuple-element.48), channel_id=1, source_target_pairs={{0,24},{4,28},{8,0},{12,4},{16,8},{20,12},{24,16},{28,20},{32,56},... | collective-permute-start | bytes 835592 | tf_op jit(solution)/shard_map/ppermute | solution.py:455
  46.1 9.5 %collective-permute-start.10 = (bf16[256,512]{1,0:T(8,128)(2,1)}, bf16[256,512]{1,0:T(8,128)(2,1)S(1)}, u32[]{:S(2)}, u32[]{:S(2)}) collective-permute-start(bf16[256,512]{1,0:T(8,128)(2,1)} %get-tuple-element.52), channel_id=1, source_target_pairs={{0,8},{4,12},{8,16},{12,20},{16,24},{20,28},{24,0},{28,4},{32,40},... | collective-permute-start | bytes 786440 | tf_op jit(solution)/shard_map/ppermute | solution.py:455
  46.1 9.5 %collective-permute-start.11 = (bf16[256,512]{1,0:T(8,128)(2,1)}, bf16[256,512]{1,0:T(8,128)(2,1)S(1)}, u32[]{:S(2)}, u32[]{:S(2)}) collective-permute-start(bf16[256,512]{1,0:T(8,128)(2,1)} %get-tuple-element.53), channel_id=1, source_target_pairs={{0,16},{4,20},{8,24},{12,28},{16,0},{20,4},{24,8},{28,12},{32,48},... | collective-permute-start | bytes 786440 | tf_op jit(solution)/shard_map/ppermute | solution.py:455
  48.0 8.1 %collective-permute-start.12 = (bf16[256,512]{1,0:T(8,128)(2,1)}, bf16[256,512]{1,0:T(8,128)(2,1)S(1)}, u32[]{:S(2)}, u32[]{:S(2)}) collective-permute-start(bf16[256,512]{1,0:T(8,128)(2,1)} %get-tuple-element.54), channel_id=1, source_target_pairs={{0,24},{4,28},{8,0},{12,4},{16,8},{20,12},{24,16},{28,20},{32,56},... | collective-permute-start | bytes 786440 | tf_op jit(solution)/shard_map/ppermute | solution.py:455
  53.4 23.8 %collective-permute-start.17 = (bf16[256,512]{1,0:T(8,128)(2,1)}, bf16[256,512]{1,0:T(8,128)(2,1)S(1)}, u32[]{:S(2)}, u32[]{:S(2)}) collective-permute-start(bf16[256,512]{1,0:T(8,128)(2,1)} %edge_forward.1), channel_id=1, source_target_pairs={{0,32},{4,36},{8,40},{12,44},{16,48},{20,52},{24,56},{28,60},{1,33... | collective-permute-start | bytes 786440 | tf_op jit(solution)/shard_map/ppermute | solution.py:455
  60.0 26.0 %collective-permute-start.13 = (bf16[256,512]{1,0:T(8,128)(2,1)}, bf16[256,512]{1,0:T(8,128)(2,1)S(1)}, u32[]{:S(2)}, u32[]{:S(2)}) collective-permute-start(bf16[256,512]{1,0:T(8,128)(2,1)} %edge_back.1), channel_id=1, source_target_pairs={{32,0},{36,4},{40,8},{44,12},{48,16},{52,20},{56,24},{60,28},{33,1... | collective-permute-start | bytes 786440 | tf_op jit(solution)/shard_map/ppermute | solution.py:455
  82.1 12.5 %collective-permute-start.18 = (bf16[256,512]{1,0:T(8,128)(2,1)}, bf16[256,512]{1,0:T(8,128)(2,1)S(1)}, u32[]{:S(2)}, u32[]{:S(2)}) collective-permute-start(bf16[256,512]{1,0:T(8,128)(2,1)} %get-tuple-element.60), channel_id=1, source_target_pairs={{0,24},{4,28},{8,0},{12,4},{16,8},{20,12},{24,16},{28,20},{32,56},... | collective-permute-start | bytes 786440 | tf_op jit(solution)/shard_map/ppermute | solution.py:455
  85.4 23.2 %collective-permute-start.19 = (bf16[256,512]{1,0:T(8,128)(2,1)}, bf16[256,512]{1,0:T(8,128)(2,1)S(1)}, u32[]{:S(2)}, u32[]{:S(2)}) collective-permute-start(bf16[256,512]{1,0:T(8,128)(2,1)} %get-tuple-element.61), channel_id=1, source_target_pairs={{0,16},{4,20},{8,24},{12,28},{16,0},{20,4},{24,8},{28,12},{32,48},... | collective-permute-start | bytes 786440 | tf_op jit(solution)/shard_map/ppermute | solution.py:455
  85.4 23.2 %collective-permute-start.20 = (bf16[256,512]{1,0:T(8,128)(2,1)}, bf16[256,512]{1,0:T(8,128)(2,1)S(1)}, u32[]{:S(2)}, u32[]{:S(2)}) collective-permute-start(bf16[256,512]{1,0:T(8,128)(2,1)} %get-tuple-element.62), channel_id=1, source_target_pairs={{0,8},{4,12},{8,16},{12,20},{16,24},{20,28},{24,0},{28,4},{32,40},... | collective-permute-start | bytes 786440 | tf_op jit(solution)/shard_map/ppermute | solution.py:455
  90.8 23.7 %collective-permute-start.14 = (bf16[256,512]{1,0:T(8,128)(2,1)}, bf16[256,512]{1,0:T(8,128)(2,1)S(1)}, u32[]{:S(2)}, u32[]{:S(2)}) collective-permute-start(bf16[256,512]{1,0:T(8,128)(2,1)} %get-tuple-element.56), channel_id=1, source_target_pairs={{0,24},{4,28},{8,0},{12,4},{16,8},{20,12},{24,16},{28,20},{32,56},... | collective-permute-start | bytes 786440 | tf_op jit(solution)/shard_map/ppermute | solution.py:455
  92.9 21.7 %collective-permute-start.15 = (bf16[256,512]{1,0:T(8,128)(2,1)}, bf16[256,512]{1,0:T(8,128)(2,1)S(1)}, u32[]{:S(2)}, u32[]{:S(2)}) collective-permute-start(bf16[256,512]{1,0:T(8,128)(2,1)} %get-tuple-element.57), channel_id=1, source_target_pairs={{0,16},{4,20},{8,24},{12,28},{16,0},{20,4},{24,8},{28,12},{32,48},... | collective-permute-start | bytes 786440 | tf_op jit(solution)/shard_map/ppermute | solution.py:455
  94.6 19.9 %collective-permute-start.16 = (bf16[256,512]{1,0:T(8,128)(2,1)}, bf16[256,512]{1,0:T(8,128)(2,1)S(1)}, u32[]{:S(2)}, u32[]{:S(2)}) collective-permute-start(bf16[256,512]{1,0:T(8,128)(2,1)} %get-tuple-element.58), channel_id=1, source_target_pairs={{0,8},{4,12},{8,16},{12,20},{16,24},{20,28},{24,0},{28,4},{32,40},... | collective-permute-start | bytes 786440 | tf_op jit(solution)/shard_map/ppermute | solution.py:455
  126.5 12.7 %collective-permute-start.21 = (bf16[128,2048]{1,0:T(8,128)(2,1)}, bf16[128,2048]{1,0:T(8,128)(2,1)S(1)}, u32[]{:S(2)}, u32[]{:S(2)}) collective-permute-start(bf16[128,2048]{1,0:T(8,128)(2,1)} %get-tuple-element.78), channel_id=1, source_target_pairs={{0,4},{4,0},{8,12},{12,8},{16,20},{20,16},{24,28},{28,24},{32,36},... | collective-permute-start | bytes 1572872 | tf_op jit(solution)/shard_map/ppermute | solution.py:455
  132.2 6.9 %collective-permute-start.22 = (bf16[128,512]{1,0:T(8,128)(2,1)}, bf16[128,512]{1,0:T(8,128)(2,1)S(1)}, u32[]{:S(2)}, u32[]{:S(2)}) collective-permute-start(bf16[128,512]{1,0:T(8,128)(2,1)} %get-tuple-element.80), channel_id=1, source_target_pairs={{0,4},{4,0},{8,12},{12,8},{16,20},{20,16},{24,28},{28,24},{32,36},... | collective-permute-start | bytes 393224 | tf_op jit(solution)/shard_map/ppermute | solution.py:455
  132.3 6.1 %collective-permute-start.24 = (f32[8,2560]{1,0:T(8,128)}, f32[8,2560]{1,0:T(8,128)S(1)}, u32[]{:S(2)}, u32[]{:S(2)}) collective-permute-start(f32[8,2560]{1,0:T(8,128)} %get-tuple-element.83), channel_id=1, source_target_pairs={{8,4},{16,12},{24,20},{32,28},{40,36},{48,44},{56,52},{9,5},{17,13... | collective-permute-start | bytes 245768 | tf_op jit(solution)/shard_map/ppermute | solution.py:455
  (30 other events, 92.8 us)
where the time goes:
time: 146 us; the launch traced here: 145 us
  Pallas kernels  62.6 us (43%)
  starting transfers between devices  52.8 us (36%)
  local copies, waits for them, and re-layouts  20.2 us (14%)
  waiting for transfers between devices  6.11 us (4%)
  other arithmetic  1.93 us (1%)
    pallas_call x10, Pallas kernels, call(): pl.pallas_call(kernel, grid_spec=pltpu.PrefetchScalarGridSpec(num_scalar_...  62.6 us
    ppermute x24, starting transfers between devices, send(): return lax.ppermute(x, 'ctx', pairs)  52.2 us
    unnamed x57, local copies, waits for them, and re-layouts  8.73 us
    ppermute x24, waiting for transfers between devices, send(): return lax.ppermute(x, 'ctx', pairs)  6.11 us
  transfers between devices with their start and end apart: 26, of which 7 were waited for; matrix products, arithmetic and copies ran while one was open for 8% of the time, Pallas kernels for 33%

commit v1 on v0

v1 whole, which is shorter than its diff:
```python
import functools

import jax
import jax.numpy as jnp
from jax import lax
from jax.experimental import pallas as pl
from jax.experimental.pallas import tpu as pltpu
from jax.sharding import PartitionSpec as P

HEAD_DIM = 64
STATE = 256
CONV = 4
CORES = 2
RING = 4
HALVES = 2
f32 = jnp.float32
bf16 = jnp.bfloat16
HIGH = lax.Precision.HIGHEST

TOK = 128
ROWS = TOK * CORES
HEADS = 32
WIDE = HEADS * HEAD_DIM
PART = WIDE // RING
TAIL = 16
LOG2E = 1.4426950408889634


def place():
    index = lax.axis_index("ctx")
    return lax.rem(index, CORES), lax.rem(lax.div(index, CORES), RING)


def rows_of(core):
    return (
        pl.ds(pl.multiple_of(core * TOK, TOK), TOK),
        pl.ds(pl.multiple_of((1 - core) * TOK, TOK), TOK),
    )


def block128(b, start=0):
    return pl.ds(pl.multiple_of(start + b * 128, 128), 128)


def head_columns(ring, slot):
    return pl.ds(pl.multiple_of(lax.rem(ring + slot, RING) * PART, PART), PART)


def nn(a, b, precision=None):
    return lax.dot_general(
        a, b, (((1,), (0,)), ((), ())), precision=precision, preferred_element_type=f32
    )


def nt(a, b):
    return lax.dot_general(a, b, (((1,), (1,)), ((), ())), preferred_element_type=f32)


def iota(shape, axis):
    return lax.broadcasted_iota(jnp.int32, shape, axis)


def split3(x):
    high = x.astype(bf16).astype(f32)
    rest = x - high
    mid = rest.astype(bf16).astype(f32)
    low = rest - mid
    part = iota(x.shape, 1) // HEADS
    picked = jnp.where(part == 0, high, jnp.where(part == 1, mid, jnp.where(part == 2, low, 0.0)))
    return picked.astype(bf16)


def head_sum(x, ones):
    high = x.astype(bf16)
    low = (x - high.astype(f32)).astype(bf16)
    return nt(high, ones) + nt(low, ones)


def tiled_heads(x, group):
    x = x.astype(f32)
    mine = jnp.where(group == 0, x[:, :HEADS], x[:, HEADS:])
    return jnp.concatenate([mine] * 4, axis=1)


def softplus(x):
    u = jnp.exp(-jnp.abs(x))
    small = u * (1.0 - u * (0.5 - u * (1.0 / 3.0 - u * 0.25)))
    return jnp.maximum(x, 0.0) + jnp.where(u < 0.01, small, jnp.log(1.0 + u))


def sigmoid(x):
    return 1.0 / (1.0 + jnp.exp(-x))


def sigmoid_by_tanh(x):
    return 0.5 + 0.5 * jnp.tanh(0.5 * x)


def pack_kernel(v, s, r, message, halo_a, halo_b, sems):
    core, ring = place()
    there = 1 - core
    copies = [
        (v.at[:, pl.ds(pl.multiple_of(there * WIDE, 128), WIDE)], message.at[:, pl.ds(0, WIDE)]),
        (
            s.at[:, pl.ds(pl.multiple_of(there * 2 * STATE, 128), 2 * STATE)],
            message.at[:, pl.ds(WIDE, 2 * STATE)],
        ),
    ]
    for group, halo in ((1, halo_a), (0, halo_b)):
        rows = pl.ds(TOK - TAIL, TAIL)
        copies.append((v.at[rows, pl.ds(group * WIDE, WIDE)], halo.at[:, pl.ds(0, WIDE)]))
        copies.append(
            (s.at[rows, pl.ds(group * 2 * STATE, 2 * STATE)], halo.at[:, pl.ds(WIDE, 2 * STATE)])
        )
    copies = [pltpu.make_async_copy(a, b, sems.at[k]) for k, (a, b) in enumerate(copies)]
    for copy in copies:
        copy.start()
    message[:, WIDE + 2 * STATE :] = tiled_heads(r[...], there).astype(bf16)
    for copy in copies:
        copy.wait()


def pack_grad_kernel(g, own, across, sems):
    core, ring = place()
    copies = [
        pltpu.make_async_copy(
            g.at[:, pl.ds(pl.multiple_of(group * WIDE, 128), WIDE)], out, sems.at[k]
        )
        for k, (group, out) in enumerate(((core, own), (1 - core, across)))
    ]
    for copy in copies:
        copy.start()
    for copy in copies:
        copy.wait()


def ones_kernel(out):
    rows = iota((128, WIDE), 0) % HEADS
    cols = iota((128, WIDE), 1) // HEAD_DIM
    out[...] = jnp.where(rows == cols, 1.0, 0.0).astype(bf16)


def first_kernel(
    v, s, r, message, halo_a, halo_b, step_bias, decay_log, v_tap, v_off, s_tap, s_off, ones,
    m0, m1, m2, m3, x_out, xs_out, sx_out, k_out, bc_out, sbc_out, delta_out, within_out, sig_out,
    buf, sbuf, raw, wide,
):
    core, ring = place()
    mine, other = rows_of(core)
    raw[mine, :] = tiled_heads(r[...], core)
    raw[other, :] = message[:, WIDE + 2 * STATE :].astype(f32)
    pre = raw[...] + tiled_heads(step_bias[...], core)
    delta = softplus(pre)
    rate = -jnp.exp(tiled_heads(decay_log[...], core))
    lower = jnp.where(iota((ROWS, ROWS), 0) >= iota((ROWS, ROWS), 1), 1.0, 0.0).astype(f32)
    within = nn(lower, delta * rate, HIGH)
    delta_out[...] = delta
    within_out[...] = within
    sig_out[...] = sigmoid(pre)
    total = within[ROWS - 1 : ROWS, :]
    wide[...] = nn(split3(delta * jnp.exp(total - within)), ones[...])

    below = pl.ds(pl.multiple_of(8 + core * TOK, 8), TOK)
    above = pl.ds(pl.multiple_of(8 + (1 - core) * TOK, 8), TOK)
    v_mine = pl.ds(pl.multiple_of(core * WIDE, 128), WIDE)
    s_mine = pl.ds(pl.multiple_of(core * 2 * STATE, 128), 2 * STATE)
    buf[below, :] = v[:, v_mine].astype(f32)
    buf[above, :] = message[:, :WIDE].astype(f32)
    sbuf[below, :] = s[:, s_mine].astype(f32)
    sbuf[above, :] = message[:, WIDE : WIDE + 2 * STATE].astype(f32)
    halo = halo_a[...].astype(f32) + halo_b[...].astype(f32)
    buf[0:8, :] = halo[8:16, :WIDE]
    sbuf[0:8, :] = halo[8:16, WIDE:]

    def conv(source, tap, off, b, width):
        cols, par = block128(b), block128(b, core * width)
        acc = off[:, par] + tap[0:1, par] * source[5 : 5 + ROWS, cols]
        for j in range(1, CONV):
            acc = acc + tap[j : j + 1, par] * source[5 + j : 5 + j + ROWS, cols]
        sig = sigmoid_by_tanh(acc)
        return acc * sig, sig * (1.0 + acc * (1.0 - sig))

    def state_block(b, carry):
        cols = block128(b)
        post, slope = conv(sbuf, s_tap, s_off, b, 2 * STATE)
        bc_out[:, cols] = post.astype(bf16)
        sbc_out[:, cols] = slope.astype(bf16)
        return carry

    lax.fori_loop(0, 4, state_block, 0)

    def value_block(b, carry):
        cols = block128(b)
        post, slope = conv(buf, v_tap, v_off, b, WIDE)
        post = post.astype(bf16)
        scale = wide[:, cols]
        x_out[:, cols] = post
        sx_out[:, cols] = slope.astype(bf16)
        k_out[:, cols] = (slope * scale).astype(bf16)
        xs_out[:, cols] = (post.astype(f32) * scale).astype(bf16)
        return carry

    lax.fori_loop(0, 16, value_block, 0)

    write_t = bc_out[:, :STATE].astype(f32).T.astype(bf16)
    total_parts = split3(jnp.broadcast_to(total, (8, 128)))
    for slot, out in enumerate((m0, m1, m2, m3)):
        cols = head_columns(ring, slot)
        out[0:STATE, :] = nn(write_t, xs_out[:, cols]).astype(bf16)
        full = nn(total_parts, ones[:, cols])[0:1, :]
        high = full.astype(bf16).astype(f32)
        mid = (full - high).astype(bf16).astype(f32)
        low = full - high - mid
        row = iota((TAIL, PART), 0)
        out[STATE : STATE + TAIL, :] = jnp.where(
            row == 0, high, jnp.where(row == 1, mid, jnp.where(row == 2, low, 0.0))
        ).astype(bf16)


def ring_totals(parts):
    out = []
    for part in parts:
        rows = part[STATE : STATE + TAIL, :].astype(f32)
        out.append(rows[0:1] + rows[1:2] + rows[2:3])
    return out


def between(totals, places, low, high):
    out = jnp.zeros_like(totals[0])
    for total, p in zip(totals, places):
        inside = jnp.logical_and(p > low, p < high)
        out = out + total * jnp.where(inside, 1.0, 0.0)
    return out


def edge_kernel(back, m0, m1, m2, m3, d0, d1, d2, d3, out):
    core, ring = place()
    places = [lax.rem(ring + RING - s, RING) for s in range(RING)]
    totals = ring_totals((m0, m1, m2, m3))
    weights = []
    for p in places:
        low, high = (-1, p) if back else (p, RING)
        weights.append(jnp.exp(between(totals, places, low, high)))
    for c in range(0, PART, 128):
        cols = slice(c, c + 128)
        acc = None
        for src, weight in zip((d0, d1, d2, d3), weights):
            term = weight[:, cols] * src[0:STATE, cols].astype(f32)
            acc = term if acc is None else acc + term
        out[:, cols] = acc.astype(bf16)


def scan_kernel(back, m0, m1, m2, m3, d0, d1, d2, d3, edge, o0, o1, o2, o3):
    core, ring = place()
    places = [lax.rem(ring + RING - s, RING) for s in range(RING)]
    totals = ring_totals((m0, m1, m2, m3))
    weights = []
    for here in places:
        low, high = (here, RING) if back else (-1, here)
        row = [jnp.exp(between(totals, places, low, high))]
        for p in places:
            low, high, live = (here, p, p > here) if back else (p, here, p < here)
            row.append(jnp.exp(between(totals, places, low, high)) * jnp.where(live, 1.0, 0.0))
        weights.append(row)
    for c in range(0, PART, 128):
        cols = slice(c, c + 128)
        for r in range(0, STATE, 64):
            rows = slice(r, r + 64)
            parts = [edge[rows, cols].astype(f32)]
            parts += [src[rows, cols].astype(f32) for src in (d0, d1, d2, d3)]
            for out, row in zip((o0, o1, o2, o3), weights):
                acc = row[0][:, cols] * parts[0]
                for weight, part in zip(row[1:], parts[1:]):
                    acc = acc + weight[:, cols] * part
                out[rows, cols] = acc.astype(bf16)


def second_kernel(g_own, g_in, bc, within, ones, d0, d1, d2, d3, dy_out, dye_out, wide):
    core, ring = place()
    mine, other = rows_of(core)
    dy_out[mine, :] = g_own[...]
    dy_out[other, :] = g_in[...]
    wide[...] = nn(split3(jnp.exp(within[...])), ones[...])
    read_t = bc[:, STATE:].astype(f32).T.astype(bf16)

    def block(b, carry):
        cols = block128(b)
        dye_out[:, cols] = (dy_out[:, cols].astype(f32) * wide[:, cols]).astype(bf16)
        return carry

    lax.fori_loop(0, 16, block, 0)
    for slot, out in enumerate((d0, d1, d2, d3)):
        out[...] = nn(read_t, dye_out[:, head_columns(ring, slot)]).astype(bf16)


def inner_kernel(
    x, dy, bc, delta, within, sx, skip_gain, ones,
    base_out, dbc_out, diff_out, vsum_out,
    wide, skips, within_3, row_sum, bcs, dbcs,
):
    core, ring = place()
    half = ROWS // 2
    wide[...] = nn(split3(delta[...]), ones[...])
    skip = jnp.broadcast_to(tiled_heads(skip_gain[...], core), (8, 128))
    skips[...] = nn(split3(skip), ones[...])
    scaled = within[...] * LOG2E
    lane_part = iota((ROWS, 128), 1) // HEADS
    left = jnp.where(lane_part == 3, 1.0, -split3(scaled).astype(f32)).astype(bf16)
    parts_t = split3(scaled).astype(f32).T
    for h in range(HEADS):
        within_3[h, 0:1, :] = parts_t[h : h + 1, :]
        within_3[h, 1:2, :] = parts_t[HEADS + h : HEADS + h + 1, :]
        within_3[h, 2:3, :] = parts_t[2 * HEADS + h : 2 * HEADS + h + 1, :]
        within_3[h, 3:8, :] = jnp.zeros((5, ROWS), f32)
    write, read = bc[:, :STATE], bc[:, STATE:]
    bcs[...] = nt(write, read)
    dbcs[...] = jnp.zeros_like(dbcs)
    diff_out[...] = jnp.zeros_like(diff_out)
    vsum_out[...] = jnp.zeros_like(vsum_out)
    keep = iota((half, half), 1) >= iota((half, half), 0)
    lanes = iota((ROWS, 128), 1)
    first = lanes < HEAD_DIM
    row_head = iota((96, ROWS), 0) % HEADS
    pad = jnp.zeros((24, ROWS), f32)

    def pair(b, carry):
        cols = block128(b)
        xb = x[:, cols].astype(f32)
        xd = (xb * wide[:, cols]).astype(bf16)
        grad = dy[:, cols]
        zero = jnp.zeros_like(grad)
        top = jnp.zeros((half, 128), f32)
        bot = jnp.zeros((half, 128), f32)
        col_total = jnp.zeros((ROWS, 128), f32)
        grads_of = [0.0, 0.0, 0.0]
        for e in range(2):
            h = 2 * b + e
            g = jnp.where(first, grad, zero) if e == 0 else jnp.where(first, zero, grad)
            right = jnp.concatenate(
                [jnp.where(row_head == h, 1.0, 0.0), within_3[h], pad], axis=0
            ).astype(bf16)
            gap0 = nn(left[:half], right)
            gap1 = nn(left[half:], right[:, half:])
            dm0 = nt(xd[:half], g)
            dm1 = nt(xd[half:], g[half:])
            blocks = (
                (jnp.where(keep, gap0[:, :half], -jnp.inf), dm0[:, :half], 0, 0),
                (gap0[:, half:], dm0[:, half:], 0, 1),
                (jnp.where(keep, gap1, -jnp.inf), dm1, 1, 1),
            )
            ps, ms = [], []
            for k, (gap, dm, r, c) in enumerate(blocks):
                decay = jnp.exp2(gap)
                m = decay * bcs[r * half : (r + 1) * half, c * half : (c + 1) * half]
                grads_of[k] = grads_of[k] + dm * decay
                ps.append(dm * m)
                ms.append(m.astype(bf16))
            sum_rows = jnp.concatenate(
                [
                    jnp.sum(ps[0], axis=0, keepdims=True),
                    jnp.sum(ps[1] + ps[2], axis=0, keepdims=True),
                ],
                axis=1,
            )
            row_sum[pl.ds(h, 1), :] = sum_rows
            top = top + nn(ms[0], g[:half]) + nn(ms[1], g[half:])
            bot = bot + nn(ms[2], g[half:])
            col = jnp.concatenate(
                [
                    jnp.sum(ps[0] + ps[1], axis=1, keepdims=True),
                    jnp.sum(ps[2], axis=1, keepdims=True),
                ],
                axis=0,
            )
            col_total = col_total + jnp.where(lanes % HEADS == h, col, 0.0)
        for k, (r, c) in enumerate(((0, 0), (0, 1), (1, 1))):
            rs, cs = slice(r * half, (r + 1) * half), slice(c * half, (c + 1) * half)
            dbcs[rs, cs] = dbcs[rs, cs] + grads_of[k]
        u = jnp.concatenate([top, bot], axis=0)
        diff_out[...] = diff_out[...] - col_total
        vsum_out[...] = vsum_out[...] + head_sum(xb * u, ones[:, cols])
        base_out[:, cols] = (
            wide[:, cols] * u + skips[0:1, cols] * grad.astype(f32)
        ) * sx[:, cols].astype(f32)
        return carry

    lax.fori_loop(0, 16, pair, 0)
    for t in range(1, 4):
        row_sum[t * HEADS : (t + 1) * HEADS, :] = row_sum[0:HEADS, :]
    diff_out[...] = diff_out[...] + row_sum[...].T
    grad = dbcs[...]
    dbc_out[:, :STATE] = nn(grad.astype(bf16), read)
    dbc_out[:, STATE:] = nn(grad.T.astype(bf16), write)


def carry_kernel(c0, c1, c2, c3, bc, dye, dbc, diff, ones, diff_out, dread_out, carried_out):
    core, ring = place()
    for slot, src in enumerate((c0, c1, c2, c3)):
        carried_out[:, head_columns(ring, slot)] = src[...]
    read = bc[:, STATE:]
    dread_out[...] = dbc[:, STATE:] + nt(dye[...], carried_out[...])
    outer = diff[...]
    for b in range(4):
        cols = slice(b * PART, (b + 1) * PART)
        part = nn(read, carried_out[:, cols]) * dye[:, cols].astype(f32)
        outer = outer + head_sum(part, ones[:, cols])
    diff_out[...] = outer


def last_kernel(
    g0, g1, g2, g3, carried, bc, xs, k, base, sbc, delta, within, sig, diff, vsum,
    dread, dbc, decay_log, v_tap, s_tap, ones,
    vg_own, sg_own, st_own, message, head_out,
    gbuf, ebuf, sbuf, dbuf, back, sback,
):
    core, ring = place()
    mine, other = rows_of(core)
    for slot, src in enumerate((g0, g1, g2, g3)):
        gbuf[:, head_columns(ring, slot)] = src[...]
    write = bc[:, :STATE]
    rsum = jnp.zeros((ROWS, 128), f32)
    tsum = jnp.zeros((8, 128), f32)
    ebuf[ROWS : ROWS + 8, :] = jnp.zeros((8, WIDE), f32)
    sbuf[ROWS : ROWS + 8, :] = jnp.zeros((8, 2 * STATE), f32)
    for b in range(4):
        cols = slice(b * PART, (b + 1) * PART)
        grad = gbuf[:, cols]
        through = nn(write, grad)
        rsum = rsum + head_sum(xs[:, cols].astype(f32) * through, ones[:, cols])
        ebuf[0:ROWS, cols] = base[:, cols] + k[:, cols].astype(f32) * through
        both = jnp.sum(
            grad.astype(f32) * carried[:, cols].astype(f32), axis=0, keepdims=True
        )
        tsum = tsum + head_sum(jnp.broadcast_to(both, (8, PART)), ones[:, cols])
    total = within[ROWS - 1 : ROWS, :]
    dtotal = tsum[0:1, :] * jnp.exp(total)
    ra, rb = iota((ROWS, ROWS), 0), iota((ROWS, ROWS), 1)
    later = jnp.where(rb >= ra, 1.0, 0.0).astype(f32)
    earlier = jnp.where(rb < ra, 1.0, 0.0).astype(f32)
    da = nn(later, diff[...], HIGH) + nn(earlier, rsum, HIGH) + dtotal
    rate = -jnp.exp(tiled_heads(decay_log[...], core))
    dbuf[...] = (vsum[...] + rsum / delta[...] + rate * da) * sig[...]
    st_own[...] = dbuf[mine, :].astype(bf16)
    message[:, WIDE + 2 * STATE :] = dbuf[other, :].astype(bf16)

    dwrite = dbc[:, :STATE] + nt(xs[...], gbuf[...])
    sbuf[0:ROWS, :STATE] = dwrite * sbc[:, :STATE].astype(f32)
    sbuf[0:ROWS, STATE:] = dread[...] * sbc[:, STATE:].astype(f32)
    head_out[:, :WIDE] = ebuf[0:8, :]
    head_out[:, WIDE:] = sbuf[0:8, :]

    def conv(source, tap, b, width):
        cols, par = block128(b), block128(b, core * width)
        acc = tap[CONV - 1 : CONV, par] * source[0:ROWS, cols]
        for shift in range(1, CONV):
            j = CONV - 1 - shift
            acc = acc + tap[j : j + 1, par] * source[shift : shift + ROWS, cols]
        return acc.astype(bf16)

    def value_block(b, carry):
        back[:, block128(b)] = conv(ebuf, v_tap, b, WIDE)
        return carry

    lax.fori_loop(0, 16, value_block, 0)

    def state_block(b, carry):
        sback[:, block128(b)] = conv(sbuf, s_tap, b, 2 * STATE)
        return carry

    lax.fori_loop(0, 4, state_block, 0)
    vg_own[...] = back[mine, :]
    message[:, :WIDE] = back[other, :]
    sg_own[...] = sback[mine, :]
    message[:, WIDE : WIDE + 2 * STATE] = sback[other, :]


def join_kernel(v_own, s_own, t_own, message, e0, e1, v_tap, s_tap, v_out, s_out, t_out):
    core, ring = place()

    def place_in(out, own, arrived, width):
        out[:, pl.ds(pl.multiple_of(core * width, 128), width)] = own
        out[:, pl.ds(pl.multiple_of((1 - core) * width, 128), width)] = arrived

    def patch(out, tap, edge, width, group, start):
        cols = slice(group * width, (group + 1) * width)
        rows = edge[:, start : start + width]
        row = iota((TAIL, width), 0)
        acc = out[TOK - TAIL :, cols].astype(f32)
        for shift in range(1, CONV):
            j = CONV - 1 - shift
            for k in range(shift):
                acc = acc + jnp.where(
                    row == TAIL - shift + k, tap[j : j + 1, cols] * rows[k : k + 1], 0.0
                )
        out[TOK - TAIL :, cols] = acc.astype(bf16)

    place_in(v_out, v_own[...], message[:, :WIDE], WIDE)
    place_in(s_out, s_own[...], message[:, WIDE : WIDE + 2 * STATE], 2 * STATE)

    @pl.when(core == CORES - 1)
    def _():
        for group, edge in enumerate((e0, e1)):
            patch(v_out, v_tap, edge, WIDE, group, 0)
            patch(s_out, s_tap, edge, 2 * STATE, group, WIDE)

    own = t_own[:, :HEADS].astype(f32)
    arrived = message[:, WIDE + 2 * STATE : WIDE + 2 * STATE + HEADS].astype(f32)
    low = jnp.where(core == 0, own, arrived)
    high = jnp.where(core == 0, arrived, own)
    t_out[...] = jnp.concatenate([low, high], axis=1).astype(bf16)


def call(kernel, args, outs, scratch=(), name=None, anywhere=(), cost=None):
    vmem = pl.BlockSpec(memory_space=pltpu.VMEM)
    return pl.pallas_call(
        kernel,
        in_specs=[
            pl.BlockSpec(memory_space=pl.ANY) if k in anywhere else vmem for k in range(len(args))
        ],
        out_specs=[vmem for _ in outs],
        out_shape=[jax.ShapeDtypeStruct(*o) for o in outs],
        scratch_shapes=[s if not isinstance(s, tuple) else pltpu.VMEM(*s) for s in scratch],
        compiler_params=pltpu.CompilerParams(vmem_limit_bytes=24 * 1024 * 1024),
        cost_estimate=None
        if cost is None
        else pl.CostEstimate(flops=0, transcendentals=0, bytes_accessed=int(cost * 3.0e6)),
        name=name,
    )(*args)


def local(
    value_input, state_input, step_raw, upstream, step_bias, decay_log, skip_gain,
    value_kernel, value_offset, state_kernel, state_offset,
):
    count = lax.axis_size("ctx")
    chips = count // CORES
    per_half = count // HALVES

    def send(x, pairs):
        return lax.ppermute(x, "ctx", pairs)

    swap_pairs = [(i, i ^ 1) for i in range(count)]

    def around(i, shift):
        half, at, c = i // (RING * CORES), (i // CORES) % RING, i % CORES
        return (half * RING + (at + shift) % RING) * CORES + c

    def exchange(parts, sign):
        out = [parts[0]]
        for k in range(1, RING):
            out.append(send(parts[k], [(i, around(i, sign * k)) for i in range(count)]))
        return out

    row = lambda x: x.reshape(1, -1)
    v, s, r, g = value_input[0], state_input[0], step_raw[0], upstream[0]
    bias, rate_log, skip = row(step_bias), row(decay_log), row(skip_gain)
    joint = WIDE + 2 * STATE + 128
    tall = (ROWS, WIDE)
    narrow = (ROWS, 128)
    marked = ((STATE + TAIL, PART), bf16)
    state_part = ((STATE, PART), bf16)
    sems = pltpu.SemaphoreType.DMA

    message, halo_a, halo_b = call(
        pack_kernel, [v, s, r],
        [((TOK, joint), bf16), ((TAIL, WIDE + 2 * STATE), bf16), ((TAIL, WIDE + 2 * STATE), bf16)],
        [sems((6,))], "pack", (0, 1),
    )
    message = send(message, swap_pairs)
    halo_a = send(halo_a, [(k * 2 + 1, k * 2 + 3) for k in range(chips - 1)])
    halo_b = send(halo_b, [(k * 2 + 1, k * 2 + 2) for k in range(chips - 1)])
    g_own, g_in = call(
        pack_grad_kernel, [g], [((TOK, WIDE), bf16)] * 2, [sems((2,))], "pack_grad", (0,)
    )
    g_own = lax.ppermute(g_own, "pipe", [(0, 1), (1, 0)])
    g_in = lax.ppermute(
        g_in,
        ("pipe", "ctx"),
        [(p * count + i, (1 - p) * count + (i ^ 1)) for p in range(2) for i in range(count)],
    )
    ones = call(ones_kernel, [], [((128, WIDE), bf16)], name="ones")[0]
    (m0, m1, m2, m3, x, xs, sx, k, bc, sbc, delta, within, sig) = call(
        first_kernel,
        [v, s, r, message, halo_a, halo_b, bias, rate_log,
         value_kernel, row(value_offset), state_kernel, row(state_offset), ones],
        [marked] * 4 + [(tall, bf16)] * 4 + [((ROWS, 2 * STATE), bf16)] * 2 + [(narrow, f32)] * 3,
        [((ROWS + 8, WIDE), f32), ((ROWS + 8, 2 * STATE), f32), (narrow, f32), (tall, f32)],
        "first", cost=8,
    )
    marks = exchange((m0, m1, m2, m3), 1)
    d0, d1, d2, d3, dy, dye = call(
        second_kernel, [g_own, g_in, bc, within, ones],
        [state_part] * 4 + [(tall, bf16)] * 2, [(tall, f32)], "second", cost=4,
    )
    grads = exchange((d0, d1, d2, d3), 1)
    edge = call(
        functools.partial(edge_kernel, False), marks + marks, [state_part], (), "edge_forward",
        cost=2,
    )[0]
    edge_in = send(edge, [(i, i + per_half) for i in range(per_half)])
    dy_now, _ = lax.optimization_barrier((dy, edge))
    base, dbc, diff, vsum = call(
        inner_kernel, [x, dy_now, bc, delta, within, sx, skip, ones],
        [(tall, f32), ((ROWS, 2 * STATE), f32), (narrow, f32), (narrow, f32)],
        [(tall, f32), ((8, WIDE), f32), ((HEADS, 8, ROWS), f32), ((128, ROWS), f32),
         ((ROWS, ROWS), f32), ((ROWS, ROWS), f32)],
        "inner", cost=12,
    )
    edge_in, diff = lax.optimization_barrier((edge_in, diff))
    carried = exchange(
        call(
            functools.partial(scan_kernel, False), marks + marks + [edge_in],
            [state_part] * 4, (), "scan_forward", cost=3,
        ),
        -1,
    )
    edge_back = call(
        functools.partial(edge_kernel, True), marks + grads, [state_part], (), "edge_back", cost=2,
    )[0]
    edge_back = send(edge_back, [(i + per_half, i) for i in range(per_half)])
    back = exchange(
        call(
            functools.partial(scan_kernel, True), marks + grads + [edge_back],
            [state_part] * 4, (), "scan_back", cost=3,
        ),
        -1,
    )
    diff, dread, held = call(
        carry_kernel, list(carried) + [bc, dye, dbc, diff, ones],
        [(narrow, f32), ((ROWS, STATE), f32), ((STATE, WIDE), bf16)], (), "carry", cost=4,
    )
    vg_own, sg_own, st_own, message, head = call(
        last_kernel,
        list(back)
        + [held, bc, xs, k, base, sbc, delta, within, sig, diff, vsum, dread, dbc,
           rate_log, value_kernel, state_kernel, ones],
        [((TOK, WIDE), bf16), ((TOK, 2 * STATE), bf16), ((TOK, 128), bf16),
         ((TOK, joint), bf16), ((8, WIDE + 2 * STATE), f32)],
        [((STATE, WIDE), bf16), ((ROWS + 8, WIDE), f32), ((ROWS + 8, 2 * STATE), f32),
         (narrow, f32), (tall, bf16), ((ROWS, 2 * STATE), bf16)],
        "last", cost=8,
    )
    e0 = send(head, [(j * 2, j * 2 - 1) for j in range(1, chips)])
    e1 = send(head, [(j * 2 + 1, j * 2 - 1) for j in range(1, chips)])
    message = send(message, swap_pairs)
    value_out, state_out, step_out = call(
        join_kernel,
        [vg_own, sg_own, st_own, message, e0, e1, value_kernel, state_kernel],
        [((TOK, 2 * WIDE), bf16), ((TOK, 4 * STATE), bf16), ((TOK, 2 * HEADS), bf16)],
        (), "join",
    )
    return value_out[None], state_out[None], step_out[None]


def solution(mesh):
    wide = P("pipe", "ctx", "tp")
    placed = (wide, wide, wide, wide, P("tp"), P("tp"), P("tp"), P(None, "tp"), P("tp"), P(None, "tp"), P("tp"))
    return jax.shard_map(
        local, mesh=mesh, in_specs=placed, out_specs=(wide, wide, wide), check_vma=False
    )
```

time: 146 us -> 127 us (0.87)
  waiting for transfers between devices: 6.11 us -> 61 us
  Pallas kernels: 62.6 us -> 31.1 us
  starting transfers between devices: 52.8 us -> 27.5 us
  local copies, waits for them, and re-layouts: 20.2 us -> 5.83 us
  other arithmetic: 1.93 us -> 0 us
    ppermute x24 -> x20, waiting for transfers between devices: 6.11 us -> 61 us  [send(): return lax.ppermute(x, 'ctx', pairs)]
    pallas_call x10 -> x13, Pallas kernels: 62.6 us -> 31.1 us  [call(): pl.pallas_call(kernel, in_specs=[pl.BlockSpec(memory_space=pl.ANY) if k i...]
    ppermute x24 -> x20, starting transfers between devices: 52.2 us -> 25.7 us  [send(): return lax.ppermute(x, 'ctx', pairs)]
    another operation x10 -> x0, local copies, waits for them, and re-layouts: 5.46 us -> none  [the longest x3 2.04 us: local(): r_in = send(jnp.tile(pick(r, 1 - core, HEADS), (1, 4)), swap_pairs)]
    dynamic_slice x6 -> x0, local copies, waits for them, and re-layouts: 3.72 us -> none  [the longest x3 2.19 us: pick(): return lax.dynamic_slice_in_dim(x, group * width, width, 1)]
    unnamed x57 -> x28, local copies, waits for them, and re-layouts: 8.73 us -> 5.83 us
    slice x2 -> x0, local copies, waits for them, and re-layouts: 2.22 us -> none  [the longest x1 1.34 us: tail(): s[TOK - TAIL:, group * 2 * STATE:(group + 1) * 2 * STATE]]
  transfers between devices with their start and end apart: 26 -> 22, of which waited for: 7 -> 9; matrix products, arithmetic and copies ran while one was open for 8% -> 0% of each run, Pallas kernels for 33% -> 20%
where the time goes in v1:
time: 127 us; the launch traced here: 126 us
  waiting for transfers between devices  61 us (48%)
  Pallas kernels  31.1 us (24%)
  starting transfers between devices  27.5 us (22%)
  local copies, waits for them, and re-layouts  5.83 us (5%)
    ppermute x20, waiting for transfers between devices, send(): return lax.ppermute(x, 'ctx', pairs)  61 us
    pallas_call x13, Pallas kernels, call(): pl.pallas_call(kernel, in_specs=[pl.BlockSpec(memory_space=pl.ANY) if k i...  31.1 us
    ppermute x20, starting transfers between devices, send(): return lax.ppermute(x, 'ctx', pairs)  25.7 us
    unnamed x28, local copies, waits for them, and re-layouts  5.83 us
  transfers between devices with their start and end apart: 22, of which 9 were waited for; matrix products, arithmetic and copies ran while one was open for 0% of the time, Pallas kernels for 20%

profile of v1, /device:TPU:15, one launch (start us, length us, event | category | flops | bytes accessed | tf_op | source)
XLA Modules:
  0.0 126.4 jit_solution(3553416223298730655)
XLA Ops:
  7.9 3.5 %collective-permute-start.1 = (bf16[16,2560]{1,0:T(8,128)(2,1)S(1)}, bf16[16,2560]{1,0:T(8,128)(2,1)S(1)}, u32[]{:S(2)}, u32[]{:S(2)}) collective-permute-start(bf16[16,2560]{1,0:T(8,128)(2,1)S(1)} %get-tuple-element.54), channel_id=1, source_target_pairs={{4,12},{12,20},{20,28},{28,36},{36,44},{44,52},{52,60},{5,13},{13,... | collective-permute-start | bytes 245768 | tf_op jit(solution)/shard_map/ppermute | solution.py:540
  11.5 1.3 %collective-permute-start.2 = (bf16[16,2560]{1,0:T(8,128)(2,1)S(1)}, bf16[16,2560]{1,0:T(8,128)(2,1)S(1)}, u32[]{:S(2)}, u32[]{:S(2)}) collective-permute-start(bf16[16,2560]{1,0:T(8,128)(2,1)S(1)} %get-tuple-element.55), channel_id=1, source_target_pairs={{4,8},{12,16},{20,24},{28,32},{36,40},{44,48},{52,56},{5,9},{13,17... | collective-permute-start | bytes 245768 | tf_op jit(solution)/shard_map/ppermute | solution.py:540
  12.8 22.6 %collective-permute-done.1.halo_a = bf16[16,2560]{1,0:T(8,128)(2,1)S(1)} collective-permute-done((bf16[16,2560]{1,0:T(8,128)(2,1)S(1)}, bf16[16,2560]{1,0:T(8,128)(2,1)S(1)}, u32[]{:S(2)}, u32[]{:S(2)}) %collective-permute-start.1) | collective-permute-done | bytes 81952 | tf_op jit(solution)/shard_map/ppermute | solution.py:540
  36.4 7.6 %first.1 = (bf16[272,512]{1,0:T(8,128)(2,1)S(1)}, bf16[272,512]{1,0:T(8,128)(2,1)S(1)}, bf16[272,512]{1,0:T(8,128)(2,1)S(1)}, bf16[272,512]{1,0:T(8,128)(2,1)S(1...) custom-call(bf16[128,4096]{1,0:T(8,128)(2,1)S(1)} %bitcast.13, ...), custom_call_target="tpu_custom_call" | custom-call | bytes 24000000 | tf_op jit(solution)/shard_map/first/pallas_call | solution.py:515
  44.1 2.6 %collective-permute-start.5 = (bf16[272,512]{1,0:T(8,128)(2,1)S(1)}, bf16[272,512]{1,0:T(8,128)(2,1)S(1)}, u32[]{:S(2)}, u32[]{:S(2)}) collective-permute-start(bf16[272,512]{1,0:T(8,128)(2,1)S(1)} %get-tuple-element.59), channel_id=1, source_target_pairs={{0,24},{4,28},{8,0},{12,4},{16,8},{20,12},{24,16},{28,20},{32,56},... | collective-permute-start | bytes 835592 | tf_op jit(solution)/shard_map/ppermute | solution.py:540
  46.7 1.6 %second.1 = (bf16[256,512]{1,0:T(8,128)(2,1)S(1)}, bf16[256,512]{1,0:T(8,128)(2,1)S(1)}, bf16[256,512]{1,0:T(8,128)(2,1)S(1)}, bf16[256,512]{1,0:T(8,128)(2,1)S(...) custom-call(bf16[128,2048]{1,0:T(8,128)(2,1)S(1)} %collective-permute-done.6.g_own, ...), custom_call_target="tpu_custom_call" | custom-call | bytes 12000000 | tf_op jit(solution)/shard_map/second/pallas_call | solution.py:515
  49.0 1.9 %collective-permute-start.9 = (bf16[256,512]{1,0:T(8,128)(2,1)S(1)}, bf16[256,512]{1,0:T(8,128)(2,1)S(1)}, u32[]{:S(2)}, u32[]{:S(2)}) collective-permute-start(bf16[256,512]{1,0:T(8,128)(2,1)S(1)} %get-tuple-element.66), channel_id=1, source_target_pairs={{0,16},{4,20},{8,24},{12,28},{16,0},{20,4},{24,8},{28,12},{32,48},... | collective-permute-start | bytes 786440 | tf_op jit(solution)/shard_map/ppermute | solution.py:540
  50.8 9.9 %collective-permute-done.3.m1.d1 = bf16[272,512]{1,0:T(8,128)(2,1)S(1)} collective-permute-done((bf16[272,512]{1,0:T(8,128)(2,1)S(1)}, bf16[272,512]{1,0:T(8,128)(2,1)S(1)}, u32[]{:S(2)}, u32[]{:S(2)}) %collective-permute-start.3) | collective-permute-done | bytes 278560 | tf_op jit(solution)/shard_map/ppermute | solution.py:540
  61.1 1.3 %collective-permute-start.15 = (bf16[256,512]{1,0:T(8,128)(2,1)S(1)}, bf16[256,512]{1,0:T(8,128)(2,1)S(1)}, u32[]{:S(2)}, u32[]{:S(2)}) collective-permute-start(bf16[256,512]{1,0:T(8,128)(2,1)S(1)} %edge_forward.1), channel_id=1, source_target_pairs={{0,32},{4,36},{8,40},{12,44},{16,48},{20,52},{24,56},{28,60},{1,33... | collective-permute-start | bytes 786440 | tf_op jit(solution)/shard_map/ppermute | solution.py:540
  62.4 8.2 %collective-permute-done.8.d1 = bf16[256,512]{1,0:T(8,128)(2,1)S(1)} collective-permute-done((bf16[256,512]{1,0:T(8,128)(2,1)S(1)}, bf16[256,512]{1,0:T(8,128)(2,1)S(1)}, u32[]{:S(2)}, u32[]{:S(2)}) %collective-permute-start.8) | collective-permute-done | bytes 262176 | tf_op jit(solution)/shard_map/ppermute | solution.py:540
  70.9 1.3 %collective-permute-start.11 = (bf16[256,512]{1,0:T(8,128)(2,1)S(1)}, bf16[256,512]{1,0:T(8,128)(2,1)S(1)}, u32[]{:S(2)}, u32[]{:S(2)}) collective-permute-start(bf16[256,512]{1,0:T(8,128)(2,1)S(1)} %edge_back.1), channel_id=1, source_target_pairs={{32,0},{36,4},{40,8},{44,12},{48,16},{52,20},{56,24},{60,28},{33,1... | collective-permute-start | bytes 786440 | tf_op jit(solution)/shard_map/ppermute | solution.py:540
  72.2 11.2 %inner.1 = (f32[256,2048]{1,0:T(8,128)S(1)}, f32[256,512]{1,0:T(8,128)S(1)}, f32[256,128]{1,0:T(8,128)S(1)}, f32[256,128]{1,0:T(8,128)S(1)}) custom-call(bf16[256,2048]{1,0:T(8,128)(2,1)S(1)} %get-tuple-element.72.x, bf16[256,2048]{1,0:T(8,128)(2,1)S(1)} %get-tuple-element.74.dy, bf16[256,512]{1,0:T(8,128)(2,1)S(1)} %get-tuple-element.62.bc, ...), custom_call_target="tpu_custom_call" | custom-call | bytes 36000000 | tf_op jit(solution)/shard_map/inner/pallas_call | solution.py:515
  85.2 2.1 %collective-permute-start.17 = (bf16[256,512]{1,0:T(8,128)(2,1)S(1)}, bf16[256,512]{1,0:T(8,128)(2,1)S(1)}, u32[]{:S(2)}, u32[]{:S(2)}) collective-permute-start(bf16[256,512]{1,0:T(8,128)(2,1)S(1)} %get-tuple-element.81), channel_id=1, source_target_pairs={{0,16},{4,20},{8,24},{12,28},{16,0},{20,4},{24,8},{28,12},{32,48},... | collective-permute-start | bytes 786440 | tf_op jit(solution)/shard_map/ppermute | solution.py:540
  88.2 2.9 %collective-permute-start.12 = (bf16[256,512]{1,0:T(8,128)(2,1)S(1)}, bf16[256,512]{1,0:T(8,128)(2,1)S(1)}, u32[]{:S(2)}, u32[]{:S(2)}) collective-permute-start(bf16[256,512]{1,0:T(8,128)(2,1)S(1)} %get-tuple-element.69), channel_id=1, source_target_pairs={{0,24},{4,28},{8,0},{12,4},{16,8},{20,12},{24,16},{28,20},{32,56},... | collective-permute-start | bytes 786440 | tf_op jit(solution)/shard_map/ppermute | solution.py:540
  92.0 8.3 %collective-permute-done.18.c3 = bf16[256,512]{1,0:T(8,128)(2,1)S(1)} collective-permute-done((bf16[256,512]{1,0:T(8,128)(2,1)S(1)}, bf16[256,512]{1,0:T(8,128)(2,1)S(1)}, u32[]{:S(2)}, u32[]{:S(2)}) %collective-permute-start.18) | collective-permute-done | bytes 262176 | tf_op jit(solution)/shard_map/ppermute | solution.py:540
  100.3 2.1 %carry.1 = (f32[256,128]{1,0:T(8,128)S(1)}, f32[256,256]{1,0:T(8,128)S(1)}, bf16[256,2048]{1,0:T(8,128)(2,1)S(1)}) custom-call(bf16[256,512]{1,0:T(8,128)(2,1)S(1)} %get-tuple-element.79.c0, bf16[256,512]{1,0:T(8,128)(2,1)S(1)} %collective-permute-done.16.c1, bf16[256,512]{1,0:T(8,128)(2,1)S(1)} %collective-permute-done.17.c2, ...), custom_call_target="tpu_custom_call" | custom-call | bytes 12000000 | tf_op jit(solution)/shard_map/carry/pallas_call | solution.py:515
  102.5 7.3 %collective-permute-done.14.g3 = bf16[256,512]{1,0:T(8,128)(2,1)S(1)} collective-permute-done((bf16[256,512]{1,0:T(8,128)(2,1)S(1)}, bf16[256,512]{1,0:T(8,128)(2,1)S(1)}, u32[]{:S(2)}, u32[]{:S(2)}) %collective-permute-start.14) | collective-permute-done | bytes 262176 | tf_op jit(solution)/shard_map/ppermute | solution.py:540
  109.8 4.4 %last.1 = (bf16[128,2048]{1,0:T(8,128)(2,1)S(1)}, bf16[128,512]{1,0:T(8,128)(2,1)S(1)}, bf16[128,128]{1,0:T(8,128)(2,1)S(1)}, bf16[128,2688]{1,0:T(8,128)(2,1)S(1)}, f32[8,2560]{1,0:T(8,128)S(1)}) custom-call(bf16[256,512]{1,0:T(8,128)(2,1)S(1)} %get-tuple-element.68.g0, bf16[256,512]{1,0:T(8,128)(2,1)S(1)} %collective-permute-done.12.g1, ...), custom_call_target="tpu_custom_call" | custom-call | bytes 24000000 | tf_op jit(solution)/shard_map/last/pallas_call | solution.py:515
  114.2 2.5 %collective-permute-start.19 = (bf16[128,2688]{1,0:T(8,128)(2,1)S(1)}, bf16[128,2688]{1,0:T(8,128)(2,1)S(1)}, u32[]{:S(2)}, u32[]{:S(2)}) collective-permute-start(bf16[128,2688]{1,0:T(8,128)(2,1)S(1)} %get-tuple-element.98), channel_id=1, source_target_pairs={{0,4},{4,0},{8,12},{12,8},{16,20},{20,16},{24,28},{28,24},{32,36},... | collective-permute-start | bytes 2064392 | tf_op jit(solution)/shard_map/ppermute | solution.py:540
  116.7 1.9 %collective-permute-start.21 = (f32[8,2560]{1,0:T(8,128)S(1)}, f32[8,2560]{1,0:T(8,128)S(1)}, u32[]{:S(2)}, u32[]{:S(2)}) collective-permute-start(f32[8,2560]{1,0:T(8,128)S(1)} %get-tuple-element.99), channel_id=1, source_target_pairs={{12,4},{20,12},{28,20},{36,28},{44,36},{52,44},{60,52},{13,5},{21,... | collective-permute-start | bytes 245768 | tf_op jit(solution)/shard_map/ppermute | solution.py:540
  118.6 1.3 %collective-permute-start.20 = (f32[8,2560]{1,0:T(8,128)S(1)}, f32[8,2560]{1,0:T(8,128)S(1)}, u32[]{:S(2)}, u32[]{:S(2)}) collective-permute-start(f32[8,2560]{1,0:T(8,128)S(1)} %get-tuple-element.99), channel_id=1, source_target_pairs={{8,4},{16,12},{24,20},{32,28},{40,36},{48,44},{56,52},{9,5},{17,13... | collective-permute-start | bytes 245768 | tf_op jit(solution)/shard_map/ppermute | solution.py:540
  119.9 2.0 %collective-permute-done.21.e1 = f32[8,2560]{1,0:T(8,128)S(1)} collective-permute-done((f32[8,2560]{1,0:T(8,128)S(1)}, f32[8,2560]{1,0:T(8,128)S(1)}, u32[]{:S(2)}, u32[]{:S(2)}) %collective-permute-start.21) | collective-permute-done | bytes 81952 | tf_op jit(solution)/shard_map/ppermute | solution.py:540
  121.9 2.5 %collective-permute-done.20.e0 = f32[8,2560]{1,0:T(8,128)S(1)} collective-permute-done((f32[8,2560]{1,0:T(8,128)S(1)}, f32[8,2560]{1,0:T(8,128)S(1)}, u32[]{:S(2)}, u32[]{:S(2)}) %collective-permute-start.20) | collective-permute-done | bytes 81952 | tf_op jit(solution)/shard_map/ppermute | solution.py:540
  124.4 1.3 %join.1 = (bf16[128,4096]{1,0:T(8,128)(2,1)}, bf16[128,1024]{1,0:T(8,128)(2,1)}, bf16[128,64]{1,0:T(8,128)(2,1)S(1)}) custom-call(bf16[128,2048]{1,0:T(8,128)(2,1)S(1)} %get-tuple-element.95.v_own, bf16[128,512]{1,0:T(8,128)(2,1)S(1)} %get-tuple-element.96.s_own, bf16[128,128]{1,0:T(8,128)(2,1)S(1)} %get-tuple-element.97.t_own, ...), custom_call_target="tpu_custom_call" | custom-call | tf_op jit(solution)/shard_map/join/pallas_call | solution.py:515
  (61 shorter events, 13.9 us)
Async XLA Ops:
  0.6 34.8 %copy-start.7 = (f32[4,1024]{1,0:T(4,128)S(1)}, f32[4,1024]{1,0:T(4,128)}, u32[]{:S(2)}) copy-start(f32[4,1024]{1,0:T(4,128)} %s_tap.5) | copy-start | bytes 49156
  0.6 34.8 %copy-start.9 = (f32[1024]{0:T(1024)S(1)}, f32[1024]{0:T(1024)}, u32[]{:S(2)}) copy-start(f32[1024]{0:T(1024)} %param.21) | copy-start | bytes 12292
  4.1 31.3 %collective-permute-start = (bf16[128,2688]{1,0:T(8,128)(2,1)S(1)}, bf16[128,2688]{1,0:T(8,128)(2,1)S(1)}, u32[]{:S(2)}, u32[]{:S(2)}) collective-permute-start(bf16[128,2688]{1,0:T(8,128)(2,1)S(1)} %get-tuple-element.53), channel_id=1, source_target_pairs={{0,4},{4,0},{8,12},{12,8},{16,20},{20,16},{24,28},{28,24},{32,36},... | collective-permute-start | bytes 2064392 | tf_op jit(solution)/shard_map/ppermute | solution.py:540
  6.2 40.5 %collective-permute-start.6 = (bf16[128,2048]{1,0:T(8,128)(2,1)S(1)}, bf16[128,2048]{1,0:T(8,128)(2,1)S(1)}, u32[]{:S(2)}, u32[]{:S(2)}) collective-permute-start(bf16[128,2048]{1,0:T(8,128)(2,1)S(1)} %get-tuple-element.60), channel_id=1, source_target_pairs={{0,64},{64,0},{1,65},{65,1},{2,66},{66,2},{3,67},{67,3},{4,68},{68... | collective-permute-start | bytes 1572872 | tf_op jit(solution)/shard_map/ppermute | solution.py:575
  6.8 39.9 %collective-permute-start.7 = (bf16[128,2048]{1,0:T(8,128)(2,1)S(1)}, bf16[128,2048]{1,0:T(8,128)(2,1)S(1)}, u32[]{:S(2)}, u32[]{:S(2)}) collective-permute-start(bf16[128,2048]{1,0:T(8,128)(2,1)S(1)} %get-tuple-element.61), channel_id=1, source_target_pairs={{0,68},{4,64},{8,76},{12,72},{16,84},{20,80},{24,92},{28,88},{32,1... | collective-permute-start | bytes 1572872 | tf_op jit(solution)/shard_map/ppermute | solution.py:576
  7.9 27.5 %collective-permute-start.1 = (bf16[16,2560]{1,0:T(8,128)(2,1)S(1)}, bf16[16,2560]{1,0:T(8,128)(2,1)S(1)}, u32[]{:S(2)}, u32[]{:S(2)}) collective-permute-start(bf16[16,2560]{1,0:T(8,128)(2,1)S(1)} %get-tuple-element.54), channel_id=1, source_target_pairs={{4,12},{12,20},{20,28},{28,36},{36,44},{44,52},{52,60},{5,13},{13,... | collective-permute-start | bytes 245768 | tf_op jit(solution)/shard_map/ppermute | solution.py:540
  11.5 24.0 %collective-permute-start.2 = (bf16[16,2560]{1,0:T(8,128)(2,1)S(1)}, bf16[16,2560]{1,0:T(8,128)(2,1)S(1)}, u32[]{:S(2)}, u32[]{:S(2)}) collective-permute-start(bf16[16,2560]{1,0:T(8,128)(2,1)S(1)} %get-tuple-element.55), channel_id=1, source_target_pairs={{4,8},{12,16},{20,24},{28,32},{36,40},{44,48},{52,56},{5,9},{13,17... | collective-permute-start | bytes 245768 | tf_op jit(solution)/shard_map/ppermute | solution.py:540
  44.0 16.8 %collective-permute-start.3 = (bf16[272,512]{1,0:T(8,128)(2,1)S(1)}, bf16[272,512]{1,0:T(8,128)(2,1)S(1)}, u32[]{:S(2)}, u32[]{:S(2)}) collective-permute-start(bf16[272,512]{1,0:T(8,128)(2,1)S(1)} %get-tuple-element.57), channel_id=1, source_target_pairs={{0,8},{4,12},{8,16},{12,20},{16,24},{20,28},{24,0},{28,4},{32,40},... | collective-permute-start | bytes 835592 | tf_op jit(solution)/shard_map/ppermute | solution.py:540
  44.1 16.7 %collective-permute-start.4 = (bf16[272,512]{1,0:T(8,128)(2,1)S(1)}, bf16[272,512]{1,0:T(8,128)(2,1)S(1)}, u32[]{:S(2)}, u32[]{:S(2)}) collective-permute-start(bf16[272,512]{1,0:T(8,128)(2,1)S(1)} %get-tuple-element.58), channel_id=1, source_target_pairs={{0,16},{4,20},{8,24},{12,28},{16,0},{20,4},{24,8},{28,12},{32,48},... | collective-permute-start | bytes 835592 | tf_op jit(solution)/shard_map/ppermute | solution.py:540
  44.1 16.6 %collective-permute-start.5 = (bf16[272,512]{1,0:T(8,128)(2,1)S(1)}, bf16[272,512]{1,0:T(8,128)(2,1)S(1)}, u32[]{:S(2)}, u32[]{:S(2)}) collective-permute-start(bf16[272,512]{1,0:T(8,128)(2,1)S(1)} %get-tuple-element.59), channel_id=1, source_target_pairs={{0,24},{4,28},{8,0},{12,4},{16,8},{20,12},{24,16},{28,20},{32,56},... | collective-permute-start | bytes 835592 | tf_op jit(solution)/shard_map/ppermute | solution.py:540
  48.3 22.3 %collective-permute-start.8 = (bf16[256,512]{1,0:T(8,128)(2,1)S(1)}, bf16[256,512]{1,0:T(8,128)(2,1)S(1)}, u32[]{:S(2)}, u32[]{:S(2)}) collective-permute-start(bf16[256,512]{1,0:T(8,128)(2,1)S(1)} %get-tuple-element.65), channel_id=1, source_target_pairs={{0,8},{4,12},{8,16},{12,20},{16,24},{20,28},{24,0},{28,4},{32,40},... | collective-permute-start | bytes 786440 | tf_op jit(solution)/shard_map/ppermute | solution.py:540
  49.0 21.6 %collective-permute-start.9 = (bf16[256,512]{1,0:T(8,128)(2,1)S(1)}, bf16[256,512]{1,0:T(8,128)(2,1)S(1)}, u32[]{:S(2)}, u32[]{:S(2)}) collective-permute-start(bf16[256,512]{1,0:T(8,128)(2,1)S(1)} %get-tuple-element.66), channel_id=1, source_target_pairs={{0,16},{4,20},{8,24},{12,28},{16,0},{20,4},{24,8},{28,12},{32,48},... | collective-permute-start | bytes 786440 | tf_op jit(solution)/shard_map/ppermute | solution.py:540
  60.7 9.8 %collective-permute-start.10 = (bf16[256,512]{1,0:T(8,128)(2,1)S(1)}, bf16[256,512]{1,0:T(8,128)(2,1)S(1)}, u32[]{:S(2)}, u32[]{:S(2)}) collective-permute-start(bf16[256,512]{1,0:T(8,128)(2,1)S(1)} %get-tuple-element.67), channel_id=1, source_target_pairs={{0,24},{4,28},{8,0},{12,4},{16,8},{20,12},{24,16},{28,20},{32,56},... | collective-permute-start | bytes 786440 | tf_op jit(solution)/shard_map/ppermute | solution.py:540
  61.1 22.4 %collective-permute-start.15 = (bf16[256,512]{1,0:T(8,128)(2,1)S(1)}, bf16[256,512]{1,0:T(8,128)(2,1)S(1)}, u32[]{:S(2)}, u32[]{:S(2)}) collective-permute-start(bf16[256,512]{1,0:T(8,128)(2,1)S(1)} %edge_forward.1), channel_id=1, source_target_pairs={{0,32},{4,36},{8,40},{12,44},{16,48},{20,52},{24,56},{28,60},{1,33... | collective-permute-start | bytes 786440 | tf_op jit(solution)/shard_map/ppermute | solution.py:540
  70.9 16.4 %collective-permute-start.11 = (bf16[256,512]{1,0:T(8,128)(2,1)S(1)}, bf16[256,512]{1,0:T(8,128)(2,1)S(1)}, u32[]{:S(2)}, u32[]{:S(2)}) collective-permute-start(bf16[256,512]{1,0:T(8,128)(2,1)S(1)} %edge_back.1), channel_id=1, source_target_pairs={{32,0},{36,4},{40,8},{44,12},{48,16},{52,20},{56,24},{60,28},{33,1... | collective-permute-start | bytes 786440 | tf_op jit(solution)/shard_map/ppermute | solution.py:540
  84.4 6.7 %collective-permute-start.16 = (bf16[256,512]{1,0:T(8,128)(2,1)S(1)}, bf16[256,512]{1,0:T(8,128)(2,1)S(1)}, u32[]{:S(2)}, u32[]{:S(2)}) collective-permute-start(bf16[256,512]{1,0:T(8,128)(2,1)S(1)} %get-tuple-element.80), channel_id=1, source_target_pairs={{0,24},{4,28},{8,0},{12,4},{16,8},{20,12},{24,16},{28,20},{32,56},... | collective-permute-start | bytes 786440 | tf_op jit(solution)/shard_map/ppermute | solution.py:540
  85.2 6.8 %collective-permute-start.17 = (bf16[256,512]{1,0:T(8,128)(2,1)S(1)}, bf16[256,512]{1,0:T(8,128)(2,1)S(1)}, u32[]{:S(2)}, u32[]{:S(2)}) collective-permute-start(bf16[256,512]{1,0:T(8,128)(2,1)S(1)} %get-tuple-element.81), channel_id=1, source_target_pairs={{0,16},{4,20},{8,24},{12,28},{16,0},{20,4},{24,8},{28,12},{32,48},... | collective-permute-start | bytes 786440 | tf_op jit(solution)/shard_map/ppermute | solution.py:540
  87.3 13.0 %collective-permute-start.18 = (bf16[256,512]{1,0:T(8,128)(2,1)S(1)}, bf16[256,512]{1,0:T(8,128)(2,1)S(1)}, u32[]{:S(2)}, u32[]{:S(2)}) collective-permute-start(bf16[256,512]{1,0:T(8,128)(2,1)S(1)} %get-tuple-element.82), channel_id=1, source_target_pairs={{0,8},{4,12},{8,16},{12,20},{16,24},{20,28},{24,0},{28,4},{32,40},... | collective-permute-start | bytes 786440 | tf_op jit(solution)/shard_map/ppermute | solution.py:540
  88.2 14.3 %collective-permute-start.12 = (bf16[256,512]{1,0:T(8,128)(2,1)S(1)}, bf16[256,512]{1,0:T(8,128)(2,1)S(1)}, u32[]{:S(2)}, u32[]{:S(2)}) collective-permute-start(bf16[256,512]{1,0:T(8,128)(2,1)S(1)} %get-tuple-element.69), channel_id=1, source_target_pairs={{0,24},{4,28},{8,0},{12,4},{16,8},{20,12},{24,16},{28,20},{32,56},... | collective-permute-start | bytes 786440 | tf_op jit(solution)/shard_map/ppermute | solution.py:540
  91.1 11.4 %collective-permute-start.13 = (bf16[256,512]{1,0:T(8,128)(2,1)S(1)}, bf16[256,512]{1,0:T(8,128)(2,1)S(1)}, u32[]{:S(2)}, u32[]{:S(2)}) collective-permute-start(bf16[256,512]{1,0:T(8,128)(2,1)S(1)} %get-tuple-element.70), channel_id=1, source_target_pairs={{0,16},{4,20},{8,24},{12,28},{16,0},{20,4},{24,8},{28,12},{32,48},... | collective-permute-start | bytes 786440 | tf_op jit(solution)/shard_map/ppermute | solution.py:540
  91.1 18.7 %collective-permute-start.14 = (bf16[256,512]{1,0:T(8,128)(2,1)S(1)}, bf16[256,512]{1,0:T(8,128)(2,1)S(1)}, u32[]{:S(2)}, u32[]{:S(2)}) collective-permute-start(bf16[256,512]{1,0:T(8,128)(2,1)S(1)} %get-tuple-element.71), channel_id=1, source_target_pairs={{0,8},{4,12},{8,16},{12,20},{16,24},{20,28},{24,0},{28,4},{32,40},... | collective-permute-start | bytes 786440 | tf_op jit(solution)/shard_map/ppermute | solution.py:540
  114.2 10.2 %collective-permute-start.19 = (bf16[128,2688]{1,0:T(8,128)(2,1)S(1)}, bf16[128,2688]{1,0:T(8,128)(2,1)S(1)}, u32[]{:S(2)}, u32[]{:S(2)}) collective-permute-start(bf16[128,2688]{1,0:T(8,128)(2,1)S(1)} %get-tuple-element.98), channel_id=1, source_target_pairs={{0,4},{4,0},{8,12},{12,8},{16,20},{20,16},{24,28},{28,24},{32,36},... | collective-permute-start | bytes 2064392 | tf_op jit(solution)/shard_map/ppermute | solution.py:540
  116.7 5.2 %collective-permute-start.21 = (f32[8,2560]{1,0:T(8,128)S(1)}, f32[8,2560]{1,0:T(8,128)S(1)}, u32[]{:S(2)}, u32[]{:S(2)}) collective-permute-start(f32[8,2560]{1,0:T(8,128)S(1)} %get-tuple-element.99), channel_id=1, source_target_pairs={{12,4},{20,12},{28,20},{36,28},{44,36},{52,44},{60,52},{13,5},{21,... | collective-permute-start | bytes 245768 | tf_op jit(solution)/shard_map/ppermute | solution.py:540
  118.6 5.8 %collective-permute-start.20 = (f32[8,2560]{1,0:T(8,128)S(1)}, f32[8,2560]{1,0:T(8,128)S(1)}, u32[]{:S(2)}, u32[]{:S(2)}) collective-permute-start(f32[8,2560]{1,0:T(8,128)S(1)} %get-tuple-element.99), channel_id=1, source_target_pairs={{8,4},{16,12},{24,20},{32,28},{40,36},{48,44},{56,52},{9,5},{17,13... | collective-permute-start | bytes 245768 | tf_op jit(solution)/shard_map/ppermute | solution.py:540
  (11 other events, 205.3 us)

commit v2 on v1

--- a/solution.py
+++ b/solution.py
@@ -80,6 +80,12 @@
     x = x.astype(f32)
     mine = jnp.where(group == 0, x[:, :HEADS], x[:, HEADS:])
     return jnp.concatenate([mine] * 4, axis=1)
+
+
+def tiled_steps(x, group):
+    x = x.astype(f32)
+    mine = jnp.where(group == 0, x[:HEADS], x[HEADS:])
+    return jnp.concatenate([mine] * 4, axis=0).T
 
 
 def softplus(x):
@@ -115,7 +121,7 @@
     copies = [pltpu.make_async_copy(a, b, sems.at[k]) for k, (a, b) in enumerate(copies)]
     for copy in copies:
         copy.start()
-    message[:, WIDE + 2 * STATE :] = tiled_heads(r[...], there).astype(bf16)
+    message[:, WIDE + 2 * STATE :] = tiled_steps(r[...], there).astype(bf16)
     for copy in copies:
         copy.wait()
 
@@ -147,7 +153,7 @@
 ):
     core, ring = place()
     mine, other = rows_of(core)
-    raw[mine, :] = tiled_heads(r[...], core)
+    raw[mine, :] = tiled_steps(r[...], core)
     raw[other, :] = message[:, WIDE + 2 * STATE :].astype(f32)
     pre = raw[...] + tiled_heads(step_bias[...], core)
     delta = softplus(pre)
@@ -503,11 +509,11 @@
             patch(v_out, v_tap, edge, WIDE, group, 0)
             patch(s_out, s_tap, edge, 2 * STATE, group, WIDE)
 
-    own = t_own[:, :HEADS].astype(f32)
-    arrived = message[:, WIDE + 2 * STATE : WIDE + 2 * STATE + HEADS].astype(f32)
+    own = t_own[...].astype(f32).T[:HEADS]
+    arrived = message[:, WIDE + 2 * STATE :].astype(f32).T[:HEADS]
     low = jnp.where(core == 0, own, arrived)
     high = jnp.where(core == 0, arrived, own)
-    t_out[...] = jnp.concatenate([low, high], axis=1).astype(bf16)
+    t_out[...] = jnp.concatenate([low, high], axis=0).astype(bf16)
 
 
 def call(kernel, args, outs, scratch=(), name=None, anywhere=(), cost=None):
@@ -515,7 +521,7 @@
     return pl.pallas_call(
         kernel,
         in_specs=[
-            pl.BlockSpec(memory_space=pl.ANY) if k in anywhere else vmem for k in range(len(args))
+            pl.BlockSpec(memory_space=pltpu.HBM) if k in anywhere else vmem for k in range(len(args))
         ],
         out_specs=[vmem for _ in outs],
         out_shape=[jax.ShapeDtypeStruct(*o) for o in outs],
@@ -552,7 +558,7 @@
         return out
 
     row = lambda x: x.reshape(1, -1)
-    v, s, r, g = value_input[0], state_input[0], step_raw[0], upstream[0]
+    v, s, r, g = value_input[0], state_input[0], step_raw[0].T, upstream[0]
     bias, rate_log, skip = row(step_bias), row(decay_log), row(skip_gain)
     joint = WIDE + 2 * STATE + 128
     tall = (ROWS, WIDE)
@@ -569,6 +575,7 @@
     message = send(message, swap_pairs)
     halo_a = send(halo_a, [(k * 2 + 1, k * 2 + 3) for k in range(chips - 1)])
     halo_b = send(halo_b, [(k * 2 + 1, k * 2 + 2) for k in range(chips - 1)])
+    g, message, halo_a, halo_b = lax.optimization_barrier((g, message, halo_a, halo_b))
     g_own, g_in = call(
         pack_grad_kernel, [g], [((TOK, WIDE), bf16)] * 2, [sems((2,))], "pack_grad", (0,)
     )
@@ -646,10 +653,10 @@
     value_out, state_out, step_out = call(
         join_kernel,
         [vg_own, sg_own, st_own, message, e0, e1, value_kernel, state_kernel],
-        [((TOK, 2 * WIDE), bf16), ((TOK, 4 * STATE), bf16), ((TOK, 2 * HEADS), bf16)],
+        [((TOK, 2 * WIDE), bf16), ((TOK, 4 * STATE), bf16), ((2 * HEADS, TOK), bf16)],
         (), "join",
     )
-    return value_out[None], state_out[None], step_out[None]
+    return value_out[None], state_out[None], step_out.T[None]
 
 
 def solution(mesh):

time: 127 us -> 108 us (0.85)
  waiting for transfers between devices: 61 us -> 37.1 us
  starting transfers between devices: 27.5 us -> 31.5 us
    ppermute x20, waiting for transfers between devices: 61 us -> 28.3 us  [send(): return lax.ppermute(x, 'ctx', pairs)]
    ppermute x1, waiting for transfers between devices: 0.01 us -> 8.77 us  [local(): lax.ppermute(g_in, ('pipe', 'ctx'), [(p * count + i, (1 - p) * count + (i...]
    ppermute x20, starting transfers between devices: 25.7 us -> 27.8 us  [send(): return lax.ppermute(x, 'ctx', pairs)]
    ppermute x1, starting transfers between devices: 1.1 us -> 3.07 us  [local(): lax.ppermute(g_in, ('pipe', 'ctx'), [(p * count + i, (1 - p) * count + (i...]
    unnamed x28 -> x30, local copies, waits for them, and re-layouts: 5.83 us -> 6.43 us
  transfers between devices with their start and end apart: 22 -> 22, of which waited for: 9 -> 11; matrix products, arithmetic and copies ran while one was open for 0% -> 0% of each run, Pallas kernels for 20% -> 23%
where the time goes in v2:
time: 108 us; the launch traced here: 107 us
  waiting for transfers between devices  37.1 us (34%)
  starting transfers between devices  31.5 us (29%)
  Pallas kernels  31.1 us (29%)
  local copies, waits for them, and re-layouts  6.43 us (6%)
    pallas_call x13, Pallas kernels, call(): pl.pallas_call(kernel, in_specs=[pl.BlockSpec(memory_space=pltpu.HBM) if...  31.1 us
    ppermute x20, waiting for transfers between devices, send(): return lax.ppermute(x, 'ctx', pairs)  28.3 us
    ppermute x20, starting transfers between devices, send(): return lax.ppermute(x, 'ctx', pairs)  27.8 us
    ppermute x1, waiting for transfers between devices, local(): lax.ppermute(g_in, ('pipe', 'ctx'), [(p * count + i, (1 - p) * count + (i...  8.77 us
    unnamed x30, local copies, waits for them, and re-layouts  6.43 us
    ppermute x1, starting transfers between devices, local(): lax.ppermute(g_in, ('pipe', 'ctx'), [(p * count + i, (1 - p) * count + (i...  3.07 us
  transfers between devices with their start and end apart: 22, of which 11 were waited for; matrix products, arithmetic and copies ran while one was open for 0% of the time, Pallas kernels for 23%

profile of v2, /device:TPU:15, one launch (start us, length us, event | category | flops | bytes accessed | tf_op | source)
XLA Modules:
  0.0 107.0 jit_solution(10297637798011602035)
XLA Ops:
  4.7 3.5 %collective-permute-start.1 = (bf16[16,2560]{1,0:T(8,128)(2,1)S(1)}, bf16[16,2560]{1,0:T(8,128)(2,1)S(1)}, u32[]{:S(2)}, u32[]{:S(2)}) collective-permute-start(bf16[16,2560]{1,0:T(8,128)(2,1)S(1)} %get-tuple-element.58), channel_id=1, source_target_pairs={{4,12},{12,20},{20,28},{28,36},{36,44},{44,52},{52,60},{5,13},{13,... | collective-permute-start | bytes 245768 | tf_op jit(solution)/shard_map/ppermute | solution.py:546
  8.2 1.3 %collective-permute-start.2 = (bf16[16,2560]{1,0:T(8,128)(2,1)S(1)}, bf16[16,2560]{1,0:T(8,128)(2,1)S(1)}, u32[]{:S(2)}, u32[]{:S(2)}) collective-permute-start(bf16[16,2560]{1,0:T(8,128)(2,1)S(1)} %get-tuple-element.59), channel_id=1, source_target_pairs={{4,8},{12,16},{20,24},{28,32},{36,40},{44,48},{52,56},{5,9},{13,17... | collective-permute-start | bytes 245768 | tf_op jit(solution)/shard_map/ppermute | solution.py:546
  9.5 3.9 %collective-permute-done.1.halo_a = bf16[16,2560]{1,0:T(8,128)(2,1)S(1)} collective-permute-done((bf16[16,2560]{1,0:T(8,128)(2,1)S(1)}, bf16[16,2560]{1,0:T(8,128)(2,1)S(1)}, u32[]{:S(2)}, u32[]{:S(2)}) %collective-permute-start.1) | collective-permute-done | bytes 81952 | tf_op jit(solution)/shard_map/ppermute | solution.py:546
  15.4 3.1 %collective-permute-start.7 = (bf16[128,2048]{1,0:T(8,128)(2,1)S(1)}, bf16[128,2048]{1,0:T(8,128)(2,1)S(1)}, u32[]{:S(2)}, u32[]{:S(2)}) collective-permute-start(bf16[128,2048]{1,0:T(8,128)(2,1)S(1)} %get-tuple-element.69), channel_id=1, source_target_pairs={{0,68},{4,64},{8,76},{12,72},{16,84},{20,80},{24,92},{28,88},{32,1... | collective-permute-start | bytes 1572872 | tf_op jit(solution)/shard_map/ppermute | solution.py:583
  20.9 7.6 %first.1 = (bf16[272,512]{1,0:T(8,128)(2,1)S(1)}, bf16[272,512]{1,0:T(8,128)(2,1)S(1)}, bf16[272,512]{1,0:T(8,128)(2,1)S(1)}, bf16[272,512]{1,0:T(8,128)(2,1)S(1...) custom-call(bf16[128,4096]{1,0:T(8,128)(2,1)S(1)} %bitcast.17, ...), custom_call_target="tpu_custom_call" | custom-call | bytes 24000000 | tf_op jit(solution)/shard_map/first/pallas_call | solution.py:521
  28.6 1.3 %collective-permute-start.4 = (bf16[272,512]{1,0:T(8,128)(2,1)S(1)}, bf16[272,512]{1,0:T(8,128)(2,1)S(1)}, u32[]{:S(2)}, u32[]{:S(2)}) collective-permute-start(bf16[272,512]{1,0:T(8,128)(2,1)S(1)} %get-tuple-element.65), channel_id=1, source_target_pairs={{0,16},{4,20},{8,24},{12,28},{16,0},{20,4},{24,8},{28,12},{32,48},... | collective-permute-start | bytes 835592 | tf_op jit(solution)/shard_map/ppermute | solution.py:546
  29.9 1.4 %collective-permute-start.5 = (bf16[272,512]{1,0:T(8,128)(2,1)S(1)}, bf16[272,512]{1,0:T(8,128)(2,1)S(1)}, u32[]{:S(2)}, u32[]{:S(2)}) collective-permute-start(bf16[272,512]{1,0:T(8,128)(2,1)S(1)} %get-tuple-element.66), channel_id=1, source_target_pairs={{0,24},{4,28},{8,0},{12,4},{16,8},{20,12},{24,16},{28,20},{32,56},... | collective-permute-start | bytes 835592 | tf_op jit(solution)/shard_map/ppermute | solution.py:546
  31.3 8.8 %collective-permute-done.7.g_in = bf16[128,2048]{1,0:T(8,128)(2,1)S(1)} collective-permute-done((bf16[128,2048]{1,0:T(8,128)(2,1)S(1)}, bf16[128,2048]{1,0:T(8,128)(2,1)S(1)}, u32[]{:S(2)}, u32[]{:S(2)}) %collective-permute-start.7) | collective-permute-done | bytes 524320 | tf_op jit(solution)/shard_map/ppermute | solution.py:583
  40.1 1.6 %second.1 = (bf16[256,512]{1,0:T(8,128)(2,1)S(1)}, bf16[256,512]{1,0:T(8,128)(2,1)S(1)}, bf16[256,512]{1,0:T(8,128)(2,1)S(1)}, bf16[256,512]{1,0:T(8,128)(2,1)S(...) custom-call(bf16[128,2048]{1,0:T(8,128)(2,1)S(1)} %collective-permute-done.6.g_own, ...), custom_call_target="tpu_custom_call" | custom-call | bytes 12000000 | tf_op jit(solution)/shard_map/second/pallas_call | solution.py:521
  41.7 1.3 %collective-permute-start.9 = (bf16[256,512]{1,0:T(8,128)(2,1)S(1)}, bf16[256,512]{1,0:T(8,128)(2,1)S(1)}, u32[]{:S(2)}, u32[]{:S(2)}) collective-permute-start(bf16[256,512]{1,0:T(8,128)(2,1)S(1)} %get-tuple-element.74), channel_id=1, source_target_pairs={{0,16},{4,20},{8,24},{12,28},{16,0},{20,4},{24,8},{28,12},{32,48},... | collective-permute-start | bytes 786440 | tf_op jit(solution)/shard_map/ppermute | solution.py:546
  46.6 11.3 %inner.1 = (f32[256,2048]{1,0:T(8,128)S(1)}, f32[256,512]{1,0:T(8,128)S(1)}, f32[256,128]{1,0:T(8,128)S(1)}, f32[256,128]{1,0:T(8,128)S(1)}) custom-call(bf16[256,2048]{1,0:T(8,128)(2,1)S(1)} %get-tuple-element.80.x, bf16[256,2048]{1,0:T(8,128)(2,1)S(1)} %get-tuple-element.82.dy, bf16[256,512]{1,0:T(8,128)(2,1)S(1)} %get-tuple-element.70.bc, ...), custom_call_target="tpu_custom_call" | custom-call | bytes 36000000 | tf_op jit(solution)/shard_map/inner/pallas_call | solution.py:521
  58.2 5.5 %collective-permute-start.11 = (bf16[256,512]{1,0:T(8,128)(2,1)S(1)}, bf16[256,512]{1,0:T(8,128)(2,1)S(1)}, u32[]{:S(2)}, u32[]{:S(2)}) collective-permute-start(bf16[256,512]{1,0:T(8,128)(2,1)S(1)} %edge_back.1), channel_id=1, source_target_pairs={{32,0},{36,4},{40,8},{44,12},{48,16},{52,20},{56,24},{60,28},{33,1... | collective-permute-start | bytes 786440 | tf_op jit(solution)/shard_map/ppermute | solution.py:546
  64.7 2.1 %collective-permute-start.16 = (bf16[256,512]{1,0:T(8,128)(2,1)S(1)}, bf16[256,512]{1,0:T(8,128)(2,1)S(1)}, u32[]{:S(2)}, u32[]{:S(2)}) collective-permute-start(bf16[256,512]{1,0:T(8,128)(2,1)S(1)} %get-tuple-element.88), channel_id=1, source_target_pairs={{0,24},{4,28},{8,0},{12,4},{16,8},{20,12},{24,16},{28,20},{32,56},... | collective-permute-start | bytes 786440 | tf_op jit(solution)/shard_map/ppermute | solution.py:546
  67.4 1.3 %collective-permute-done.11.edge = bf16[256,512]{1,0:T(8,128)(2,1)S(1)} collective-permute-done((bf16[256,512]{1,0:T(8,128)(2,1)S(1)}, bf16[256,512]{1,0:T(8,128)(2,1)S(1)}, u32[]{:S(2)}, u32[]{:S(2)}) %collective-permute-start.11) | collective-permute-done | bytes 262176 | tf_op jit(solution)/shard_map/ppermute | solution.py:546
  69.7 2.2 %collective-permute-start.12 = (bf16[256,512]{1,0:T(8,128)(2,1)S(1)}, bf16[256,512]{1,0:T(8,128)(2,1)S(1)}, u32[]{:S(2)}, u32[]{:S(2)}) collective-permute-start(bf16[256,512]{1,0:T(8,128)(2,1)S(1)} %get-tuple-element.77), channel_id=1, source_target_pairs={{0,24},{4,28},{8,0},{12,4},{16,8},{20,12},{24,16},{28,20},{32,56},... | collective-permute-start | bytes 786440 | tf_op jit(solution)/shard_map/ppermute | solution.py:546
  73.3 1.6 %collective-permute-done.17.c2 = bf16[256,512]{1,0:T(8,128)(2,1)S(1)} collective-permute-done((bf16[256,512]{1,0:T(8,128)(2,1)S(1)}, bf16[256,512]{1,0:T(8,128)(2,1)S(1)}, u32[]{:S(2)}, u32[]{:S(2)}) %collective-permute-start.17) | collective-permute-done | bytes 262176 | tf_op jit(solution)/shard_map/ppermute | solution.py:546
  74.9 7.8 %collective-permute-done.18.c3 = bf16[256,512]{1,0:T(8,128)(2,1)S(1)} collective-permute-done((bf16[256,512]{1,0:T(8,128)(2,1)S(1)}, bf16[256,512]{1,0:T(8,128)(2,1)S(1)}, u32[]{:S(2)}, u32[]{:S(2)}) %collective-permute-start.18) | collective-permute-done | bytes 262176 | tf_op jit(solution)/shard_map/ppermute | solution.py:546
  82.7 2.1 %carry.1 = (f32[256,128]{1,0:T(8,128)S(1)}, f32[256,256]{1,0:T(8,128)S(1)}, bf16[256,2048]{1,0:T(8,128)(2,1)S(1)}) custom-call(bf16[256,512]{1,0:T(8,128)(2,1)S(1)} %get-tuple-element.87.c0, bf16[256,512]{1,0:T(8,128)(2,1)S(1)} %collective-permute-done.16.c1, bf16[256,512]{1,0:T(8,128)(2,1)S(1)} %collective-permute-done.17.c2, ...), custom_call_target="tpu_custom_call" | custom-call | bytes 12000000 | tf_op jit(solution)/shard_map/carry/pallas_call | solution.py:521
  84.9 1.3 %collective-permute-done.13.g2 = bf16[256,512]{1,0:T(8,128)(2,1)S(1)} collective-permute-done((bf16[256,512]{1,0:T(8,128)(2,1)S(1)}, bf16[256,512]{1,0:T(8,128)(2,1)S(1)}, u32[]{:S(2)}, u32[]{:S(2)}) %collective-permute-start.13) | collective-permute-done | bytes 262176 | tf_op jit(solution)/shard_map/ppermute | solution.py:546
  86.2 6.6 %collective-permute-done.14.g3 = bf16[256,512]{1,0:T(8,128)(2,1)S(1)} collective-permute-done((bf16[256,512]{1,0:T(8,128)(2,1)S(1)}, bf16[256,512]{1,0:T(8,128)(2,1)S(1)}, u32[]{:S(2)}, u32[]{:S(2)}) %collective-permute-start.14) | collective-permute-done | bytes 262176 | tf_op jit(solution)/shard_map/ppermute | solution.py:546
  92.8 4.3 %last.1 = (bf16[128,2048]{1,0:T(8,128)(2,1)S(1)}, bf16[128,512]{1,0:T(8,128)(2,1)S(1)}, bf16[128,128]{1,0:T(8,128)(2,1)S(1)}, bf16[128,2688]{1,0:T(8,128)(2,1)S(1)}, f32[8,2560]{1,0:T(8,128)S(1)}) custom-call(bf16[256,512]{1,0:T(8,128)(2,1)S(1)} %get-tuple-element.76.g0, bf16[256,512]{1,0:T(8,128)(2,1)S(1)} %collective-permute-done.12.g1, ...), custom_call_target="tpu_custom_call" | custom-call | bytes 24000000 | tf_op jit(solution)/shard_map/last/pallas_call | solution.py:521
  98.0 1.9 %collective-permute-start.21 = (f32[8,2560]{1,0:T(8,128)S(1)}, f32[8,2560]{1,0:T(8,128)S(1)}, u32[]{:S(2)}, u32[]{:S(2)}) collective-permute-start(f32[8,2560]{1,0:T(8,128)S(1)} %get-tuple-element.107), channel_id=1, source_target_pairs={{12,4},{20,12},{28,20},{36,28},{44,36},{52,44},{60,52},{13,5},{21,... | collective-permute-start | bytes 245768 | tf_op jit(solution)/shard_map/ppermute | solution.py:546
  101.2 2.0 %collective-permute-done.21.e1 = f32[8,2560]{1,0:T(8,128)S(1)} collective-permute-done((f32[8,2560]{1,0:T(8,128)S(1)}, f32[8,2560]{1,0:T(8,128)S(1)}, u32[]{:S(2)}, u32[]{:S(2)}) %collective-permute-start.21) | collective-permute-done | bytes 81952 | tf_op jit(solution)/shard_map/ppermute | solution.py:546
  103.2 2.5 %collective-permute-done.20.e0 = f32[8,2560]{1,0:T(8,128)S(1)} collective-permute-done((f32[8,2560]{1,0:T(8,128)S(1)}, f32[8,2560]{1,0:T(8,128)S(1)}, u32[]{:S(2)}, u32[]{:S(2)}) %collective-permute-start.20) | collective-permute-done | bytes 81952 | tf_op jit(solution)/shard_map/ppermute | solution.py:546
  (63 shorter events, 19.7 us)
Async XLA Ops:
  0.6 17.9 %copy-start.11 = (f32[1024]{0:T(1024)S(1)}, f32[1024]{0:T(1024)}, u32[]{:S(2)}) copy-start(f32[1024]{0:T(1024)} %param.21) | copy-start | bytes 12292
  3.9 9.5 %collective-permute-start = (bf16[128,2688]{1,0:T(8,128)(2,1)S(1)}, bf16[128,2688]{1,0:T(8,128)(2,1)S(1)}, u32[]{:S(2)}, u32[]{:S(2)}) collective-permute-start(bf16[128,2688]{1,0:T(8,128)(2,1)S(1)} %get-tuple-element.57), channel_id=1, source_target_pairs={{0,4},{4,0},{8,12},{12,8},{16,20},{20,16},{24,28},{28,24},{32,36},... | collective-permute-start | bytes 2064392 | tf_op jit(solution)/shard_map/ppermute | solution.py:546
  4.7 8.8 %collective-permute-start.1 = (bf16[16,2560]{1,0:T(8,128)(2,1)S(1)}, bf16[16,2560]{1,0:T(8,128)(2,1)S(1)}, u32[]{:S(2)}, u32[]{:S(2)}) collective-permute-start(bf16[16,2560]{1,0:T(8,128)(2,1)S(1)} %get-tuple-element.58), channel_id=1, source_target_pairs={{4,12},{12,20},{20,28},{28,36},{36,44},{44,52},{52,60},{5,13},{13,... | collective-permute-start | bytes 245768 | tf_op jit(solution)/shard_map/ppermute | solution.py:546
  8.2 5.2 %collective-permute-start.2 = (bf16[16,2560]{1,0:T(8,128)(2,1)S(1)}, bf16[16,2560]{1,0:T(8,128)(2,1)S(1)}, u32[]{:S(2)}, u32[]{:S(2)}) collective-permute-start(bf16[16,2560]{1,0:T(8,128)(2,1)S(1)} %get-tuple-element.59), channel_id=1, source_target_pairs={{4,8},{12,16},{20,24},{28,32},{36,40},{44,48},{52,56},{5,9},{13,17... | collective-permute-start | bytes 245768 | tf_op jit(solution)/shard_map/ppermute | solution.py:546
  14.8 16.5 %collective-permute-start.6 = (bf16[128,2048]{1,0:T(8,128)(2,1)S(1)}, bf16[128,2048]{1,0:T(8,128)(2,1)S(1)}, u32[]{:S(2)}, u32[]{:S(2)}) collective-permute-start(bf16[128,2048]{1,0:T(8,128)(2,1)S(1)} %get-tuple-element.68), channel_id=1, source_target_pairs={{0,64},{64,0},{1,65},{65,1},{2,66},{66,2},{3,67},{67,3},{4,68},{68... | collective-permute-start | bytes 1572872 | tf_op jit(solution)/shard_map/ppermute | solution.py:582
  15.4 24.6 %collective-permute-start.7 = (bf16[128,2048]{1,0:T(8,128)(2,1)S(1)}, bf16[128,2048]{1,0:T(8,128)(2,1)S(1)}, u32[]{:S(2)}, u32[]{:S(2)}) collective-permute-start(bf16[128,2048]{1,0:T(8,128)(2,1)S(1)} %get-tuple-element.69), channel_id=1, source_target_pairs={{0,68},{4,64},{8,76},{12,72},{16,84},{20,80},{24,92},{28,88},{32,1... | collective-permute-start | bytes 1572872 | tf_op jit(solution)/shard_map/ppermute | solution.py:583
  28.5 15.3 %collective-permute-start.3 = (bf16[272,512]{1,0:T(8,128)(2,1)S(1)}, bf16[272,512]{1,0:T(8,128)(2,1)S(1)}, u32[]{:S(2)}, u32[]{:S(2)}) collective-permute-start(bf16[272,512]{1,0:T(8,128)(2,1)S(1)} %get-tuple-element.64), channel_id=1, source_target_pairs={{0,8},{4,12},{8,16},{12,20},{16,24},{20,28},{24,0},{28,4},{32,40},... | collective-permute-start | bytes 835592 | tf_op jit(solution)/shard_map/ppermute | solution.py:546
  28.6 16.0 %collective-permute-start.4 = (bf16[272,512]{1,0:T(8,128)(2,1)S(1)}, bf16[272,512]{1,0:T(8,128)(2,1)S(1)}, u32[]{:S(2)}, u32[]{:S(2)}) collective-permute-start(bf16[272,512]{1,0:T(8,128)(2,1)S(1)} %get-tuple-element.65), channel_id=1, source_target_pairs={{0,16},{4,20},{8,24},{12,28},{16,0},{20,4},{24,8},{28,12},{32,48},... | collective-permute-start | bytes 835592 | tf_op jit(solution)/shard_map/ppermute | solution.py:546
  29.9 15.1 %collective-permute-start.5 = (bf16[272,512]{1,0:T(8,128)(2,1)S(1)}, bf16[272,512]{1,0:T(8,128)(2,1)S(1)}, u32[]{:S(2)}, u32[]{:S(2)}) collective-permute-start(bf16[272,512]{1,0:T(8,128)(2,1)S(1)} %get-tuple-element.66), channel_id=1, source_target_pairs={{0,24},{4,28},{8,0},{12,4},{16,8},{20,12},{24,16},{28,20},{32,56},... | collective-permute-start | bytes 835592 | tf_op jit(solution)/shard_map/ppermute | solution.py:546
  41.6 16.2 %collective-permute-start.8 = (bf16[256,512]{1,0:T(8,128)(2,1)S(1)}, bf16[256,512]{1,0:T(8,128)(2,1)S(1)}, u32[]{:S(2)}, u32[]{:S(2)}) collective-permute-start(bf16[256,512]{1,0:T(8,128)(2,1)S(1)} %get-tuple-element.73), channel_id=1, source_target_pairs={{0,8},{4,12},{8,16},{12,20},{16,24},{20,28},{24,0},{28,4},{32,40},... | collective-permute-start | bytes 786440 | tf_op jit(solution)/shard_map/ppermute | solution.py:546
  41.7 16.2 %collective-permute-start.9 = (bf16[256,512]{1,0:T(8,128)(2,1)S(1)}, bf16[256,512]{1,0:T(8,128)(2,1)S(1)}, u32[]{:S(2)}, u32[]{:S(2)}) collective-permute-start(bf16[256,512]{1,0:T(8,128)(2,1)S(1)} %get-tuple-element.74), channel_id=1, source_target_pairs={{0,16},{4,20},{8,24},{12,28},{16,0},{20,4},{24,8},{28,12},{32,48},... | collective-permute-start | bytes 786440 | tf_op jit(solution)/shard_map/ppermute | solution.py:546
  43.8 14.1 %collective-permute-start.10 = (bf16[256,512]{1,0:T(8,128)(2,1)S(1)}, bf16[256,512]{1,0:T(8,128)(2,1)S(1)}, u32[]{:S(2)}, u32[]{:S(2)}) collective-permute-start(bf16[256,512]{1,0:T(8,128)(2,1)S(1)} %get-tuple-element.75), channel_id=1, source_target_pairs={{0,24},{4,28},{8,0},{12,4},{16,8},{20,12},{24,16},{28,20},{32,56},... | collective-permute-start | bytes 786440 | tf_op jit(solution)/shard_map/ppermute | solution.py:546
  45.3 18.4 %collective-permute-start.15 = (bf16[256,512]{1,0:T(8,128)(2,1)S(1)}, bf16[256,512]{1,0:T(8,128)(2,1)S(1)}, u32[]{:S(2)}, u32[]{:S(2)}) collective-permute-start(bf16[256,512]{1,0:T(8,128)(2,1)S(1)} %edge_forward.1), channel_id=1, source_target_pairs={{0,32},{4,36},{8,40},{12,44},{16,48},{20,52},{24,56},{28,60},{1,33... | collective-permute-start | bytes 786440 | tf_op jit(solution)/shard_map/ppermute | solution.py:546
  58.2 10.5 %collective-permute-start.11 = (bf16[256,512]{1,0:T(8,128)(2,1)S(1)}, bf16[256,512]{1,0:T(8,128)(2,1)S(1)}, u32[]{:S(2)}, u32[]{:S(2)}) collective-permute-start(bf16[256,512]{1,0:T(8,128)(2,1)S(1)} %edge_back.1), channel_id=1, source_target_pairs={{32,0},{36,4},{40,8},{44,12},{48,16},{52,20},{56,24},{60,28},{33,1... | collective-permute-start | bytes 786440 | tf_op jit(solution)/shard_map/ppermute | solution.py:546
  64.7 7.8 %collective-permute-start.16 = (bf16[256,512]{1,0:T(8,128)(2,1)S(1)}, bf16[256,512]{1,0:T(8,128)(2,1)S(1)}, u32[]{:S(2)}, u32[]{:S(2)}) collective-permute-start(bf16[256,512]{1,0:T(8,128)(2,1)S(1)} %get-tuple-element.88), channel_id=1, source_target_pairs={{0,24},{4,28},{8,0},{12,4},{16,8},{20,12},{24,16},{28,20},{32,56},... | collective-permute-start | bytes 786440 | tf_op jit(solution)/shard_map/ppermute | solution.py:546
  66.7 8.2 %collective-permute-start.17 = (bf16[256,512]{1,0:T(8,128)(2,1)S(1)}, bf16[256,512]{1,0:T(8,128)(2,1)S(1)}, u32[]{:S(2)}, u32[]{:S(2)}) collective-permute-start(bf16[256,512]{1,0:T(8,128)(2,1)S(1)} %get-tuple-element.89), channel_id=1, source_target_pairs={{0,16},{4,20},{8,24},{12,28},{16,0},{20,4},{24,8},{28,12},{32,48},... | collective-permute-start | bytes 786440 | tf_op jit(solution)/shard_map/ppermute | solution.py:546
  66.8 15.9 %collective-permute-start.18 = (bf16[256,512]{1,0:T(8,128)(2,1)S(1)}, bf16[256,512]{1,0:T(8,128)(2,1)S(1)}, u32[]{:S(2)}, u32[]{:S(2)}) collective-permute-start(bf16[256,512]{1,0:T(8,128)(2,1)S(1)} %get-tuple-element.90), channel_id=1, source_target_pairs={{0,8},{4,12},{8,16},{12,20},{16,24},{20,28},{24,0},{28,4},{32,40},... | collective-permute-start | bytes 786440 | tf_op jit(solution)/shard_map/ppermute | solution.py:546
  69.7 23.1 %copy-start.6 = (f32[4,4096]{1,0:T(4,128)S(1)}, f32[4,4096]{1,0:T(4,128)}, u32[]{:S(2)}) copy-start(f32[4,4096]{1,0:T(4,128)} %v_tap.5) | copy-start | bytes 196612
  69.7 15.2 %collective-permute-start.12 = (bf16[256,512]{1,0:T(8,128)(2,1)S(1)}, bf16[256,512]{1,0:T(8,128)(2,1)S(1)}, u32[]{:S(2)}, u32[]{:S(2)}) collective-permute-start(bf16[256,512]{1,0:T(8,128)(2,1)S(1)} %get-tuple-element.77), channel_id=1, source_target_pairs={{0,24},{4,28},{8,0},{12,4},{16,8},{20,12},{24,16},{28,20},{32,56},... | collective-permute-start | bytes 786440 | tf_op jit(solution)/shard_map/ppermute | solution.py:546
  71.8 14.3 %collective-permute-start.13 = (bf16[256,512]{1,0:T(8,128)(2,1)S(1)}, bf16[256,512]{1,0:T(8,128)(2,1)S(1)}, u32[]{:S(2)}, u32[]{:S(2)}) collective-permute-start(bf16[256,512]{1,0:T(8,128)(2,1)S(1)} %get-tuple-element.78), channel_id=1, source_target_pairs={{0,16},{4,20},{8,24},{12,28},{16,0},{20,4},{24,8},{28,12},{32,48},... | collective-permute-start | bytes 786440 | tf_op jit(solution)/shard_map/ppermute | solution.py:546
  72.5 20.2 %collective-permute-start.14 = (bf16[256,512]{1,0:T(8,128)(2,1)S(1)}, bf16[256,512]{1,0:T(8,128)(2,1)S(1)}, u32[]{:S(2)}, u32[]{:S(2)}) collective-permute-start(bf16[256,512]{1,0:T(8,128)(2,1)S(1)} %get-tuple-element.79), channel_id=1, source_target_pairs={{0,8},{4,12},{8,16},{12,20},{16,24},{20,28},{24,0},{28,4},{32,40},... | collective-permute-start | bytes 786440 | tf_op jit(solution)/shard_map/ppermute | solution.py:546
  97.1 8.6 %collective-permute-start.19 = (bf16[128,2688]{1,0:T(8,128)(2,1)S(1)}, bf16[128,2688]{1,0:T(8,128)(2,1)S(1)}, u32[]{:S(2)}, u32[]{:S(2)}) collective-permute-start(bf16[128,2688]{1,0:T(8,128)(2,1)S(1)} %get-tuple-element.106), channel_id=1, source_target_pairs={{0,4},{4,0},{8,12},{12,8},{16,20},{20,16},{24,28},{28,24},{32,36},... | collective-permute-start | bytes 2064392 | tf_op jit(solution)/shard_map/ppermute | solution.py:546
  98.0 5.2 %collective-permute-start.21 = (f32[8,2560]{1,0:T(8,128)S(1)}, f32[8,2560]{1,0:T(8,128)S(1)}, u32[]{:S(2)}, u32[]{:S(2)}) collective-permute-start(f32[8,2560]{1,0:T(8,128)S(1)} %get-tuple-element.107), channel_id=1, source_target_pairs={{12,4},{20,12},{28,20},{36,28},{44,36},{52,44},{60,52},{13,5},{21,... | collective-permute-start | bytes 245768 | tf_op jit(solution)/shard_map/ppermute | solution.py:546
  99.9 5.8 %collective-permute-start.20 = (f32[8,2560]{1,0:T(8,128)S(1)}, f32[8,2560]{1,0:T(8,128)S(1)}, u32[]{:S(2)}, u32[]{:S(2)}) collective-permute-start(f32[8,2560]{1,0:T(8,128)S(1)} %get-tuple-element.107), channel_id=1, source_target_pairs={{8,4},{16,12},{24,20},{32,28},{40,36},{48,44},{56,52},{9,5},{17,13... | collective-permute-start | bytes 245768 | tf_op jit(solution)/shard_map/ppermute | solution.py:546
  (13 other events, 93.8 us)

commit v3 on v2

--- a/solution.py
+++ b/solution.py
@@ -299,30 +299,43 @@
         out[...] = nn(read_t, dye_out[:, head_columns(ring, slot)]).astype(bf16)
 
 
-def inner_kernel(
-    x, dy, bc, delta, within, sx, skip_gain, ones,
-    base_out, dbc_out, diff_out, vsum_out,
-    wide, skips, within_3, row_sum, bcs, dbcs,
-):
+def inner_kernel(part, x, dy, bc, delta, within, sx, skip_gain, ones, *refs):
+    if part == 0:
+        base_out, dbcs, diff_out, vsum_out = refs[:4]
+        scratch = refs[4:]
+    else:
+        dbcs_in, diff_in, vsum_in, base_in = refs[:4]
+        base_out, dbc_out, diff_out, vsum_out, top_out = refs[4:9]
+        scratch = refs[9:]
+        dbcs = scratch[-1]
+    wide, skips, within_3, row_sum, bcs = scratch[:5]
     core, ring = place()
     half = ROWS // 2
-    wide[...] = nn(split3(delta[...]), ones[...])
+    low_col, low_head = part * (WIDE // 2), part * (HEADS // 2)
+    own = ones[:, low_col : low_col + WIDE // 2]
+    wide[...] = nn(split3(delta[...]), own)
     skip = jnp.broadcast_to(tiled_heads(skip_gain[...], core), (8, 128))
-    skips[...] = nn(split3(skip), ones[...])
+    skips[...] = nn(split3(skip), own)
     scaled = within[...] * LOG2E
     lane_part = iota((ROWS, 128), 1) // HEADS
     left = jnp.where(lane_part == 3, 1.0, -split3(scaled).astype(f32)).astype(bf16)
     parts_t = split3(scaled).astype(f32).T
-    for h in range(HEADS):
-        within_3[h, 0:1, :] = parts_t[h : h + 1, :]
-        within_3[h, 1:2, :] = parts_t[HEADS + h : HEADS + h + 1, :]
-        within_3[h, 2:3, :] = parts_t[2 * HEADS + h : 2 * HEADS + h + 1, :]
+    for h in range(HEADS // 2):
+        for piece in range(3):
+            at = piece * HEADS + low_head + h
+            within_3[h, piece : piece + 1, :] = parts_t[at : at + 1, :]
         within_3[h, 3:8, :] = jnp.zeros((5, ROWS), f32)
     write, read = bc[:, :STATE], bc[:, STATE:]
     bcs[...] = nt(write, read)
-    dbcs[...] = jnp.zeros_like(dbcs)
-    diff_out[...] = jnp.zeros_like(diff_out)
-    vsum_out[...] = jnp.zeros_like(vsum_out)
+    if part == 0:
+        dbcs[...] = jnp.zeros_like(dbcs)
+        diff_out[...] = jnp.zeros_like(diff_out)
+        vsum_out[...] = jnp.zeros_like(vsum_out)
+    else:
+        dbcs[...] = dbcs_in[...]
+        diff_out[...] = diff_in[...]
+        vsum_out[...] = vsum_in[...]
+    row_sum[...] = jnp.zeros_like(row_sum)
     keep = iota((half, half), 1) >= iota((half, half), 0)
     lanes = iota((ROWS, 128), 1)
     first = lanes < HEAD_DIM
@@ -330,9 +343,9 @@
     pad = jnp.zeros((24, ROWS), f32)
 
     def pair(b, carry):
-        cols = block128(b)
+        cols, here = block128(b, low_col), block128(b)
         xb = x[:, cols].astype(f32)
-        xd = (xb * wide[:, cols]).astype(bf16)
+        xd = (xb * wide[:, here]).astype(bf16)
         grad = dy[:, cols]
         zero = jnp.zeros_like(grad)
         top = jnp.zeros((half, 128), f32)
@@ -340,10 +353,10 @@
         col_total = jnp.zeros((ROWS, 128), f32)
         grads_of = [0.0, 0.0, 0.0]
         for e in range(2):
-            h = 2 * b + e
+            h = low_head + 2 * b + e
             g = jnp.where(first, grad, zero) if e == 0 else jnp.where(first, zero, grad)
             right = jnp.concatenate(
-                [jnp.where(row_head == h, 1.0, 0.0), within_3[h], pad], axis=0
+                [jnp.where(row_head == h, 1.0, 0.0), within_3[2 * b + e], pad], axis=0
             ).astype(bf16)
             gap0 = nn(left[:half], right)
             gap1 = nn(left[half:], right[:, half:])
@@ -385,18 +398,21 @@
         u = jnp.concatenate([top, bot], axis=0)
         diff_out[...] = diff_out[...] - col_total
         vsum_out[...] = vsum_out[...] + head_sum(xb * u, ones[:, cols])
-        base_out[:, cols] = (
-            wide[:, cols] * u + skips[0:1, cols] * grad.astype(f32)
+        base_out[:, here] = (
+            wide[:, here] * u + skips[0:1, here] * grad.astype(f32)
         ) * sx[:, cols].astype(f32)
         return carry
 
-    lax.fori_loop(0, 16, pair, 0)
+    lax.fori_loop(0, 8, pair, 0)
     for t in range(1, 4):
         row_sum[t * HEADS : (t + 1) * HEADS, :] = row_sum[0:HEADS, :]
     diff_out[...] = diff_out[...] + row_sum[...].T
-    grad = dbcs[...]
-    dbc_out[:, :STATE] = nn(grad.astype(bf16), read)
-    dbc_out[:, STATE:] = nn(grad.T.astype(bf16), write)
+    if part == 1:
+        grad = dbcs[...]
+        dbc_out[:, :STATE] = nn(grad.astype(bf16), read)
+        dbc_out[:, STATE:] = nn(grad.T.astype(bf16), write)
+        top_out[:, : WIDE // 2] = base_in[0:8, :]
+        top_out[:, WIDE // 2 :] = base_out[0:8, :]
 
 
 def carry_kernel(c0, c1, c2, c3, bc, dye, dbc, diff, ones, diff_out, dread_out, carried_out):
@@ -414,9 +430,9 @@
 
 
 def last_kernel(
-    g0, g1, g2, g3, carried, bc, xs, k, base, sbc, delta, within, sig, diff, vsum,
+    g0, g1, g2, g3, carried, bc, xs, k, base_0, base_1, sbc, delta, within, sig, diff, vsum,
     dread, dbc, decay_log, v_tap, s_tap, ones,
-    vg_own, sg_own, st_own, message, head_out,
+    vg_own, sg_own, st_own, message,
     gbuf, ebuf, sbuf, dbuf, back, sback,
 ):
     core, ring = place()
@@ -433,7 +449,8 @@
         grad = gbuf[:, cols]
         through = nn(write, grad)
         rsum = rsum + head_sum(xs[:, cols].astype(f32) * through, ones[:, cols])
-        ebuf[0:ROWS, cols] = base[:, cols] + k[:, cols].astype(f32) * through
+        base = (base_0, base_1)[b // 2][:, (b % 2) * PART : (b % 2 + 1) * PART]
+        ebuf[0:ROWS, cols] = base + k[:, cols].astype(f32) * through
         both = jnp.sum(
             grad.astype(f32) * carried[:, cols].astype(f32), axis=0, keepdims=True
         )
@@ -452,8 +469,6 @@
     dwrite = dbc[:, :STATE] + nt(xs[...], gbuf[...])
     sbuf[0:ROWS, :STATE] = dwrite * sbc[:, :STATE].astype(f32)
     sbuf[0:ROWS, STATE:] = dread[...] * sbc[:, STATE:].astype(f32)
-    head_out[:, :WIDE] = ebuf[0:8, :]
-    head_out[:, WIDE:] = sbuf[0:8, :]
 
     def conv(source, tap, b, width):
         cols, par = block128(b), block128(b, core * width)
@@ -478,6 +493,21 @@
     message[:, :WIDE] = back[other, :]
     sg_own[...] = sback[mine, :]
     message[:, WIDE : WIDE + 2 * STATE] = sback[other, :]
+
+
+def head_kernel(g0, g1, g2, g3, bc, xs, k, base_top, sbc, dread, dbc, out):
+    core, ring = place()
+    write = bc[0:TAIL, :STATE]
+    dwrite = dbc[0:8, :STATE]
+    for slot, src in enumerate((g0, g1, g2, g3)):
+        cols = head_columns(ring, slot)
+        grad = src[...]
+        through = nn(write, grad)[0:8]
+        out[:, cols] = base_top[:, cols] + k[0:TAIL, cols].astype(f32)[0:8] * through
+        dwrite = dwrite + nt(xs[0:TAIL, cols], grad)[0:8]
+    slope = sbc[0:TAIL, :].astype(f32)[0:8]
+    out[:, WIDE : WIDE + STATE] = dwrite * slope[:, :STATE]
+    out[:, WIDE + STATE :] = dread[0:8, :] * slope[:, STATE:]
 
 
 def join_kernel(v_own, s_own, t_own, message, e0, e1, v_tap, s_tap, v_out, s_out, t_out):
@@ -518,6 +548,7 @@
 
 def call(kernel, args, outs, scratch=(), name=None, anywhere=(), cost=None):
     vmem = pl.BlockSpec(memory_space=pltpu.VMEM)
+    args = [pltpu.with_memory_space_constraint(a, pltpu.HBM) if k in anywhere else a for k, a in enumerate(args)]
     return pl.pallas_call(
         kernel,
         in_specs=[
@@ -575,9 +606,11 @@
     message = send(message, swap_pairs)
     halo_a = send(halo_a, [(k * 2 + 1, k * 2 + 3) for k in range(chips - 1)])
     halo_b = send(halo_b, [(k * 2 + 1, k * 2 + 2) for k in range(chips - 1)])
-    g, message, halo_a, halo_b = lax.optimization_barrier((g, message, halo_a, halo_b))
     g_own, g_in = call(
         pack_grad_kernel, [g], [((TOK, WIDE), bf16)] * 2, [sems((2,))], "pack_grad", (0,)
+    )
+    g_own, g_in, message, halo_a, halo_b = lax.optimization_barrier(
+        (g_own, g_in, message, halo_a, halo_b)
     )
     g_own = lax.ppermute(g_own, "pipe", [(0, 1), (1, 0)])
     g_in = lax.ppermute(
@@ -605,50 +638,63 @@
         cost=2,
     )[0]
     edge_in = send(edge, [(i, i + per_half) for i in range(per_half)])
+    half_wide = (ROWS, WIDE // 2)
+    inner_scratch = [
+        (half_wide, f32), ((8, WIDE // 2), f32), ((HEADS // 2, 8, ROWS), f32), ((128, ROWS), f32),
+        ((ROWS, ROWS), f32),
+    ]
     dy_now, _ = lax.optimization_barrier((dy, edge))
-    base, dbc, diff, vsum = call(
-        inner_kernel, [x, dy_now, bc, delta, within, sx, skip, ones],
-        [(tall, f32), ((ROWS, 2 * STATE), f32), (narrow, f32), (narrow, f32)],
-        [(tall, f32), ((8, WIDE), f32), ((HEADS, 8, ROWS), f32), ((128, ROWS), f32),
-         ((ROWS, ROWS), f32), ((ROWS, ROWS), f32)],
-        "inner", cost=12,
+    base_0, dbcs, diff, vsum = call(
+        functools.partial(inner_kernel, 0), [x, dy_now, bc, delta, within, sx, skip, ones],
+        [(half_wide, f32), ((ROWS, ROWS), f32), (narrow, f32), (narrow, f32)],
+        inner_scratch, "inner_0", cost=6,
     )
     edge_in, diff = lax.optimization_barrier((edge_in, diff))
-    carried = exchange(
-        call(
-            functools.partial(scan_kernel, False), marks + marks + [edge_in],
-            [state_part] * 4, (), "scan_forward", cost=3,
-        ),
-        -1,
-    )
+    steps = call(
+        functools.partial(scan_kernel, False), marks + marks + [edge_in],
+        [state_part] * 4, (), "scan_forward", cost=3,
+    )
+    carried = exchange(steps, -1)
     edge_back = call(
         functools.partial(edge_kernel, True), marks + grads, [state_part], (), "edge_back", cost=2,
     )[0]
     edge_back = send(edge_back, [(i + per_half, i) for i in range(per_half)])
-    back = exchange(
-        call(
-            functools.partial(scan_kernel, True), marks + grads + [edge_back],
-            [state_part] * 4, (), "scan_back", cost=3,
-        ),
-        -1,
-    )
+    steps_back = call(
+        functools.partial(scan_kernel, True), marks + grads + [edge_back],
+        [state_part] * 4, (), "scan_back", cost=3,
+    )
+    dy_now, _ = lax.optimization_barrier((dy, steps_back[0]))
+    base_1, dbc, diff, vsum, base_top = call(
+        functools.partial(inner_kernel, 1),
+        [x, dy_now, bc, delta, within, sx, skip, ones, dbcs, diff, vsum, base_0],
+        [(half_wide, f32), ((ROWS, 2 * STATE), f32), (narrow, f32), (narrow, f32),
+         ((8, WIDE), f32)],
+        inner_scratch + [((ROWS, ROWS), f32)], "inner_1", cost=6,
+    )
+    back = exchange(steps_back, -1)
     diff, dread, held = call(
         carry_kernel, list(carried) + [bc, dye, dbc, diff, ones],
         [(narrow, f32), ((ROWS, STATE), f32), ((STATE, WIDE), bf16)], (), "carry", cost=4,
     )
-    vg_own, sg_own, st_own, message, head = call(
+    head = call(
+        head_kernel, list(back) + [bc, xs, k, base_top, sbc, dread, dbc],
+        [((8, WIDE + 2 * STATE), f32)], (), "head", cost=1,
+    )[0]
+    back[0], head = lax.optimization_barrier((back[0], head))
+    e0 = send(head, [(j * 2, j * 2 - 1) for j in range(1, chips)])
+    e1 = send(head, [(j * 2 + 1, j * 2 - 1) for j in range(1, chips)])
+    vg_own, sg_own, st_own, message = call(
         last_kernel,
         list(back)
-        + [held, bc, xs, k, base, sbc, delta, within, sig, diff, vsum, dread, dbc,
+        + [held, bc, xs, k, base_0, base_1, sbc, delta, within, sig, diff, vsum, dread, dbc,
            rate_log, value_kernel, state_kernel, ones],
         [((TOK, WIDE), bf16), ((TOK, 2 * STATE), bf16), ((TOK, 128), bf16),
-         ((TOK, joint), bf16), ((8, WIDE + 2 * STATE), f32)],
+         ((TOK, joint), bf16)],
         [((STATE, WIDE), bf16), ((ROWS + 8, WIDE), f32), ((ROWS + 8, 2 * STATE), f32),
          (narrow, f32), (tall, bf16), ((ROWS, 2 * STATE), bf16)],
         "last", cost=8,
     )
-    e0 = send(head, [(j * 2, j * 2 - 1) for j in range(1, chips)])
-    e1 = send(head, [(j * 2 + 1, j * 2 - 1) for j in range(1, chips)])
+    message, e0, e1 = lax.optimization_barrier((message, e0, e1))
     message = send(message, swap_pairs)
     value_out, state_out, step_out = call(
         join_kernel,

time: 108 us -> 98.3 us (0.910)
  local copies, waits for them, and re-layouts: 6.43 us -> 2.04 us
  waiting for transfers between devices: 37.1 us -> 32.8 us
  starting transfers between devices: 31.5 us -> 28.3 us
  Pallas kernels: 31.1 us -> 33.9 us
    ppermute x20, waiting for transfers between devices: 28.3 us -> 22.4 us  [send(): return lax.ppermute(x, 'ctx', pairs)]
    unnamed x30 -> x22, local copies, waits for them, and re-layouts: 6.43 us -> 2.04 us
    ppermute x20, starting transfers between devices: 27.8 us -> 24.6 us  [send(): return lax.ppermute(x, 'ctx', pairs)]
    pallas_call x13 -> x15, Pallas kernels: 31.1 us -> 33.9 us  [call(): pl.pallas_call(kernel, in_specs=[pl.BlockSpec(memory_space=pltpu.HBM) if...]
    ppermute x1, waiting for transfers between devices: 8.77 us -> 10.4 us  [local(): lax.ppermute(g_in, ('pipe', 'ctx'), [(p * count + i, (1 - p) * count + (i...]
  transfers between devices with their start and end apart: 22 -> 22, of which waited for: 11 -> 11; matrix products, arithmetic and copies ran while one was open for 0% -> 0% of each run, Pallas kernels for 23% -> 32%
where the time goes in v3:
time: 98.3 us; the launch traced here: 97.9 us
  Pallas kernels  33.9 us (34%)
  waiting for transfers between devices  32.8 us (33%)
  starting transfers between devices  28.3 us (29%)
  local copies, waits for them, and re-layouts  2.04 us (2%)
    pallas_call x15, Pallas kernels, call(): pl.pallas_call(kernel, in_specs=[pl.BlockSpec(memory_space=pltpu.HBM) if...  33.9 us
    ppermute x20, starting transfers between devices, send(): return lax.ppermute(x, 'ctx', pairs)  24.6 us
    ppermute x20, waiting for transfers between devices, send(): return lax.ppermute(x, 'ctx', pairs)  22.4 us
    ppermute x1, waiting for transfers between devices, local(): lax.ppermute(g_in, ('pipe', 'ctx'), [(p * count + i, (1 - p) * count + (i...  10.4 us
    ppermute x1, starting transfers between devices, local(): lax.ppermute(g_in, ('pipe', 'ctx'), [(p * count + i, (1 - p) * count + (i...  3.05 us
    unnamed x22, local copies, waits for them, and re-layouts  2.04 us
  transfers between devices with their start and end apart: 22, of which 11 were waited for; matrix products, arithmetic and copies ran while one was open for 0% of the time, Pallas kernels for 32%

profile of v3, /device:TPU:15, one launch (start us, length us, event | category | flops | bytes accessed | tf_op | source)
XLA Modules:
  0.0 97.9 jit_solution(12454762916893587413)
XLA Ops:
  3.3 3.5 %collective-permute-start.1 = (bf16[16,2560]{1,0:T(8,128)(2,1)S(1)}, bf16[16,2560]{1,0:T(8,128)(2,1)S(1)}, u32[]{:S(2)}, u32[]{:S(2)}) collective-permute-start(bf16[16,2560]{1,0:T(8,128)(2,1)S(1)} %get-tuple-element.71), channel_id=1, source_target_pairs={{4,12},{12,20},{20,28},{28,36},{36,44},{44,52},{52,60},{5,13},{13,... | collective-permute-start | bytes 245768 | tf_op jit(solution)/shard_map/ppermute | solution.py:577
  6.8 1.3 %collective-permute-start.2 = (bf16[16,2560]{1,0:T(8,128)(2,1)S(1)}, bf16[16,2560]{1,0:T(8,128)(2,1)S(1)}, u32[]{:S(2)}, u32[]{:S(2)}) collective-permute-start(bf16[16,2560]{1,0:T(8,128)(2,1)S(1)} %get-tuple-element.72), channel_id=1, source_target_pairs={{4,8},{12,16},{20,24},{28,32},{36,40},{44,48},{52,56},{5,9},{13,17... | collective-permute-start | bytes 245768 | tf_op jit(solution)/shard_map/ppermute | solution.py:577
  9.3 2.7 %collective-permute-done.1.halo_a = bf16[16,2560]{1,0:T(8,128)(2,1)S(1)} collective-permute-done((bf16[16,2560]{1,0:T(8,128)(2,1)S(1)}, bf16[16,2560]{1,0:T(8,128)(2,1)S(1)}, u32[]{:S(2)}, u32[]{:S(2)}) %collective-permute-start.1) | collective-permute-done | bytes 81952 | tf_op jit(solution)/shard_map/ppermute | solution.py:577
  12.7 3.1 %collective-permute-start.7 = (bf16[128,2048]{1,0:T(8,128)(2,1)S(1)}, bf16[128,2048]{1,0:T(8,128)(2,1)S(1)}, u32[]{:S(2)}, u32[]{:S(2)}) collective-permute-start(bf16[128,2048]{1,0:T(8,128)(2,1)S(1)} %get-tuple-element.81), channel_id=1, source_target_pairs={{0,68},{4,64},{8,76},{12,72},{16,84},{20,80},{24,92},{28,88},{32,1... | collective-permute-start | bytes 1572872 | tf_op jit(solution)/shard_map/ppermute | solution.py:616
  16.5 7.7 %first.1 = (bf16[272,512]{1,0:T(8,128)(2,1)S(1)}, bf16[272,512]{1,0:T(8,128)(2,1)S(1)}, bf16[272,512]{1,0:T(8,128)(2,1)S(1)}, bf16[272,512]{1,0:T(8,128)(2,1)S(1...) custom-call(bf16[128,4096]{1,0:T(8,128)(2,1)S(1)} %bitcast.17, ...), custom_call_target="tpu_custom_call" | custom-call | bytes 24000000 | tf_op jit(solution)/shard_map/first/pallas_call | solution.py:552
  24.3 1.3 %collective-permute-start.4 = (bf16[272,512]{1,0:T(8,128)(2,1)S(1)}, bf16[272,512]{1,0:T(8,128)(2,1)S(1)}, u32[]{:S(2)}, u32[]{:S(2)}) collective-permute-start(bf16[272,512]{1,0:T(8,128)(2,1)S(1)} %get-tuple-element.78), channel_id=1, source_target_pairs={{0,16},{4,20},{8,24},{12,28},{16,0},{20,4},{24,8},{28,12},{32,48},... | collective-permute-start | bytes 835592 | tf_op jit(solution)/shard_map/ppermute | solution.py:577
  25.6 1.4 %collective-permute-start.5 = (bf16[272,512]{1,0:T(8,128)(2,1)S(1)}, bf16[272,512]{1,0:T(8,128)(2,1)S(1)}, u32[]{:S(2)}, u32[]{:S(2)}) collective-permute-start(bf16[272,512]{1,0:T(8,128)(2,1)S(1)} %get-tuple-element.79), channel_id=1, source_target_pairs={{0,24},{4,28},{8,0},{12,4},{16,8},{20,12},{24,16},{28,20},{32,56},... | collective-permute-start | bytes 835592 | tf_op jit(solution)/shard_map/ppermute | solution.py:577
  26.9 10.4 %collective-permute-done.7.g_in = bf16[128,2048]{1,0:T(8,128)(2,1)S(1)} collective-permute-done((bf16[128,2048]{1,0:T(8,128)(2,1)S(1)}, bf16[128,2048]{1,0:T(8,128)(2,1)S(1)}, u32[]{:S(2)}, u32[]{:S(2)}) %collective-permute-start.7) | collective-permute-done | bytes 524320 | tf_op jit(solution)/shard_map/ppermute | solution.py:616
  37.3 1.6 %second.1 = (bf16[256,512]{1,0:T(8,128)(2,1)S(1)}, bf16[256,512]{1,0:T(8,128)(2,1)S(1)}, bf16[256,512]{1,0:T(8,128)(2,1)S(1)}, bf16[256,512]{1,0:T(8,128)(2,1)S(...) custom-call(bf16[128,2048]{1,0:T(8,128)(2,1)S(1)} %collective-permute-done.6.g_own, ...), custom_call_target="tpu_custom_call" | custom-call | bytes 12000000 | tf_op jit(solution)/shard_map/second/pallas_call | solution.py:552
  39.0 1.3 %collective-permute-start.9 = (bf16[256,512]{1,0:T(8,128)(2,1)S(1)}, bf16[256,512]{1,0:T(8,128)(2,1)S(1)}, u32[]{:S(2)}, u32[]{:S(2)}) collective-permute-start(bf16[256,512]{1,0:T(8,128)(2,1)S(1)} %get-tuple-element.86), channel_id=1, source_target_pairs={{0,16},{4,20},{8,24},{12,28},{16,0},{20,4},{24,8},{28,12},{32,48},... | collective-permute-start | bytes 786440 | tf_op jit(solution)/shard_map/ppermute | solution.py:577
  40.3 1.5 %collective-permute-start.10 = (bf16[256,512]{1,0:T(8,128)(2,1)S(1)}, bf16[256,512]{1,0:T(8,128)(2,1)S(1)}, u32[]{:S(2)}, u32[]{:S(2)}) collective-permute-start(bf16[256,512]{1,0:T(8,128)(2,1)S(1)} %get-tuple-element.87), channel_id=1, source_target_pairs={{0,24},{4,28},{8,0},{12,4},{16,8},{20,12},{24,16},{28,20},{32,56},... | collective-permute-start | bytes 786440 | tf_op jit(solution)/shard_map/ppermute | solution.py:577
  44.0 5.7 %inner_0.1 = (f32[256,1024]{1,0:T(8,128)S(1)}, f32[256,256]{1,0:T(8,128)S(1)}, f32[256,128]{1,0:T(8,128)S(1)}, f32[256,128]{1,0:T(8,128)S(1)}) custom-call(bf16[256,2048]{1,0:T(8,128)(2,1)S(1)} %get-tuple-element.94.x, bf16[256,2048]{1,0:T(8,128)(2,1)S(1)} %get-tuple-element.99.dy, bf16[256,512]{1,0:T(8,128)(2,1)S(1)} %get-tuple-element.82.bc, ...), custom_call_target="tpu_custom_call" | custom-call | bytes 18000000 | tf_op jit(solution)/shard_map/inner_0/pallas_call | solution.py:552
  49.7 3.6 %collective-permute-done.8.d1 = bf16[256,512]{1,0:T(8,128)(2,1)S(1)} collective-permute-done((bf16[256,512]{1,0:T(8,128)(2,1)S(1)}, bf16[256,512]{1,0:T(8,128)(2,1)S(1)}, u32[]{:S(2)}, u32[]{:S(2)}) %collective-permute-start.8) | collective-permute-done | bytes 262176 | tf_op jit(solution)/shard_map/ppermute | solution.py:577
  54.2 1.3 %collective-permute-start.11 = (bf16[256,512]{1,0:T(8,128)(2,1)S(1)}, bf16[256,512]{1,0:T(8,128)(2,1)S(1)}, u32[]{:S(2)}, u32[]{:S(2)}) collective-permute-start(bf16[256,512]{1,0:T(8,128)(2,1)S(1)} %edge_back.1), channel_id=1, source_target_pairs={{32,0},{36,4},{40,8},{44,12},{48,16},{52,20},{56,24},{60,28},{33,1... | collective-permute-start | bytes 786440 | tf_op jit(solution)/shard_map/ppermute | solution.py:577
  56.5 2.7 %collective-permute-start.16 = (bf16[256,512]{1,0:T(8,128)(2,1)S(1)}, bf16[256,512]{1,0:T(8,128)(2,1)S(1)}, u32[]{:S(2)}, u32[]{:S(2)}) collective-permute-start(bf16[256,512]{1,0:T(8,128)(2,1)S(1)} %get-tuple-element.109), channel_id=1, source_target_pairs={{0,24},{4,28},{8,0},{12,4},{16,8},{20,12},{24,16},{28,20},{32,56},... | collective-permute-start | bytes 786440 | tf_op jit(solution)/shard_map/ppermute | solution.py:577
  61.8 2.9 %collective-permute-start.12 = (bf16[256,512]{1,0:T(8,128)(2,1)S(1)}, bf16[256,512]{1,0:T(8,128)(2,1)S(1)}, u32[]{:S(2)}, u32[]{:S(2)}) collective-permute-start(bf16[256,512]{1,0:T(8,128)(2,1)S(1)} %get-tuple-element.89), channel_id=1, source_target_pairs={{0,24},{4,28},{8,0},{12,4},{16,8},{20,12},{24,16},{28,20},{32,56},... | collective-permute-start | bytes 786440 | tf_op jit(solution)/shard_map/ppermute | solution.py:577
  65.0 4.0 %collective-permute-done.16.c1 = bf16[256,512]{1,0:T(8,128)(2,1)S(1)} collective-permute-done((bf16[256,512]{1,0:T(8,128)(2,1)S(1)}, bf16[256,512]{1,0:T(8,128)(2,1)S(1)}, u32[]{:S(2)}, u32[]{:S(2)}) %collective-permute-start.16) | collective-permute-done | bytes 262176 | tf_op jit(solution)/shard_map/ppermute | solution.py:577
  69.0 5.9 %inner_1.1 = (f32[256,1024]{1,0:T(8,128)S(1)}, f32[256,512]{1,0:T(8,128)S(1)}, f32[256,128]{1,0:T(8,128)S(1)}, f32[256,128]{1,0:T(8,128)S(1)}, f32[8,2048]{1,0:T(8,128)S(1)}) custom-call(bf16[256,2048]{1,0:T(8,128)(2,1)S(1)} %get-tuple-element.94.x, bf16[256,2048]{1,0:T(8,128)(2,1)S(1)} %get-tuple-element.99.dy, bf16[256,512]{1,0:T(8,128)(2,1)S(1)} %get-tuple-element.82.bc, ...), custom_call_target="tpu_custom_call" | custom-call | bytes 18000000 | tf_op jit(solution)/shard_map/inner_1/pallas_call | solution.py:552
  75.5 2.1 %carry.1 = (f32[256,128]{1,0:T(8,128)S(1)}, f32[256,256]{1,0:T(8,128)S(1)}, bf16[256,2048]{1,0:T(8,128)(2,1)S(1)}) custom-call(bf16[256,512]{1,0:T(8,128)(2,1)S(1)} %get-tuple-element.108.c0, bf16[256,512]{1,0:T(8,128)(2,1)S(1)} %collective-permute-done.16.c1, bf16[256,512]{1,0:T(8,128)(2,1)S(1)} %collective-permute-done.17.c2, ...), custom_call_target="tpu_custom_call" | custom-call | bytes 12000000 | tf_op jit(solution)/shard_map/carry/pallas_call | solution.py:552
  77.6 3.5 %collective-permute-done.12.g1 = bf16[256,512]{1,0:T(8,128)(2,1)S(1)} collective-permute-done((bf16[256,512]{1,0:T(8,128)(2,1)S(1)}, bf16[256,512]{1,0:T(8,128)(2,1)S(1)}, u32[]{:S(2)}, u32[]{:S(2)}) %collective-permute-start.12) | collective-permute-done | bytes 262176 | tf_op jit(solution)/shard_map/ppermute | solution.py:577
  81.2 4.5 %collective-permute-done.14.g3 = bf16[256,512]{1,0:T(8,128)(2,1)S(1)} collective-permute-done((bf16[256,512]{1,0:T(8,128)(2,1)S(1)}, bf16[256,512]{1,0:T(8,128)(2,1)S(1)}, u32[]{:S(2)}, u32[]{:S(2)}) %collective-permute-start.14) | collective-permute-done | bytes 262176 | tf_op jit(solution)/shard_map/ppermute | solution.py:577
  86.2 1.9 %collective-permute-start.20 = (f32[8,2560]{1,0:T(8,128)S(1)}, f32[8,2560]{1,0:T(8,128)S(1)}, u32[]{:S(2)}, u32[]{:S(2)}) collective-permute-start(f32[8,2560]{1,0:T(8,128)S(1)} %head.1), channel_id=1, source_target_pairs={{12,4},{20,12},{28,20},{36,28},{44,36},{52,44},{60,52},{13,5},{21,... | collective-permute-start | bytes 245768 | tf_op jit(solution)/shard_map/ppermute | solution.py:577
  89.4 4.4 %last.1 = (bf16[128,2048]{1,0:T(8,128)(2,1)S(1)}, bf16[128,512]{1,0:T(8,128)(2,1)S(1)}, bf16[128,128]{1,0:T(8,128)(2,1)S(1)}, bf16[128,2688]{1,0:T(8,128)(2,1)S(1)}) custom-call(bf16[256,512]{1,0:T(8,128)(2,1)S(1)} %get-tuple-element.116.g0, bf16[256,512]{1,0:T(8,128)(2,1)S(1)} %collective-permute-done.12.g1, ...), custom_call_target="tpu_custom_call" | custom-call | bytes 24000000 | tf_op jit(solution)/shard_map/last/pallas_call | solution.py:552
  94.9 1.8 %collective-permute-done.21.message = bf16[128,2688]{1,0:T(8,128)(2,1)S(1)} collective-permute-done((bf16[128,2688]{1,0:T(8,128)(2,1)S(1)}, bf16[128,2688]{1,0:T(8,128)(2,1)S(1)}, u32[]{:S(2)}, u32[]{:S(2)}) %collective-permute-start.21) | collective-permute-done | bytes 688160 | tf_op jit(solution)/shard_map/ppermute | solution.py:577
  (57 shorter events, 17.1 us)
Async XLA Ops:
  2.5 13.3 %copy-start = (bf16[1,128,4096]{2,1,0:T(8,128)(2,1)S(1)}, bf16[1,128,4096]{2,1,0:T(8,128)(2,1)}, u32[]{:S(2)}) copy-start(bf16[1,128,4096]{2,1,0:T(8,128)(2,1)} %param.11) | copy-start | bytes 3145732
  2.5 9.5 %collective-permute-start = (bf16[128,2688]{1,0:T(8,128)(2,1)S(1)}, bf16[128,2688]{1,0:T(8,128)(2,1)S(1)}, u32[]{:S(2)}, u32[]{:S(2)}) collective-permute-start(bf16[128,2688]{1,0:T(8,128)(2,1)S(1)} %get-tuple-element.70), channel_id=1, source_target_pairs={{0,4},{4,0},{8,12},{12,8},{16,20},{20,16},{24,28},{28,24},{32,36},... | collective-permute-start | bytes 2064392 | tf_op jit(solution)/shard_map/ppermute | solution.py:577
  3.3 8.8 %collective-permute-start.1 = (bf16[16,2560]{1,0:T(8,128)(2,1)S(1)}, bf16[16,2560]{1,0:T(8,128)(2,1)S(1)}, u32[]{:S(2)}, u32[]{:S(2)}) collective-permute-start(bf16[16,2560]{1,0:T(8,128)(2,1)S(1)} %get-tuple-element.71), channel_id=1, source_target_pairs={{4,12},{12,20},{20,28},{28,36},{36,44},{44,52},{52,60},{5,13},{13,... | collective-permute-start | bytes 245768 | tf_op jit(solution)/shard_map/ppermute | solution.py:577
  6.8 5.2 %collective-permute-start.2 = (bf16[16,2560]{1,0:T(8,128)(2,1)S(1)}, bf16[16,2560]{1,0:T(8,128)(2,1)S(1)}, u32[]{:S(2)}, u32[]{:S(2)}) collective-permute-start(bf16[16,2560]{1,0:T(8,128)(2,1)S(1)} %get-tuple-element.72), channel_id=1, source_target_pairs={{4,8},{12,16},{20,24},{28,32},{36,40},{44,48},{52,56},{5,9},{13,17... | collective-permute-start | bytes 245768 | tf_op jit(solution)/shard_map/ppermute | solution.py:577
  12.1 3.8 %copy-start.2 = (f32[4,4096]{1,0:T(4,128)S(1)}, f32[4,4096]{1,0:T(4,128)}, u32[]{:S(2)}) copy-start(f32[4,4096]{1,0:T(4,128)} %v_tap.5) | copy-start | bytes 196612
  12.1 14.9 %collective-permute-start.6 = (bf16[128,2048]{1,0:T(8,128)(2,1)S(1)}, bf16[128,2048]{1,0:T(8,128)(2,1)S(1)}, u32[]{:S(2)}, u32[]{:S(2)}) collective-permute-start(bf16[128,2048]{1,0:T(8,128)(2,1)S(1)} %get-tuple-element.80), channel_id=1, source_target_pairs={{0,64},{64,0},{1,65},{65,1},{2,66},{66,2},{3,67},{67,3},{4,68},{68... | collective-permute-start | bytes 1572872 | tf_op jit(solution)/shard_map/ppermute | solution.py:615
  12.7 24.6 %collective-permute-start.7 = (bf16[128,2048]{1,0:T(8,128)(2,1)S(1)}, bf16[128,2048]{1,0:T(8,128)(2,1)S(1)}, u32[]{:S(2)}, u32[]{:S(2)}) collective-permute-start(bf16[128,2048]{1,0:T(8,128)(2,1)S(1)} %get-tuple-element.81), channel_id=1, source_target_pairs={{0,68},{4,64},{8,76},{12,72},{16,84},{20,80},{24,92},{28,88},{32,1... | collective-permute-start | bytes 1572872 | tf_op jit(solution)/shard_map/ppermute | solution.py:616
  24.2 16.1 %collective-permute-start.3 = (bf16[272,512]{1,0:T(8,128)(2,1)S(1)}, bf16[272,512]{1,0:T(8,128)(2,1)S(1)}, u32[]{:S(2)}, u32[]{:S(2)}) collective-permute-start(bf16[272,512]{1,0:T(8,128)(2,1)S(1)} %get-tuple-element.77), channel_id=1, source_target_pairs={{0,8},{4,12},{8,16},{12,20},{16,24},{20,28},{24,0},{28,4},{32,40},... | collective-permute-start | bytes 835592 | tf_op jit(solution)/shard_map/ppermute | solution.py:577
  24.3 17.5 %collective-permute-start.4 = (bf16[272,512]{1,0:T(8,128)(2,1)S(1)}, bf16[272,512]{1,0:T(8,128)(2,1)S(1)}, u32[]{:S(2)}, u32[]{:S(2)}) collective-permute-start(bf16[272,512]{1,0:T(8,128)(2,1)S(1)} %get-tuple-element.78), channel_id=1, source_target_pairs={{0,16},{4,20},{8,24},{12,28},{16,0},{20,4},{24,8},{28,12},{32,48},... | collective-permute-start | bytes 835592 | tf_op jit(solution)/shard_map/ppermute | solution.py:577
  25.6 16.2 %collective-permute-start.5 = (bf16[272,512]{1,0:T(8,128)(2,1)S(1)}, bf16[272,512]{1,0:T(8,128)(2,1)S(1)}, u32[]{:S(2)}, u32[]{:S(2)}) collective-permute-start(bf16[272,512]{1,0:T(8,128)(2,1)S(1)} %get-tuple-element.79), channel_id=1, source_target_pairs={{0,24},{4,28},{8,0},{12,4},{16,8},{20,12},{24,16},{28,20},{32,56},... | collective-permute-start | bytes 835592 | tf_op jit(solution)/shard_map/ppermute | solution.py:577
  38.9 14.4 %collective-permute-start.8 = (bf16[256,512]{1,0:T(8,128)(2,1)S(1)}, bf16[256,512]{1,0:T(8,128)(2,1)S(1)}, u32[]{:S(2)}, u32[]{:S(2)}) collective-permute-start(bf16[256,512]{1,0:T(8,128)(2,1)S(1)} %get-tuple-element.85), channel_id=1, source_target_pairs={{0,8},{4,12},{8,16},{12,20},{16,24},{20,28},{24,0},{28,4},{32,40},... | collective-permute-start | bytes 786440 | tf_op jit(solution)/shard_map/ppermute | solution.py:577
  39.0 14.3 %collective-permute-start.9 = (bf16[256,512]{1,0:T(8,128)(2,1)S(1)}, bf16[256,512]{1,0:T(8,128)(2,1)S(1)}, u32[]{:S(2)}, u32[]{:S(2)}) collective-permute-start(bf16[256,512]{1,0:T(8,128)(2,1)S(1)} %get-tuple-element.86), channel_id=1, source_target_pairs={{0,16},{4,20},{8,24},{12,28},{16,0},{20,4},{24,8},{28,12},{32,48},... | collective-permute-start | bytes 786440 | tf_op jit(solution)/shard_map/ppermute | solution.py:577
  40.3 13.6 %collective-permute-start.10 = (bf16[256,512]{1,0:T(8,128)(2,1)S(1)}, bf16[256,512]{1,0:T(8,128)(2,1)S(1)}, u32[]{:S(2)}, u32[]{:S(2)}) collective-permute-start(bf16[256,512]{1,0:T(8,128)(2,1)S(1)} %get-tuple-element.87), channel_id=1, source_target_pairs={{0,24},{4,28},{8,0},{12,4},{16,8},{20,12},{24,16},{28,20},{32,56},... | collective-permute-start | bytes 786440 | tf_op jit(solution)/shard_map/ppermute | solution.py:577
  42.1 13.5 %collective-permute-start.15 = (bf16[256,512]{1,0:T(8,128)(2,1)S(1)}, bf16[256,512]{1,0:T(8,128)(2,1)S(1)}, u32[]{:S(2)}, u32[]{:S(2)}) collective-permute-start(bf16[256,512]{1,0:T(8,128)(2,1)S(1)} %edge_forward.1), channel_id=1, source_target_pairs={{0,32},{4,36},{8,40},{12,44},{16,48},{20,52},{24,56},{28,60},{1,33... | collective-permute-start | bytes 786440 | tf_op jit(solution)/shard_map/ppermute | solution.py:577
  54.2 6.7 %collective-permute-start.11 = (bf16[256,512]{1,0:T(8,128)(2,1)S(1)}, bf16[256,512]{1,0:T(8,128)(2,1)S(1)}, u32[]{:S(2)}, u32[]{:S(2)}) collective-permute-start(bf16[256,512]{1,0:T(8,128)(2,1)S(1)} %edge_back.1), channel_id=1, source_target_pairs={{32,0},{36,4},{40,8},{44,12},{48,16},{52,20},{56,24},{60,28},{33,1... | collective-permute-start | bytes 786440 | tf_op jit(solution)/shard_map/ppermute | solution.py:577
  56.5 12.5 %collective-permute-start.16 = (bf16[256,512]{1,0:T(8,128)(2,1)S(1)}, bf16[256,512]{1,0:T(8,128)(2,1)S(1)}, u32[]{:S(2)}, u32[]{:S(2)}) collective-permute-start(bf16[256,512]{1,0:T(8,128)(2,1)S(1)} %get-tuple-element.109), channel_id=1, source_target_pairs={{0,24},{4,28},{8,0},{12,4},{16,8},{20,12},{24,16},{28,20},{32,56},... | collective-permute-start | bytes 786440 | tf_op jit(solution)/shard_map/ppermute | solution.py:577
  59.2 15.8 %collective-permute-start.17 = (bf16[256,512]{1,0:T(8,128)(2,1)S(1)}, bf16[256,512]{1,0:T(8,128)(2,1)S(1)}, u32[]{:S(2)}, u32[]{:S(2)}) collective-permute-start(bf16[256,512]{1,0:T(8,128)(2,1)S(1)} %get-tuple-element.110), channel_id=1, source_target_pairs={{0,16},{4,20},{8,24},{12,28},{16,0},{20,4},{24,8},{28,12},{32,48},... | collective-permute-start | bytes 786440 | tf_op jit(solution)/shard_map/ppermute | solution.py:577
  59.8 15.7 %collective-permute-start.18 = (bf16[256,512]{1,0:T(8,128)(2,1)S(1)}, bf16[256,512]{1,0:T(8,128)(2,1)S(1)}, u32[]{:S(2)}, u32[]{:S(2)}) collective-permute-start(bf16[256,512]{1,0:T(8,128)(2,1)S(1)} %get-tuple-element.111), channel_id=1, source_target_pairs={{0,8},{4,12},{8,16},{12,20},{16,24},{20,28},{24,0},{28,4},{32,40},... | collective-permute-start | bytes 786440 | tf_op jit(solution)/shard_map/ppermute | solution.py:577
  61.8 19.3 %collective-permute-start.12 = (bf16[256,512]{1,0:T(8,128)(2,1)S(1)}, bf16[256,512]{1,0:T(8,128)(2,1)S(1)}, u32[]{:S(2)}, u32[]{:S(2)}) collective-permute-start(bf16[256,512]{1,0:T(8,128)(2,1)S(1)} %get-tuple-element.89), channel_id=1, source_target_pairs={{0,24},{4,28},{8,0},{12,4},{16,8},{20,12},{24,16},{28,20},{32,56},... | collective-permute-start | bytes 786440 | tf_op jit(solution)/shard_map/ppermute | solution.py:577
  64.7 16.5 %collective-permute-start.13 = (bf16[256,512]{1,0:T(8,128)(2,1)S(1)}, bf16[256,512]{1,0:T(8,128)(2,1)S(1)}, u32[]{:S(2)}, u32[]{:S(2)}) collective-permute-start(bf16[256,512]{1,0:T(8,128)(2,1)S(1)} %get-tuple-element.90), channel_id=1, source_target_pairs={{0,16},{4,20},{8,24},{12,28},{16,0},{20,4},{24,8},{28,12},{32,48},... | collective-permute-start | bytes 786440 | tf_op jit(solution)/shard_map/ppermute | solution.py:577
  69.0 16.6 %collective-permute-start.14 = (bf16[256,512]{1,0:T(8,128)(2,1)S(1)}, bf16[256,512]{1,0:T(8,128)(2,1)S(1)}, u32[]{:S(2)}, u32[]{:S(2)}) collective-permute-start(bf16[256,512]{1,0:T(8,128)(2,1)S(1)} %get-tuple-element.91), channel_id=1, source_target_pairs={{0,8},{4,12},{8,16},{12,20},{16,24},{20,28},{24,0},{28,4},{32,40},... | collective-permute-start | bytes 786440 | tf_op jit(solution)/shard_map/ppermute | solution.py:577
  86.2 7.6 %collective-permute-start.20 = (f32[8,2560]{1,0:T(8,128)S(1)}, f32[8,2560]{1,0:T(8,128)S(1)}, u32[]{:S(2)}, u32[]{:S(2)}) collective-permute-start(f32[8,2560]{1,0:T(8,128)S(1)} %head.1), channel_id=1, source_target_pairs={{12,4},{20,12},{28,20},{36,28},{44,36},{52,44},{60,52},{13,5},{21,... | collective-permute-start | bytes 245768 | tf_op jit(solution)/shard_map/ppermute | solution.py:577
  88.1 5.8 %collective-permute-start.19 = (f32[8,2560]{1,0:T(8,128)S(1)}, f32[8,2560]{1,0:T(8,128)S(1)}, u32[]{:S(2)}, u32[]{:S(2)}) collective-permute-start(f32[8,2560]{1,0:T(8,128)S(1)} %head.1), channel_id=1, source_target_pairs={{8,4},{16,12},{24,20},{32,28},{40,36},{48,44},{56,52},{9,5},{17,13... | collective-permute-start | bytes 245768 | tf_op jit(solution)/shard_map/ppermute | solution.py:577
  93.8 2.8 %collective-permute-start.21 = (bf16[128,2688]{1,0:T(8,128)(2,1)S(1)}, bf16[128,2688]{1,0:T(8,128)(2,1)S(1)}, u32[]{:S(2)}, u32[]{:S(2)}) collective-permute-start(bf16[128,2688]{1,0:T(8,128)(2,1)S(1)} %get-tuple-element.127), channel_id=1, source_target_pairs={{0,4},{4,0},{8,12},{12,8},{16,20},{20,16},{24,28},{28,24},{32,36},... | collective-permute-start | bytes 2064392 | tf_op jit(solution)/shard_map/ppermute | solution.py:577
  (9 other events, 9.5 us)

commit v4 on v3

--- a/solution.py
+++ b/solution.py
@@ -23,6 +23,7 @@
 WIDE = HEADS * HEAD_DIM
 PART = WIDE // RING
 TAIL = 16
+HALO = 8
 LOG2E = 1.4426950408889634
 
 
@@ -102,28 +103,50 @@
     return 0.5 + 0.5 * jnp.tanh(0.5 * x)
 
 
-def pack_kernel(v, s, r, message, halo_a, halo_b, sems):
+def run_copies(pairs, sems):
+    copies = [pltpu.make_async_copy(a, b, sems.at[k]) for k, (a, b) in enumerate(pairs)]
+    for copy in copies:
+        copy.start()
+    return copies
+
+
+def pack_kernel(v, s, r, message, halo_a, halo_b, halos, r_here, sems):
     core, ring = place()
     there = 1 - core
-    copies = [
-        (v.at[:, pl.ds(pl.multiple_of(there * WIDE, 128), WIDE)], message.at[:, pl.ds(0, WIDE)]),
-        (
-            s.at[:, pl.ds(pl.multiple_of(there * 2 * STATE, 128), 2 * STATE)],
-            message.at[:, pl.ds(WIDE, 2 * STATE)],
-        ),
-    ]
+    pairs = []
+    rows = pl.ds(TOK - HALO, HALO)
     for group, halo in ((1, halo_a), (0, halo_b)):
-        rows = pl.ds(TOK - TAIL, TAIL)
-        copies.append((v.at[rows, pl.ds(group * WIDE, WIDE)], halo.at[:, pl.ds(0, WIDE)]))
-        copies.append(
+        pairs.append((v.at[rows, pl.ds(group * WIDE, WIDE)], halo.at[:, pl.ds(0, WIDE)]))
+        pairs.append(
             (s.at[rows, pl.ds(group * 2 * STATE, 2 * STATE)], halo.at[:, pl.ds(WIDE, 2 * STATE)])
         )
-    copies = [pltpu.make_async_copy(a, b, sems.at[k]) for k, (a, b) in enumerate(copies)]
-    for copy in copies:
-        copy.start()
-    message[:, WIDE + 2 * STATE :] = tiled_steps(r[...], there).astype(bf16)
+    v_there = pl.ds(pl.multiple_of(there * WIDE, 128), WIDE)
+    s_there = pl.ds(pl.multiple_of(there * 2 * STATE, 128), 2 * STATE)
+    for k, group in enumerate((1, 0)):
+        at = pl.ds(k * HALO, HALO)
+        pairs.append((v.at[rows, pl.ds(group * WIDE, WIDE)], halos.at[at, pl.ds(0, WIDE)]))
+        pairs.append(
+            (s.at[rows, pl.ds(group * 2 * STATE, 2 * STATE)], halos.at[at, pl.ds(WIDE, 2 * STATE)])
+        )
+    pairs.append((v.at[:, v_there], message.at[:, pl.ds(0, WIDE)]))
+    pairs.append((s.at[:, s_there], message.at[:, pl.ds(WIDE, 2 * STATE)]))
+    pairs.append((r, r_here))
+    copies = run_copies(pairs, sems)
+    copies.pop().wait()
+    message[:, WIDE + 2 * STATE :] = tiled_steps(r_here[...], there).astype(bf16)
     for copy in copies:
         copy.wait()
+
+
+def relay_kernel(halo_a, halo_b, relayed, out_a, out_b):
+    index = lax.axis_index("ctx")
+    handing = index == CORES * RING - 1
+    out_a[...] = jnp.where(
+        handing, relayed[:HALO].astype(f32), halo_a[...].astype(f32)
+    ).astype(bf16)
+    out_b[...] = jnp.where(
+        handing, relayed[HALO:].astype(f32), halo_b[...].astype(f32)
+    ).astype(bf16)
 
 
 def pack_grad_kernel(g, own, across, sems):
@@ -148,8 +171,8 @@
 
 def first_kernel(
     v, s, r, message, halo_a, halo_b, step_bias, decay_log, v_tap, v_off, s_tap, s_off, ones,
-    m0, m1, m2, m3, x_out, xs_out, sx_out, k_out, bc_out, sbc_out, delta_out, within_out, sig_out,
-    buf, sbuf, raw, wide,
+    m0, m1, m2, m3, x_out, xs_out, bc_out, pre_out, spre_out, wide, delta_out, within_out, sig_out,
+    buf, sbuf, raw,
 ):
     core, ring = place()
     mine, other = rows_of(core)
@@ -175,35 +198,32 @@
     sbuf[below, :] = s[:, s_mine].astype(f32)
     sbuf[above, :] = message[:, WIDE : WIDE + 2 * STATE].astype(f32)
     halo = halo_a[...].astype(f32) + halo_b[...].astype(f32)
-    buf[0:8, :] = halo[8:16, :WIDE]
-    sbuf[0:8, :] = halo[8:16, WIDE:]
+    buf[0:8, :] = halo[:, :WIDE]
+    sbuf[0:8, :] = halo[:, WIDE:]
 
     def conv(source, tap, off, b, width):
         cols, par = block128(b), block128(b, core * width)
         acc = off[:, par] + tap[0:1, par] * source[5 : 5 + ROWS, cols]
         for j in range(1, CONV):
             acc = acc + tap[j : j + 1, par] * source[5 + j : 5 + j + ROWS, cols]
-        sig = sigmoid_by_tanh(acc)
-        return acc * sig, sig * (1.0 + acc * (1.0 - sig))
+        return acc
 
     def state_block(b, carry):
         cols = block128(b)
-        post, slope = conv(sbuf, s_tap, s_off, b, 2 * STATE)
-        bc_out[:, cols] = post.astype(bf16)
-        sbc_out[:, cols] = slope.astype(bf16)
+        acc = conv(sbuf, s_tap, s_off, b, 2 * STATE)
+        spre_out[:, cols] = acc
+        bc_out[:, cols] = (acc * sigmoid_by_tanh(acc)).astype(bf16)
         return carry
 
     lax.fori_loop(0, 4, state_block, 0)
 
     def value_block(b, carry):
         cols = block128(b)
-        post, slope = conv(buf, v_tap, v_off, b, WIDE)
-        post = post.astype(bf16)
-        scale = wide[:, cols]
+        acc = conv(buf, v_tap, v_off, b, WIDE)
+        pre_out[:, cols] = acc
+        post = (acc * sigmoid_by_tanh(acc)).astype(bf16)
         x_out[:, cols] = post
-        sx_out[:, cols] = slope.astype(bf16)
-        k_out[:, cols] = (slope * scale).astype(bf16)
-        xs_out[:, cols] = (post.astype(f32) * scale).astype(bf16)
+        xs_out[:, cols] = (post.astype(f32) * wide[:, cols]).astype(bf16)
         return carry
 
     lax.fori_loop(0, 16, value_block, 0)
@@ -221,6 +241,28 @@
         out[STATE : STATE + TAIL, :] = jnp.where(
             row == 0, high, jnp.where(row == 1, mid, jnp.where(row == 2, low, 0.0))
         ).astype(bf16)
+
+
+def slope_kernel(pre, spre, wide, sx_out, k_out, sbc_out):
+    def slope(acc):
+        sig = sigmoid_by_tanh(acc)
+        return sig * (1.0 + acc * (1.0 - sig))
+
+    def value_block(b, carry):
+        cols = block128(b)
+        out = slope(pre[:, cols])
+        sx_out[:, cols] = out.astype(bf16)
+        k_out[:, cols] = (out * wide[:, cols]).astype(bf16)
+        return carry
+
+    lax.fori_loop(0, 16, value_block, 0)
+
+    def state_block(b, carry):
+        cols = block128(b)
+        sbc_out[:, cols] = slope(spre[:, cols]).astype(bf16)
+        return carry
+
+    lax.fori_loop(0, 4, state_block, 0)
 
 
 def ring_totals(parts):
@@ -431,26 +473,23 @@
 
 def last_kernel(
     g0, g1, g2, g3, carried, bc, xs, k, base_0, base_1, sbc, delta, within, sig, diff, vsum,
-    dread, dbc, decay_log, v_tap, s_tap, ones,
-    vg_own, sg_own, st_own, message,
-    gbuf, ebuf, sbuf, dbuf, back, sback,
+    dread, dbc, decay_log, ones,
+    e_out, es_out, steps_out,
+    gbuf,
 ):
     core, ring = place()
-    mine, other = rows_of(core)
     for slot, src in enumerate((g0, g1, g2, g3)):
         gbuf[:, head_columns(ring, slot)] = src[...]
     write = bc[:, :STATE]
     rsum = jnp.zeros((ROWS, 128), f32)
     tsum = jnp.zeros((8, 128), f32)
-    ebuf[ROWS : ROWS + 8, :] = jnp.zeros((8, WIDE), f32)
-    sbuf[ROWS : ROWS + 8, :] = jnp.zeros((8, 2 * STATE), f32)
     for b in range(4):
         cols = slice(b * PART, (b + 1) * PART)
         grad = gbuf[:, cols]
         through = nn(write, grad)
         rsum = rsum + head_sum(xs[:, cols].astype(f32) * through, ones[:, cols])
         base = (base_0, base_1)[b // 2][:, (b % 2) * PART : (b % 2 + 1) * PART]
-        ebuf[0:ROWS, cols] = base + k[:, cols].astype(f32) * through
+        e_out[:, cols] = base + k[:, cols].astype(f32) * through
         both = jnp.sum(
             grad.astype(f32) * carried[:, cols].astype(f32), axis=0, keepdims=True
         )
@@ -462,30 +501,41 @@
     earlier = jnp.where(rb < ra, 1.0, 0.0).astype(f32)
     da = nn(later, diff[...], HIGH) + nn(earlier, rsum, HIGH) + dtotal
     rate = -jnp.exp(tiled_heads(decay_log[...], core))
-    dbuf[...] = (vsum[...] + rsum / delta[...] + rate * da) * sig[...]
-    st_own[...] = dbuf[mine, :].astype(bf16)
-    message[:, WIDE + 2 * STATE :] = dbuf[other, :].astype(bf16)
-
+    steps_out[...] = (vsum[...] + rsum / delta[...] + rate * da) * sig[...]
     dwrite = dbc[:, :STATE] + nt(xs[...], gbuf[...])
-    sbuf[0:ROWS, :STATE] = dwrite * sbc[:, :STATE].astype(f32)
-    sbuf[0:ROWS, STATE:] = dread[...] * sbc[:, STATE:].astype(f32)
-
-    def conv(source, tap, b, width):
+    es_out[:, :STATE] = dwrite * sbc[:, :STATE].astype(f32)
+    es_out[:, STATE:] = dread[...] * sbc[:, STATE:].astype(f32)
+
+
+def back_kernel(
+    e, es, steps, head, v_tap, s_tap, vg_own, sg_own, st_own, message, back, sback
+):
+    core, ring = place()
+    mine, other = rows_of(core)
+    body = ROWS - TAIL
+
+    def conv(source, start, tap, b, width, out):
         cols, par = block128(b), block128(b, core * width)
-        acc = tap[CONV - 1 : CONV, par] * source[0:ROWS, cols]
+        edge = jnp.concatenate(
+            [source[body:, cols], head[:, block128(b, start)].astype(f32)], axis=0
+        )
+        acc = tap[CONV - 1 : CONV, par] * source[0:body, cols]
+        end = tap[CONV - 1 : CONV, par] * edge[0:TAIL]
         for shift in range(1, CONV):
-            j = CONV - 1 - shift
-            acc = acc + tap[j : j + 1, par] * source[shift : shift + ROWS, cols]
-        return acc.astype(bf16)
+            weight = tap[CONV - 1 - shift : CONV - shift, par]
+            acc = acc + weight * source[shift : shift + body, cols]
+            end = end + weight * edge[shift : shift + TAIL]
+        out[0:body, cols] = acc.astype(bf16)
+        out[body:, cols] = end.astype(bf16)
 
     def value_block(b, carry):
-        back[:, block128(b)] = conv(ebuf, v_tap, b, WIDE)
+        conv(e, 0, v_tap, b, WIDE, back)
         return carry
 
     lax.fori_loop(0, 16, value_block, 0)
 
     def state_block(b, carry):
-        sback[:, block128(b)] = conv(sbuf, s_tap, b, 2 * STATE)
+        conv(es, WIDE, s_tap, b, 2 * STATE, sback)
         return carry
 
     lax.fori_loop(0, 4, state_block, 0)
@@ -493,6 +543,8 @@
     message[:, :WIDE] = back[other, :]
     sg_own[...] = sback[mine, :]
     message[:, WIDE : WIDE + 2 * STATE] = sback[other, :]
+    st_own[...] = steps[mine, :].astype(bf16)
+    message[:, WIDE + 2 * STATE :] = steps[other, :].astype(bf16)
 
 
 def head_kernel(g0, g1, g2, g3, bc, xs, k, base_top, sbc, dread, dbc, out):
@@ -503,42 +555,24 @@
         cols = head_columns(ring, slot)
         grad = src[...]
         through = nn(write, grad)[0:8]
-        out[:, cols] = base_top[:, cols] + k[0:TAIL, cols].astype(f32)[0:8] * through
+        out[:, cols] = (
+            base_top[:, cols] + k[0:TAIL, cols].astype(f32)[0:8] * through
+        ).astype(bf16)
         dwrite = dwrite + nt(xs[0:TAIL, cols], grad)[0:8]
     slope = sbc[0:TAIL, :].astype(f32)[0:8]
-    out[:, WIDE : WIDE + STATE] = dwrite * slope[:, :STATE]
-    out[:, WIDE + STATE :] = dread[0:8, :] * slope[:, STATE:]
-
-
-def join_kernel(v_own, s_own, t_own, message, e0, e1, v_tap, s_tap, v_out, s_out, t_out):
+    out[:, WIDE : WIDE + STATE] = (dwrite * slope[:, :STATE]).astype(bf16)
+    out[:, WIDE + STATE :] = (dread[0:8, :] * slope[:, STATE:]).astype(bf16)
+
+
+def join_kernel(v_own, s_own, t_own, message, v_out, s_out, t_out):
     core, ring = place()
 
     def place_in(out, own, arrived, width):
         out[:, pl.ds(pl.multiple_of(core * width, 128), width)] = own
         out[:, pl.ds(pl.multiple_of((1 - core) * width, 128), width)] = arrived
 
-    def patch(out, tap, edge, width, group, start):
-        cols = slice(group * width, (group + 1) * width)
-        rows = edge[:, start : start + width]
-        row = iota((TAIL, width), 0)
-        acc = out[TOK - TAIL :, cols].astype(f32)
-        for shift in range(1, CONV):
-            j = CONV - 1 - shift
-            for k in range(shift):
-                acc = acc + jnp.where(
-                    row == TAIL - shift + k, tap[j : j + 1, cols] * rows[k : k + 1], 0.0
-                )
-        out[TOK - TAIL :, cols] = acc.astype(bf16)
-
     place_in(v_out, v_own[...], message[:, :WIDE], WIDE)
     place_in(s_out, s_own[...], message[:, WIDE : WIDE + 2 * STATE], 2 * STATE)
-
-    @pl.when(core == CORES - 1)
-    def _():
-        for group, edge in enumerate((e0, e1)):
-            patch(v_out, v_tap, edge, WIDE, group, 0)
-            patch(s_out, s_tap, edge, 2 * STATE, group, WIDE)
-
     own = t_own[...].astype(f32).T[:HEADS]
     arrived = message[:, WIDE + 2 * STATE :].astype(f32).T[:HEADS]
     low = jnp.where(core == 0, own, arrived)
@@ -583,9 +617,9 @@
         return (half * RING + (at + shift) % RING) * CORES + c
 
     def exchange(parts, sign):
-        out = [parts[0]]
-        for k in range(1, RING):
-            out.append(send(parts[k], [(i, around(i, sign * k)) for i in range(count)]))
+        out = list(parts)
+        for k in (2, 1, 3):
+            out[k] = send(parts[k], [(i, around(i, sign * k)) for i in range(count)])
         return out
 
     row = lambda x: x.reshape(1, -1)
@@ -598,20 +632,37 @@
     state_part = ((STATE, PART), bf16)
     sems = pltpu.SemaphoreType.DMA
 
-    message, halo_a, halo_b = call(
+    message, halo_a, halo_b, halos = call(
         pack_kernel, [v, s, r],
-        [((TOK, joint), bf16), ((TAIL, WIDE + 2 * STATE), bf16), ((TAIL, WIDE + 2 * STATE), bf16)],
-        [sems((6,))], "pack", (0, 1),
+        [((TOK, joint), bf16), ((HALO, WIDE + 2 * STATE), bf16), ((HALO, WIDE + 2 * STATE), bf16),
+         ((2 * HALO, WIDE + 2 * STATE), bf16)],
+        [((2 * HEADS, TOK), bf16), sems((11,))], "pack", (0, 1, 2),
+    )
+    middle = per_half - 1
+    relayed = lax.ppermute(
+        halos, ("pipe", "ctx"),
+        [(p * count + middle, (1 - p) * count + middle) for p in range(2)],
     )
     message = send(message, swap_pairs)
-    halo_a = send(halo_a, [(k * 2 + 1, k * 2 + 3) for k in range(chips - 1)])
-    halo_b = send(halo_b, [(k * 2 + 1, k * 2 + 2) for k in range(chips - 1)])
+    halo_a, halo_b = call(
+        relay_kernel, [halo_a, halo_b, relayed], [((HALO, WIDE + 2 * STATE), bf16)] * 2, (), "relay"
+    )
+
+    def onward(x, step):
+        pairs = []
+        for p in range(2):
+            for k in range(chips - 1):
+                source = k * CORES + 1
+                held = 1 - p if source == middle else p
+                pairs.append((held * count + source, p * count + source + step))
+        return lax.ppermute(x, ("pipe", "ctx"), pairs)
+
     g_own, g_in = call(
         pack_grad_kernel, [g], [((TOK, WIDE), bf16)] * 2, [sems((2,))], "pack_grad", (0,)
     )
-    g_own, g_in, message, halo_a, halo_b = lax.optimization_barrier(
-        (g_own, g_in, message, halo_a, halo_b)
-    )
+    g_own, g_in, halo_a, halo_b = lax.optimization_barrier((g_own, g_in, halo_a, halo_b))
+    halo_a = onward(halo_a, 2)
+    halo_b = onward(halo_b, 1)
     g_own = lax.ppermute(g_own, "pipe", [(0, 1), (1, 0)])
     g_in = lax.ppermute(
         g_in,
@@ -619,15 +670,22 @@
         [(p * count + i, (1 - p) * count + (i ^ 1)) for p in range(2) for i in range(count)],
     )
     ones = call(ones_kernel, [], [((128, WIDE), bf16)], name="ones")[0]
-    (m0, m1, m2, m3, x, xs, sx, k, bc, sbc, delta, within, sig) = call(
+    (m0, m1, m2, m3, x, xs, bc, pre, spre, spread_scale, delta, within, sig) = call(
         first_kernel,
         [v, s, r, message, halo_a, halo_b, bias, rate_log,
          value_kernel, row(value_offset), state_kernel, row(state_offset), ones],
-        [marked] * 4 + [(tall, bf16)] * 4 + [((ROWS, 2 * STATE), bf16)] * 2 + [(narrow, f32)] * 3,
-        [((ROWS + 8, WIDE), f32), ((ROWS + 8, 2 * STATE), f32), (narrow, f32), (tall, f32)],
+        [marked] * 4 + [(tall, bf16)] * 2
+        + [((ROWS, 2 * STATE), bf16), (tall, f32), ((ROWS, 2 * STATE), f32), (tall, f32)]
+        + [(narrow, f32)] * 3,
+        [((ROWS + 8, WIDE), f32), ((ROWS + 8, 2 * STATE), f32), (narrow, f32)],
         "first", cost=8,
     )
     marks = exchange((m0, m1, m2, m3), 1)
+    sx, k, sbc = call(
+        slope_kernel, [pre, spre, spread_scale],
+        [(tall, bf16), (tall, bf16), ((ROWS, 2 * STATE), bf16)], (), "slopes", cost=2,
+    )
+    g_own, sx = lax.optimization_barrier((g_own, sx))
     d0, d1, d2, d3, dy, dye = call(
         second_kernel, [g_own, g_in, bc, within, ones],
         [state_part] * 4 + [(tall, bf16)] * 2, [(tall, f32)], "second", cost=4,
@@ -655,6 +713,7 @@
         [state_part] * 4, (), "scan_forward", cost=3,
     )
     carried = exchange(steps, -1)
+    *grads, _ = lax.optimization_barrier((*grads, base_0))
     edge_back = call(
         functools.partial(edge_kernel, True), marks + grads, [state_part], (), "edge_back", cost=2,
     )[0]
@@ -678,27 +737,27 @@
     )
     head = call(
         head_kernel, list(back) + [bc, xs, k, base_top, sbc, dread, dbc],
-        [((8, WIDE + 2 * STATE), f32)], (), "head", cost=1,
+        [((8, WIDE + 2 * STATE), bf16)], (), "head", cost=1,
     )[0]
     back[0], head = lax.optimization_barrier((back[0], head))
-    e0 = send(head, [(j * 2, j * 2 - 1) for j in range(1, chips)])
-    e1 = send(head, [(j * 2 + 1, j * 2 - 1) for j in range(1, chips)])
-    vg_own, sg_own, st_own, message = call(
+    head = send(head, [(i, i - CORES) for i in range(CORES, count)])
+    e, es, steps = call(
         last_kernel,
         list(back)
         + [held, bc, xs, k, base_0, base_1, sbc, delta, within, sig, diff, vsum, dread, dbc,
-           rate_log, value_kernel, state_kernel, ones],
+           rate_log, ones],
+        [(tall, f32), ((ROWS, 2 * STATE), f32), (narrow, f32)],
+        [((STATE, WIDE), bf16)], "last", cost=5,
+    )
+    vg_own, sg_own, st_own, message = call(
+        back_kernel, [e, es, steps, head, value_kernel, state_kernel],
         [((TOK, WIDE), bf16), ((TOK, 2 * STATE), bf16), ((TOK, 128), bf16),
          ((TOK, joint), bf16)],
-        [((STATE, WIDE), bf16), ((ROWS + 8, WIDE), f32), ((ROWS + 8, 2 * STATE), f32),
-         (narrow, f32), (tall, bf16), ((ROWS, 2 * STATE), bf16)],
-        "last", cost=8,
-    )
-    message, e0, e1 = lax.optimization_barrier((message, e0, e1))
+        [(tall, bf16), ((ROWS, 2 * STATE), bf16)], "back", cost=3,
+    )
     message = send(message, swap_pairs)
     value_out, state_out, step_out = call(
-        join_kernel,
-        [vg_own, sg_own, st_own, message, e0, e1, value_kernel, state_kernel],
+        join_kernel, [vg_own, sg_own, st_own, message],
         [((TOK, 2 * WIDE), bf16), ((TOK, 4 * STATE), bf16), ((2 * HEADS, TOK), bf16)],
         (), "join",
     )

time: 98.3 us -> 94.9 us (0.965)
  waiting for transfers between devices: 32.8 us -> 23.8 us
  starting transfers between devices: 28.3 us -> 36.3 us
  local copies, waits for them, and re-layouts: 2.04 us -> 0.04 us
    ppermute x20 -> x17, waiting for transfers between devices: 22.4 us -> 15.2 us  [send(): return lax.ppermute(x, 'ctx', pairs)]
    ppermute x1, waiting for transfers between devices: 10.4 us -> 3.18 us  [local(): lax.ppermute(g_in, ('pipe', 'ctx'), [(p * count + i, (1 - p) * count + (i...]
    ppermute x0 -> x3, starting transfers between devices: none -> 5.48 us  [the longest x2 4.83 us: onward(): return lax.ppermute(x, ('pipe', 'ctx'), pairs)]
    ppermute x0 -> x3, waiting for transfers between devices: none -> 5.46 us  [the longest x2 5.46 us: onward(): return lax.ppermute(x, ('pipe', 'ctx'), pairs)]
    ppermute x20 -> x17, starting transfers between devices: 24.6 us -> 29.1 us  [send(): return lax.ppermute(x, 'ctx', pairs)]
    unnamed x22 -> x20, local copies, waits for them, and re-layouts: 2.04 us -> 0.04 us
    ppermute x1, starting transfers between devices: 3.05 us -> 1.11 us  [local(): lax.ppermute(g_in, ('pipe', 'ctx'), [(p * count + i, (1 - p) * count + (i...]
    pallas_call x15 -> x18, Pallas kernels: 33.9 us -> 33.5 us  [call(): pl.pallas_call(kernel, in_specs=[pl.BlockSpec(memory_space=pltpu.HBM) if...]
  transfers between devices with their start and end apart: 22 -> 22, of which waited for: 11 -> 10; matrix products, arithmetic and copies ran while one was open for 0% -> 0% of each run, Pallas kernels for 32% -> 31%
where the time goes in v4:
time: 94.9 us; the launch traced here: 94.6 us
  starting transfers between devices  36.3 us (38%)
  Pallas kernels  33.5 us (35%)
  waiting for transfers between devices  23.8 us (25%)
  between operations  1.01 us (1%)
    pallas_call x18, Pallas kernels, call(): pl.pallas_call(kernel, in_specs=[pl.BlockSpec(memory_space=pltpu.HBM) if...  33.5 us
    ppermute x17, starting transfers between devices, send(): return lax.ppermute(x, 'ctx', pairs)  29.1 us
    ppermute x17, waiting for transfers between devices, send(): return lax.ppermute(x, 'ctx', pairs)  15.2 us
    ppermute x2, waiting for transfers between devices, onward(): return lax.ppermute(x, ('pipe', 'ctx'), pairs)  5.46 us
    ppermute x2, starting transfers between devices, onward(): return lax.ppermute(x, ('pipe', 'ctx'), pairs)  4.83 us
    ppermute x1, waiting for transfers between devices, local(): lax.ppermute(g_in, ('pipe', 'ctx'), [(p * count + i, (1 - p) * count + (i...  3.18 us
  transfers between devices with their start and end apart: 22, of which 10 were waited for; matrix products, arithmetic and copies ran while one was open for 0% of the time, Pallas kernels for 31%

profile of v4, /device:TPU:15, one launch (start us, length us, event | category | flops | bytes accessed | tf_op | source)
XLA Modules:
  0.0 94.6 jit_solution(12285463562593057334)
XLA Ops:
  6.5 3.5 %collective-permute-start.2 = (bf16[8,2560]{1,0:T(8,128)(2,1)S(1)}, bf16[8,2560]{1,0:T(8,128)(2,1)S(1)}, u32[]{:S(2)}, u32[]{:S(2)}) collective-permute-start(bf16[8,2560]{1,0:T(8,128)(2,1)S(1)} %get-tuple-element.87), channel_id=1, source_target_pairs={{4,12},{12,20},{20,28},{92,36},{36,44},{44,52},{52,60},{68,76},{76... | collective-permute-start | bytes 122888 | tf_op jit(solution)/shard_map/ppermute | solution.py:658
  11.4 5.5 %collective-permute-done.2.halo_a = bf16[8,2560]{1,0:T(8,128)(2,1)S(1)} collective-permute-done((bf16[8,2560]{1,0:T(8,128)(2,1)S(1)}, bf16[8,2560]{1,0:T(8,128)(2,1)S(1)}, u32[]{:S(2)}, u32[]{:S(2)}) %collective-permute-start.2) | collective-permute-done | bytes 40992 | tf_op jit(solution)/shard_map/ppermute | solution.py:658
  17.0 6.0 %first.1 = (bf16[272,512]{1,0:T(8,128)(2,1)S(1)}, bf16[272,512]{1,0:T(8,128)(2,1)S(1)}, bf16[272,512]{1,0:T(8,128)(2,1)S(1)}, bf16[272,512]{1,0:T(8,128)(2,1)S(1...) custom-call(bf16[128,4096]{1,0:T(8,128)(2,1)S(1)} %bitcast.17, ...), custom_call_target="tpu_custom_call" | custom-call | bytes 24000000 | tf_op jit(solution)/shard_map/first/pallas_call | solution.py:586
  23.2 2.6 %collective-permute-start.6 = (bf16[272,512]{1,0:T(8,128)(2,1)S(1)}, bf16[272,512]{1,0:T(8,128)(2,1)S(1)}, u32[]{:S(2)}, u32[]{:S(2)}) collective-permute-start(bf16[272,512]{1,0:T(8,128)(2,1)S(1)} %get-tuple-element.92), channel_id=1, source_target_pairs={{0,24},{4,28},{8,0},{12,4},{16,8},{20,12},{24,16},{28,20},{32,56},... | collective-permute-start | bytes 835592 | tf_op jit(solution)/shard_map/ppermute | solution.py:611
  26.9 3.2 %collective-permute-done.8.g_in = bf16[128,2048]{1,0:T(8,128)(2,1)S(1)} collective-permute-done((bf16[128,2048]{1,0:T(8,128)(2,1)S(1)}, bf16[128,2048]{1,0:T(8,128)(2,1)S(1)}, u32[]{:S(2)}, u32[]{:S(2)}) %collective-permute-start.8) | collective-permute-done | bytes 524320 | tf_op jit(solution)/shard_map/ppermute | solution.py:667
  30.0 1.6 %second.1 = (bf16[256,512]{1,0:T(8,128)(2,1)S(1)}, bf16[256,512]{1,0:T(8,128)(2,1)S(1)}, bf16[256,512]{1,0:T(8,128)(2,1)S(1)}, bf16[256,512]{1,0:T(8,128)(2,1)S(...) custom-call(bf16[128,2048]{1,0:T(8,128)(2,1)S(1)} %collective-permute-done.7.g_own, ...), custom_call_target="tpu_custom_call" | custom-call | bytes 12000000 | tf_op jit(solution)/shard_map/second/pallas_call | solution.py:586
  31.6 1.7 %collective-permute-start.9 = (bf16[256,512]{1,0:T(8,128)(2,1)S(1)}, bf16[256,512]{1,0:T(8,128)(2,1)S(1)}, u32[]{:S(2)}, u32[]{:S(2)}) collective-permute-start(bf16[256,512]{1,0:T(8,128)(2,1)S(1)} %get-tuple-element.103), channel_id=1, source_target_pairs={{0,8},{4,12},{8,16},{12,20},{16,24},{20,28},{24,0},{28,4},{32,40},... | collective-permute-start | bytes 786440 | tf_op jit(solution)/shard_map/ppermute | solution.py:611
  33.3 3.3 %collective-permute-start.10 = (bf16[256,512]{1,0:T(8,128)(2,1)S(1)}, bf16[256,512]{1,0:T(8,128)(2,1)S(1)}, u32[]{:S(2)}, u32[]{:S(2)}) collective-permute-start(bf16[256,512]{1,0:T(8,128)(2,1)S(1)} %get-tuple-element.104), channel_id=1, source_target_pairs={{0,16},{4,20},{8,24},{12,28},{16,0},{20,4},{24,8},{28,12},{32,48},... | collective-permute-start | bytes 786440 | tf_op jit(solution)/shard_map/ppermute | solution.py:611
  40.1 5.7 %inner_0.1 = (f32[256,1024]{1,0:T(8,128)S(1)}, f32[256,256]{1,0:T(8,128)S(1)}, f32[256,128]{1,0:T(8,128)S(1)}, f32[256,128]{1,0:T(8,128)S(1)}) custom-call(bf16[256,2048]{1,0:T(8,128)(2,1)S(1)} %get-tuple-element.106.x, bf16[256,2048]{1,0:T(8,128)(2,1)S(1)} %get-tuple-element.122.dy, bf16[256,512]{1,0:T(8,128)(2,1)S(1)} %get-tuple-element.100.bc, ...), custom_call_target="tpu_custom_call" | custom-call | bytes 18000000 | tf_op jit(solution)/shard_map/inner_0/pallas_call | solution.py:586
  45.9 2.9 %collective-permute-done.10.d2 = bf16[256,512]{1,0:T(8,128)(2,1)S(1)} collective-permute-done((bf16[256,512]{1,0:T(8,128)(2,1)S(1)}, bf16[256,512]{1,0:T(8,128)(2,1)S(1)}, u32[]{:S(2)}, u32[]{:S(2)}) %collective-permute-start.10) | collective-permute-done | bytes 262176 | tf_op jit(solution)/shard_map/ppermute | solution.py:611
  49.2 2.5 %collective-permute-start.12 = (bf16[256,512]{1,0:T(8,128)(2,1)S(1)}, bf16[256,512]{1,0:T(8,128)(2,1)S(1)}, u32[]{:S(2)}, u32[]{:S(2)}) collective-permute-start(bf16[256,512]{1,0:T(8,128)(2,1)S(1)} %edge_back.1), channel_id=1, source_target_pairs={{32,0},{36,4},{40,8},{44,12},{48,16},{52,20},{56,24},{60,28},{33,1... | collective-permute-start | bytes 786440 | tf_op jit(solution)/shard_map/ppermute | solution.py:611
  52.7 4.0 %collective-permute-start.17 = (bf16[256,512]{1,0:T(8,128)(2,1)S(1)}, bf16[256,512]{1,0:T(8,128)(2,1)S(1)}, u32[]{:S(2)}, u32[]{:S(2)}) collective-permute-start(bf16[256,512]{1,0:T(8,128)(2,1)S(1)} %get-tuple-element.131), channel_id=1, source_target_pairs={{0,24},{4,28},{8,0},{12,4},{16,8},{20,12},{24,16},{28,20},{32,56},... | collective-permute-start | bytes 786440 | tf_op jit(solution)/shard_map/ppermute | solution.py:611
  58.3 2.0 %collective-permute-start.13 = (bf16[256,512]{1,0:T(8,128)(2,1)S(1)}, bf16[256,512]{1,0:T(8,128)(2,1)S(1)}, u32[]{:S(2)}, u32[]{:S(2)}) collective-permute-start(bf16[256,512]{1,0:T(8,128)(2,1)S(1)} %get-tuple-element.117), channel_id=1, source_target_pairs={{0,24},{4,28},{8,0},{12,4},{16,8},{20,12},{24,16},{28,20},{32,56},... | collective-permute-start | bytes 786440 | tf_op jit(solution)/shard_map/ppermute | solution.py:611
  60.3 1.8 %collective-permute-start.14 = (bf16[256,512]{1,0:T(8,128)(2,1)S(1)}, bf16[256,512]{1,0:T(8,128)(2,1)S(1)}, u32[]{:S(2)}, u32[]{:S(2)}) collective-permute-start(bf16[256,512]{1,0:T(8,128)(2,1)S(1)} %get-tuple-element.118), channel_id=1, source_target_pairs={{0,16},{4,20},{8,24},{12,28},{16,0},{20,4},{24,8},{28,12},{32,48},... | collective-permute-start | bytes 786440 | tf_op jit(solution)/shard_map/ppermute | solution.py:611
  62.1 1.7 %collective-permute-done.17.c1 = bf16[256,512]{1,0:T(8,128)(2,1)S(1)} collective-permute-done((bf16[256,512]{1,0:T(8,128)(2,1)S(1)}, bf16[256,512]{1,0:T(8,128)(2,1)S(1)}, u32[]{:S(2)}, u32[]{:S(2)}) %collective-permute-start.17) | collective-permute-done | bytes 262176 | tf_op jit(solution)/shard_map/ppermute | solution.py:611
  63.7 5.9 %inner_1.1 = (f32[256,1024]{1,0:T(8,128)S(1)}, f32[256,512]{1,0:T(8,128)S(1)}, f32[256,128]{1,0:T(8,128)S(1)}, f32[256,128]{1,0:T(8,128)S(1)}, f32[8,2048]{1,0:T(8,128)S(1)}) custom-call(bf16[256,2048]{1,0:T(8,128)(2,1)S(1)} %get-tuple-element.106.x, bf16[256,2048]{1,0:T(8,128)(2,1)S(1)} %get-tuple-element.122.dy, ...), custom_call_target="tpu_custom_call" | custom-call | bytes 18000000 | tf_op jit(solution)/shard_map/inner_1/pallas_call | solution.py:586
  69.6 2.1 %carry.1 = (f32[256,128]{1,0:T(8,128)S(1)}, f32[256,256]{1,0:T(8,128)S(1)}, bf16[256,2048]{1,0:T(8,128)(2,1)S(1)}) custom-call(bf16[256,512]{1,0:T(8,128)(2,1)S(1)} %get-tuple-element.130.c0, bf16[256,512]{1,0:T(8,128)(2,1)S(1)} %collective-permute-done.17.c1, bf16[256,512]{1,0:T(8,128)(2,1)S(1)} %collective-permute-done.18.c2, ...), custom_call_target="tpu_custom_call" | custom-call | bytes 12000000 | tf_op jit(solution)/shard_map/carry/pallas_call | solution.py:586
  71.7 3.1 %collective-permute-done.13.g1 = bf16[256,512]{1,0:T(8,128)(2,1)S(1)} collective-permute-done((bf16[256,512]{1,0:T(8,128)(2,1)S(1)}, bf16[256,512]{1,0:T(8,128)(2,1)S(1)}, u32[]{:S(2)}, u32[]{:S(2)}) %collective-permute-start.13) | collective-permute-done | bytes 262176 | tf_op jit(solution)/shard_map/ppermute | solution.py:611
  74.8 3.6 %collective-permute-done.15.g3 = bf16[256,512]{1,0:T(8,128)(2,1)S(1)} collective-permute-done((bf16[256,512]{1,0:T(8,128)(2,1)S(1)}, bf16[256,512]{1,0:T(8,128)(2,1)S(1)}, u32[]{:S(2)}, u32[]{:S(2)}) %collective-permute-start.15) | collective-permute-done | bytes 262176 | tf_op jit(solution)/shard_map/ppermute | solution.py:611
  79.0 4.5 %collective-permute-start.20 = (bf16[8,2560]{1,0:T(8,128)(2,1)S(1)}, bf16[8,2560]{1,0:T(8,128)(2,1)S(1)}, u32[]{:S(2)}, u32[]{:S(2)}) collective-permute-start(bf16[8,2560]{1,0:T(8,128)(2,1)S(1)} %head.1), channel_id=1, source_target_pairs={{8,0},{12,4},{16,8},{20,12},{24,16},{28,20},{32,24},{36,28},{40,32... | collective-permute-start | bytes 122888 | tf_op jit(solution)/shard_map/ppermute | solution.py:611
  83.5 2.9 %last.1 = (f32[256,2048]{1,0:T(8,128)S(1)}, f32[256,512]{1,0:T(8,128)S(1)}, f32[256,128]{1,0:T(8,128)S(1)}) custom-call(bf16[256,512]{1,0:T(8,128)(2,1)S(1)} %get-tuple-element.138.g0, bf16[256,512]{1,0:T(8,128)(2,1)S(1)} %collective-permute-done.13.g1, bf16[256,512]{1,0:T(8,128)(2,1)S(1)} %collective-permute-done.14.g2, ...), custom_call_target="tpu_custom_call" | custom-call | bytes 15000000 | tf_op jit(solution)/shard_map/last/pallas_call | solution.py:586
  86.4 1.5 %back.1 = (bf16[128,2048]{1,0:T(8,128)(2,1)S(1)}, bf16[128,512]{1,0:T(8,128)(2,1)S(1)}, bf16[128,128]{1,0:T(8,128)(2,1)S(1)}, bf16[128,2688]{1,0:T(8,128)(2,1)S(1)}) custom-call(f32[256,2048]{1,0:T(8,128)S(1)} %get-tuple-element.144.e, f32[256,512]{1,0:T(8,128)S(1)} %get-tuple-element.145.es, f32[256,128]{1,0:T(8,128)S(1)} %get-tuple-element.146.steps, ...), custom_call_target="tpu_custom_call" | custom-call | bytes 9000000 | tf_op jit(solution)/shard_map/back/pallas_call | solution.py:586
  87.9 3.8 %collective-permute-start.21 = (bf16[128,2688]{1,0:T(8,128)(2,1)S(1)}, bf16[128,2688]{1,0:T(8,128)(2,1)S(1)}, u32[]{:S(2)}, u32[]{:S(2)}) collective-permute-start(bf16[128,2688]{1,0:T(8,128)(2,1)S(1)} %get-tuple-element.151), channel_id=1, source_target_pairs={{0,4},{4,0},{8,12},{12,8},{16,20},{20,16},{24,28},{28,24},{32,36},... | collective-permute-start | bytes 2064392 | tf_op jit(solution)/shard_map/ppermute | solution.py:611
  91.7 1.8 %collective-permute-done.21.message = bf16[128,2688]{1,0:T(8,128)(2,1)S(1)} collective-permute-done((bf16[128,2688]{1,0:T(8,128)(2,1)S(1)}, bf16[128,2688]{1,0:T(8,128)(2,1)S(1)}, u32[]{:S(2)}, u32[]{:S(2)}) %collective-permute-start.21) | collective-permute-done | bytes 688160 | tf_op jit(solution)/shard_map/ppermute | solution.py:611
  (58 shorter events, 16.6 us)
Async XLA Ops:
  0.6 16.2 %copy-start.4 = (bf16[1,128,64]{1,2,0:T(8,128)(2,1)S(1)}, bf16[1,128,64]{1,2,0:T(8,128)(2,1)}, u32[]{:S(2)}) copy-start(bf16[1,128,64]{1,2,0:T(8,128)(2,1)} %param.13) | copy-start | bytes 49156
  0.6 16.2 %copy-start.1 = (bf16[1,128,1024]{2,1,0:T(8,128)(2,1)S(1)}, bf16[1,128,1024]{2,1,0:T(8,128)(2,1)}, u32[]{:S(2)}) copy-start(bf16[1,128,1024]{2,1,0:T(8,128)(2,1)} %param.12) | copy-start | bytes 786436
  2.1 14.8 %collective-permute-start = (bf16[128,2688]{1,0:T(8,128)(2,1)S(1)}, bf16[128,2688]{1,0:T(8,128)(2,1)S(1)}, u32[]{:S(2)}, u32[]{:S(2)}) collective-permute-start(bf16[128,2688]{1,0:T(8,128)(2,1)S(1)} %get-tuple-element.79), channel_id=1, source_target_pairs={{0,4},{4,0},{8,12},{12,8},{16,20},{20,16},{24,28},{28,24},{32,36},... | collective-permute-start | bytes 2064392 | tf_op jit(solution)/shard_map/ppermute | solution.py:611
  2.8 1.9 %collective-permute-start.1 = (bf16[16,2560]{1,0:T(8,128)(2,1)S(1)}, bf16[16,2560]{1,0:T(8,128)(2,1)S(1)}, u32[]{:S(2)}, u32[]{:S(2)}) collective-permute-start(bf16[16,2560]{1,0:T(8,128)(2,1)S(1)} %get-tuple-element.84), channel_id=1, source_target_pairs={{28,92},{92,28},{29,93},{93,29},{30,94},{94,30},{31,95},{95,31}} | collective-permute-start | bytes 245768 | tf_op jit(solution)/shard_map/ppermute | solution.py:642
  4.8 22.1 %collective-permute-start.7 = (bf16[128,2048]{1,0:T(8,128)(2,1)S(1)}, bf16[128,2048]{1,0:T(8,128)(2,1)S(1)}, u32[]{:S(2)}, u32[]{:S(2)}) collective-permute-start(bf16[128,2048]{1,0:T(8,128)(2,1)S(1)} %get-tuple-element.93), channel_id=1, source_target_pairs={{0,64},{64,0},{1,65},{65,1},{2,66},{66,2},{3,67},{67,3},{4,68},{68... | collective-permute-start | bytes 1572872 | tf_op jit(solution)/shard_map/ppermute | solution.py:666
  5.4 24.6 %collective-permute-start.8 = (bf16[128,2048]{1,0:T(8,128)(2,1)S(1)}, bf16[128,2048]{1,0:T(8,128)(2,1)S(1)}, u32[]{:S(2)}, u32[]{:S(2)}) collective-permute-start(bf16[128,2048]{1,0:T(8,128)(2,1)S(1)} %get-tuple-element.99), channel_id=1, source_target_pairs={{0,68},{4,64},{8,76},{12,72},{16,84},{20,80},{24,92},{28,88},{32,1... | collective-permute-start | bytes 1572872 | tf_op jit(solution)/shard_map/ppermute | solution.py:667
  6.5 10.3 %collective-permute-start.2 = (bf16[8,2560]{1,0:T(8,128)(2,1)S(1)}, bf16[8,2560]{1,0:T(8,128)(2,1)S(1)}, u32[]{:S(2)}, u32[]{:S(2)}) collective-permute-start(bf16[8,2560]{1,0:T(8,128)(2,1)S(1)} %get-tuple-element.87), channel_id=1, source_target_pairs={{4,12},{12,20},{20,28},{92,36},{36,44},{44,52},{52,60},{68,76},{76... | collective-permute-start | bytes 122888 | tf_op jit(solution)/shard_map/ppermute | solution.py:658
  10.1 6.8 %collective-permute-start.3 = (bf16[8,2560]{1,0:T(8,128)(2,1)S(1)}, bf16[8,2560]{1,0:T(8,128)(2,1)S(1)}, u32[]{:S(2)}, u32[]{:S(2)}) collective-permute-start(bf16[8,2560]{1,0:T(8,128)(2,1)S(1)} %get-tuple-element.88), channel_id=1, source_target_pairs={{4,8},{12,16},{20,24},{92,32},{36,40},{44,48},{52,56},{68,72},{76,... | collective-permute-start | bytes 122888 | tf_op jit(solution)/shard_map/ppermute | solution.py:658
  23.0 14.3 %collective-permute-start.4 = (bf16[272,512]{1,0:T(8,128)(2,1)S(1)}, bf16[272,512]{1,0:T(8,128)(2,1)S(1)}, u32[]{:S(2)}, u32[]{:S(2)}) collective-permute-start(bf16[272,512]{1,0:T(8,128)(2,1)S(1)} %get-tuple-element.90), channel_id=1, source_target_pairs={{0,8},{4,12},{8,16},{12,20},{16,24},{20,28},{24,0},{28,4},{32,40},... | collective-permute-start | bytes 835592 | tf_op jit(solution)/shard_map/ppermute | solution.py:611
  23.1 14.2 %collective-permute-start.5 = (bf16[272,512]{1,0:T(8,128)(2,1)S(1)}, bf16[272,512]{1,0:T(8,128)(2,1)S(1)}, u32[]{:S(2)}, u32[]{:S(2)}) collective-permute-start(bf16[272,512]{1,0:T(8,128)(2,1)S(1)} %get-tuple-element.91), channel_id=1, source_target_pairs={{0,16},{4,20},{8,24},{12,28},{16,0},{20,4},{24,8},{28,12},{32,48},... | collective-permute-start | bytes 835592 | tf_op jit(solution)/shard_map/ppermute | solution.py:611
  23.2 15.4 %collective-permute-start.6 = (bf16[272,512]{1,0:T(8,128)(2,1)S(1)}, bf16[272,512]{1,0:T(8,128)(2,1)S(1)}, u32[]{:S(2)}, u32[]{:S(2)}) collective-permute-start(bf16[272,512]{1,0:T(8,128)(2,1)S(1)} %get-tuple-element.92), channel_id=1, source_target_pairs={{0,24},{4,28},{8,0},{12,4},{16,8},{20,12},{24,16},{28,20},{32,56},... | collective-permute-start | bytes 835592 | tf_op jit(solution)/shard_map/ppermute | solution.py:611
  31.6 14.2 %collective-permute-start.9 = (bf16[256,512]{1,0:T(8,128)(2,1)S(1)}, bf16[256,512]{1,0:T(8,128)(2,1)S(1)}, u32[]{:S(2)}, u32[]{:S(2)}) collective-permute-start(bf16[256,512]{1,0:T(8,128)(2,1)S(1)} %get-tuple-element.103), channel_id=1, source_target_pairs={{0,8},{4,12},{8,16},{12,20},{16,24},{20,28},{24,0},{28,4},{32,40},... | collective-permute-start | bytes 786440 | tf_op jit(solution)/shard_map/ppermute | solution.py:611
  33.3 15.5 %collective-permute-start.10 = (bf16[256,512]{1,0:T(8,128)(2,1)S(1)}, bf16[256,512]{1,0:T(8,128)(2,1)S(1)}, u32[]{:S(2)}, u32[]{:S(2)}) collective-permute-start(bf16[256,512]{1,0:T(8,128)(2,1)S(1)} %get-tuple-element.104), channel_id=1, source_target_pairs={{0,16},{4,20},{8,24},{12,28},{16,0},{20,4},{24,8},{28,12},{32,48},... | collective-permute-start | bytes 786440 | tf_op jit(solution)/shard_map/ppermute | solution.py:611
  37.3 11.7 %collective-permute-start.11 = (bf16[256,512]{1,0:T(8,128)(2,1)S(1)}, bf16[256,512]{1,0:T(8,128)(2,1)S(1)}, u32[]{:S(2)}, u32[]{:S(2)}) collective-permute-start(bf16[256,512]{1,0:T(8,128)(2,1)S(1)} %get-tuple-element.105), channel_id=1, source_target_pairs={{0,24},{4,28},{8,0},{12,4},{16,8},{20,12},{24,16},{28,20},{32,56},... | collective-permute-start | bytes 786440 | tf_op jit(solution)/shard_map/ppermute | solution.py:611
  38.8 12.9 %collective-permute-start.16 = (bf16[256,512]{1,0:T(8,128)(2,1)S(1)}, bf16[256,512]{1,0:T(8,128)(2,1)S(1)}, u32[]{:S(2)}, u32[]{:S(2)}) collective-permute-start(bf16[256,512]{1,0:T(8,128)(2,1)S(1)} %edge_forward.1), channel_id=1, source_target_pairs={{0,32},{4,36},{8,40},{12,44},{16,48},{20,52},{24,56},{28,60},{1,33... | collective-permute-start | bytes 786440 | tf_op jit(solution)/shard_map/ppermute | solution.py:611
  49.2 8.1 %collective-permute-start.12 = (bf16[256,512]{1,0:T(8,128)(2,1)S(1)}, bf16[256,512]{1,0:T(8,128)(2,1)S(1)}, u32[]{:S(2)}, u32[]{:S(2)}) collective-permute-start(bf16[256,512]{1,0:T(8,128)(2,1)S(1)} %edge_back.1), channel_id=1, source_target_pairs={{32,0},{36,4},{40,8},{44,12},{48,16},{52,20},{56,24},{60,28},{33,1... | collective-permute-start | bytes 786440 | tf_op jit(solution)/shard_map/ppermute | solution.py:611
  52.7 11.1 %collective-permute-start.17 = (bf16[256,512]{1,0:T(8,128)(2,1)S(1)}, bf16[256,512]{1,0:T(8,128)(2,1)S(1)}, u32[]{:S(2)}, u32[]{:S(2)}) collective-permute-start(bf16[256,512]{1,0:T(8,128)(2,1)S(1)} %get-tuple-element.131), channel_id=1, source_target_pairs={{0,24},{4,28},{8,0},{12,4},{16,8},{20,12},{24,16},{28,20},{32,56},... | collective-permute-start | bytes 786440 | tf_op jit(solution)/shard_map/ppermute | solution.py:611
  56.6 13.0 %collective-permute-start.18 = (bf16[256,512]{1,0:T(8,128)(2,1)S(1)}, bf16[256,512]{1,0:T(8,128)(2,1)S(1)}, u32[]{:S(2)}, u32[]{:S(2)}) collective-permute-start(bf16[256,512]{1,0:T(8,128)(2,1)S(1)} %get-tuple-element.132), channel_id=1, source_target_pairs={{0,16},{4,20},{8,24},{12,28},{16,0},{20,4},{24,8},{28,12},{32,48},... | collective-permute-start | bytes 786440 | tf_op jit(solution)/shard_map/ppermute | solution.py:611
  56.6 13.0 %collective-permute-start.19 = (bf16[256,512]{1,0:T(8,128)(2,1)S(1)}, bf16[256,512]{1,0:T(8,128)(2,1)S(1)}, u32[]{:S(2)}, u32[]{:S(2)}) collective-permute-start(bf16[256,512]{1,0:T(8,128)(2,1)S(1)} %get-tuple-element.133), channel_id=1, source_target_pairs={{0,8},{4,12},{8,16},{12,20},{16,24},{20,28},{24,0},{28,4},{32,40},... | collective-permute-start | bytes 786440 | tf_op jit(solution)/shard_map/ppermute | solution.py:611
  58.3 16.5 %collective-permute-start.13 = (bf16[256,512]{1,0:T(8,128)(2,1)S(1)}, bf16[256,512]{1,0:T(8,128)(2,1)S(1)}, u32[]{:S(2)}, u32[]{:S(2)}) collective-permute-start(bf16[256,512]{1,0:T(8,128)(2,1)S(1)} %get-tuple-element.117), channel_id=1, source_target_pairs={{0,24},{4,28},{8,0},{12,4},{16,8},{20,12},{24,16},{28,20},{32,56},... | collective-permute-start | bytes 786440 | tf_op jit(solution)/shard_map/ppermute | solution.py:611
  60.3 14.5 %collective-permute-start.14 = (bf16[256,512]{1,0:T(8,128)(2,1)S(1)}, bf16[256,512]{1,0:T(8,128)(2,1)S(1)}, u32[]{:S(2)}, u32[]{:S(2)}) collective-permute-start(bf16[256,512]{1,0:T(8,128)(2,1)S(1)} %get-tuple-element.118), channel_id=1, source_target_pairs={{0,16},{4,20},{8,24},{12,28},{16,0},{20,4},{24,8},{28,12},{32,48},... | collective-permute-start | bytes 786440 | tf_op jit(solution)/shard_map/ppermute | solution.py:611
  63.7 14.7 %collective-permute-start.15 = (bf16[256,512]{1,0:T(8,128)(2,1)S(1)}, bf16[256,512]{1,0:T(8,128)(2,1)S(1)}, u32[]{:S(2)}, u32[]{:S(2)}) collective-permute-start(bf16[256,512]{1,0:T(8,128)(2,1)S(1)} %get-tuple-element.119), channel_id=1, source_target_pairs={{0,8},{4,12},{8,16},{12,20},{16,24},{20,28},{24,0},{28,4},{32,40},... | collective-permute-start | bytes 786440 | tf_op jit(solution)/shard_map/ppermute | solution.py:611
  79.0 7.4 %collective-permute-start.20 = (bf16[8,2560]{1,0:T(8,128)(2,1)S(1)}, bf16[8,2560]{1,0:T(8,128)(2,1)S(1)}, u32[]{:S(2)}, u32[]{:S(2)}) collective-permute-start(bf16[8,2560]{1,0:T(8,128)(2,1)S(1)} %head.1), channel_id=1, source_target_pairs={{8,0},{12,4},{16,8},{20,12},{24,16},{28,20},{32,24},{36,28},{40,32... | collective-permute-start | bytes 122888 | tf_op jit(solution)/shard_map/ppermute | solution.py:611
  87.9 5.6 %collective-permute-start.21 = (bf16[128,2688]{1,0:T(8,128)(2,1)S(1)}, bf16[128,2688]{1,0:T(8,128)(2,1)S(1)}, u32[]{:S(2)}, u32[]{:S(2)}) collective-permute-start(bf16[128,2688]{1,0:T(8,128)(2,1)S(1)} %get-tuple-element.151), channel_id=1, source_target_pairs={{0,4},{4,0},{8,12},{12,8},{16,20},{20,16},{24,28},{28,24},{32,36},... | collective-permute-start | bytes 2064392 | tf_op jit(solution)/shard_map/ppermute | solution.py:611
  (8 other events, 123.8 us)

commit v5 on v4

--- a/solution.py
+++ b/solution.py
@@ -170,8 +170,9 @@
 
 
 def first_kernel(
-    v, s, r, message, halo_a, halo_b, step_bias, decay_log, v_tap, v_off, s_tap, s_off, ones,
-    m0, m1, m2, m3, x_out, xs_out, bc_out, pre_out, spre_out, wide, delta_out, within_out, sig_out,
+    v, s, r, message, step_bias, decay_log, v_tap, v_off, s_tap, s_off, ones,
+    x_out, xs_out, bc_out, pre_out, spre_out, wide, delta_out, within_out, sig_out, top_out,
+    stop_out,
     buf, sbuf, raw,
 ):
     core, ring = place()
@@ -197,9 +198,10 @@
     buf[above, :] = message[:, :WIDE].astype(f32)
     sbuf[below, :] = s[:, s_mine].astype(f32)
     sbuf[above, :] = message[:, WIDE : WIDE + 2 * STATE].astype(f32)
-    halo = halo_a[...].astype(f32) + halo_b[...].astype(f32)
-    buf[0:8, :] = halo[:, :WIDE]
-    sbuf[0:8, :] = halo[:, WIDE:]
+    buf[0:8, :] = jnp.zeros((8, WIDE), f32)
+    sbuf[0:8, :] = jnp.zeros((8, 2 * STATE), f32)
+    top_out[...] = buf[8 : 8 + TAIL, :]
+    stop_out[...] = sbuf[8 : 8 + TAIL, :]
 
     def conv(source, tap, off, b, width):
         cols, par = block128(b), block128(b, core * width)
@@ -228,6 +230,35 @@
 
     lax.fori_loop(0, 16, value_block, 0)
 
+
+def state_kernel_body(
+    halo_a, halo_b, top, stop, wide, within, v_tap, v_off, s_tap, s_off, ones,
+    x_in, xs_in, bc_in, pre_in, spre_in,
+    m0, m1, m2, m3, x_out, xs_out, bc_out, pre_out, spre_out,
+):
+    core, ring = place()
+    halo = halo_a[...].astype(f32) + halo_b[...].astype(f32)
+
+    def first_rows(source, start, tap, off, c, width):
+        par = pl.ds(pl.multiple_of(core * width + c, 128), PART)
+        both = jnp.concatenate(
+            [halo[:, start + c : start + c + PART], source[:, c : c + PART]], axis=0
+        )
+        acc = off[:, par] + tap[0:1, par] * both[5 : 5 + TAIL]
+        for j in range(1, CONV):
+            acc = acc + tap[j : j + 1, par] * both[5 + j : 5 + j + TAIL]
+        return acc, (acc * sigmoid_by_tanh(acc)).astype(bf16)
+
+    for c in range(0, WIDE, PART):
+        cols = slice(c, c + PART)
+        acc, post = first_rows(top, 0, v_tap, v_off, c, WIDE)
+        pre_out[0:TAIL, cols] = acc
+        x_out[0:TAIL, cols] = post
+        xs_out[0:TAIL, cols] = (post.astype(f32) * wide[0:TAIL, cols]).astype(bf16)
+    acc, post = first_rows(stop, WIDE, s_tap, s_off, 0, 2 * STATE)
+    spre_out[0:TAIL, :] = acc
+    bc_out[0:TAIL, :] = post
+    total = within[ROWS - 1 : ROWS, :]
     write_t = bc_out[:, :STATE].astype(f32).T.astype(bf16)
     total_parts = split3(jnp.broadcast_to(total, (8, 128)))
     for slot, out in enumerate((m0, m1, m2, m3)):
@@ -580,7 +611,7 @@
     t_out[...] = jnp.concatenate([low, high], axis=0).astype(bf16)
 
 
-def call(kernel, args, outs, scratch=(), name=None, anywhere=(), cost=None):
+def call(kernel, args, outs, scratch=(), name=None, anywhere=(), cost=None, aliases={}):
     vmem = pl.BlockSpec(memory_space=pltpu.VMEM)
     args = [pltpu.with_memory_space_constraint(a, pltpu.HBM) if k in anywhere else a for k, a in enumerate(args)]
     return pl.pallas_call(
@@ -595,6 +626,7 @@
         cost_estimate=None
         if cost is None
         else pl.CostEstimate(flops=0, transcendentals=0, bytes_accessed=int(cost * 3.0e6)),
+        input_output_aliases=aliases,
         name=name,
     )(*args)
 
@@ -670,15 +702,24 @@
         [(p * count + i, (1 - p) * count + (i ^ 1)) for p in range(2) for i in range(count)],
     )
     ones = call(ones_kernel, [], [((128, WIDE), bf16)], name="ones")[0]
-    (m0, m1, m2, m3, x, xs, bc, pre, spre, spread_scale, delta, within, sig) = call(
+    taps = [value_kernel, row(value_offset), state_kernel, row(state_offset)]
+    half_done = [
+        (tall, bf16), (tall, bf16), ((ROWS, 2 * STATE), bf16), (tall, f32),
+        ((ROWS, 2 * STATE), f32),
+    ]
+    *begun, spread_scale, delta, within, sig, top, stop = call(
         first_kernel,
-        [v, s, r, message, halo_a, halo_b, bias, rate_log,
-         value_kernel, row(value_offset), state_kernel, row(state_offset), ones],
-        [marked] * 4 + [(tall, bf16)] * 2
-        + [((ROWS, 2 * STATE), bf16), (tall, f32), ((ROWS, 2 * STATE), f32), (tall, f32)]
-        + [(narrow, f32)] * 3,
+        [v, s, r, message, bias, rate_log] + taps + [ones],
+        half_done + [(tall, f32)] + [(narrow, f32)] * 3
+        + [((TAIL, WIDE), f32), ((TAIL, 2 * STATE), f32)],
         [((ROWS + 8, WIDE), f32), ((ROWS + 8, 2 * STATE), f32), (narrow, f32)],
         "first", cost=8,
+    )
+    m0, m1, m2, m3, x, xs, bc, pre, spre = call(
+        state_kernel_body,
+        [halo_a, halo_b, top, stop, spread_scale, within] + taps + [ones] + begun,
+        [marked] * 4 + half_done, (), "states", cost=2,
+        aliases={11 + j: 4 + j for j in range(5)},
     )
     marks = exchange((m0, m1, m2, m3), 1)
     sx, k, sbc = call(

time: 94.9 us -> 92.9 us (0.979)
  starting transfers between devices: 36.3 us -> 34 us
    ppermute x2, waiting for transfers between devices: 5.46 us -> 0.01 us  [onward(): return lax.ppermute(x, ('pipe', 'ctx'), pairs)]
    ppermute x17, waiting for transfers between devices: 15.2 us -> 18.1 us  [send(): return lax.ppermute(x, 'ctx', pairs)]
    ppermute x1, waiting for transfers between devices: 3.18 us -> 5.67 us  [local(): lax.ppermute(g_in, ('pipe', 'ctx'), [(p * count + i, (1 - p) * count + (i...]
    ppermute x17, starting transfers between devices: 29.1 us -> 26.8 us  [send(): return lax.ppermute(x, 'ctx', pairs)]
    pallas_call x18 -> x19, Pallas kernels: 33.5 us -> 33.7 us  [call(): pl.pallas_call(kernel, in_specs=[pl.BlockSpec(memory_space=pltpu.HBM) if...]
  transfers between devices with their start and end apart: 22 -> 22, of which waited for: 10 -> 7; matrix products, arithmetic and copies ran while one was open for 0% -> 0% of each run, Pallas kernels for 31% -> 32%
where the time goes in v5:
time: 92.9 us; the launch traced here: 92.6 us
  starting transfers between devices  34 us (37%)
  Pallas kernels  33.7 us (36%)
  waiting for transfers between devices  23.8 us (26%)
  between operations  1.02 us (1%)
    pallas_call x19, Pallas kernels, call(): pl.pallas_call(kernel, in_specs=[pl.BlockSpec(memory_space=pltpu.HBM) if...  33.7 us
    ppermute x17, starting transfers between devices, send(): return lax.ppermute(x, 'ctx', pairs)  26.8 us
    ppermute x17, waiting for transfers between devices, send(): return lax.ppermute(x, 'ctx', pairs)  18.1 us
    ppermute x1, waiting for transfers between devices, local(): lax.ppermute(g_in, ('pipe', 'ctx'), [(p * count + i, (1 - p) * count + (i...  5.67 us
    ppermute x2, starting transfers between devices, onward(): return lax.ppermute(x, ('pipe', 'ctx'), pairs)  4.83 us
  transfers between devices with their start and end apart: 22, of which 7 were waited for; matrix products, arithmetic and copies ran while one was open for 0% of the time, Pallas kernels for 32%

profile of v5, /device:TPU:15, one launch (start us, length us, event | category | flops | bytes accessed | tf_op | source)
XLA Modules:
  0.0 92.6 jit_solution(1087199720040113189)
XLA Ops:
  6.5 3.5 %collective-permute-start.1 = (bf16[8,2560]{1,0:T(8,128)(2,1)S(1)}, bf16[8,2560]{1,0:T(8,128)(2,1)S(1)}, u32[]{:S(2)}, u32[]{:S(2)}) collective-permute-start(bf16[8,2560]{1,0:T(8,128)(2,1)S(1)} %get-tuple-element.93), channel_id=1, source_target_pairs={{4,12},{12,20},{20,28},{92,36},{36,44},{44,52},{52,60},{68,76},{76... | collective-permute-start | bytes 122888 | tf_op jit(solution)/shard_map/ppermute | solution.py:690
  11.5 5.4 %first.1 = (bf16[256,2048]{1,0:T(8,128)(2,1)S(1)}, bf16[256,2048]{1,0:T(8,128)(2,1)S(1)}, bf16[256,512]{1,0:T(8,128)(2,1)S(1)}, f32[256,2048]{1,0:T(8,128)S(1)},...) custom-call(bf16[128,4096]{1,0:T(8,128)(2,1)S(1)} %bitcast.17, ...), custom_call_target="tpu_custom_call" | custom-call | bytes 24000000 | tf_op jit(solution)/shard_map/first/pallas_call | solution.py:617
  17.7 1.7 %collective-permute-start.4 = (bf16[272,512]{1,0:T(8,128)(2,1)S(1)}, bf16[272,512]{1,0:T(8,128)(2,1)S(1)}, u32[]{:S(2)}, u32[]{:S(2)}) collective-permute-start(bf16[272,512]{1,0:T(8,128)(2,1)S(1)} %get-tuple-element.106), channel_id=1, source_target_pairs={{0,8},{4,12},{8,16},{12,20},{16,24},{20,28},{24,0},{28,4},{32,40},... | collective-permute-start | bytes 835592 | tf_op jit(solution)/shard_map/ppermute | solution.py:643
  19.5 1.8 %collective-permute-start.5 = (bf16[272,512]{1,0:T(8,128)(2,1)S(1)}, bf16[272,512]{1,0:T(8,128)(2,1)S(1)}, u32[]{:S(2)}, u32[]{:S(2)}) collective-permute-start(bf16[272,512]{1,0:T(8,128)(2,1)S(1)} %get-tuple-element.107), channel_id=1, source_target_pairs={{0,16},{4,20},{8,24},{12,28},{16,0},{20,4},{24,8},{28,12},{32,48},... | collective-permute-start | bytes 835592 | tf_op jit(solution)/shard_map/ppermute | solution.py:643
  21.2 2.0 %collective-permute-start.6 = (bf16[272,512]{1,0:T(8,128)(2,1)S(1)}, bf16[272,512]{1,0:T(8,128)(2,1)S(1)}, u32[]{:S(2)}, u32[]{:S(2)}) collective-permute-start(bf16[272,512]{1,0:T(8,128)(2,1)S(1)} %get-tuple-element.108), channel_id=1, source_target_pairs={{0,24},{4,28},{8,0},{12,4},{16,8},{20,12},{24,16},{28,20},{32,56},... | collective-permute-start | bytes 835592 | tf_op jit(solution)/shard_map/ppermute | solution.py:643
  24.4 5.7 %collective-permute-done.8.g_in = bf16[128,2048]{1,0:T(8,128)(2,1)S(1)} collective-permute-done((bf16[128,2048]{1,0:T(8,128)(2,1)S(1)}, bf16[128,2048]{1,0:T(8,128)(2,1)S(1)}, u32[]{:S(2)}, u32[]{:S(2)}) %collective-permute-start.8) | collective-permute-done | bytes 524320 | tf_op jit(solution)/shard_map/ppermute | solution.py:699
  30.0 1.6 %second.1 = (bf16[256,512]{1,0:T(8,128)(2,1)S(1)}, bf16[256,512]{1,0:T(8,128)(2,1)S(1)}, bf16[256,512]{1,0:T(8,128)(2,1)S(1)}, bf16[256,512]{1,0:T(8,128)(2,1)S(...) custom-call(bf16[128,2048]{1,0:T(8,128)(2,1)S(1)} %collective-permute-done.7.g_own, ...), custom_call_target="tpu_custom_call" | custom-call | bytes 12000000 | tf_op jit(solution)/shard_map/second/pallas_call | solution.py:617
  31.6 1.7 %collective-permute-start.9 = (bf16[256,512]{1,0:T(8,128)(2,1)S(1)}, bf16[256,512]{1,0:T(8,128)(2,1)S(1)}, u32[]{:S(2)}, u32[]{:S(2)}) collective-permute-start(bf16[256,512]{1,0:T(8,128)(2,1)S(1)} %get-tuple-element.117), channel_id=1, source_target_pairs={{0,8},{4,12},{8,16},{12,20},{16,24},{20,28},{24,0},{28,4},{32,40},... | collective-permute-start | bytes 786440 | tf_op jit(solution)/shard_map/ppermute | solution.py:643
  33.3 3.3 %collective-permute-start.10 = (bf16[256,512]{1,0:T(8,128)(2,1)S(1)}, bf16[256,512]{1,0:T(8,128)(2,1)S(1)}, u32[]{:S(2)}, u32[]{:S(2)}) collective-permute-start(bf16[256,512]{1,0:T(8,128)(2,1)S(1)} %get-tuple-element.118), channel_id=1, source_target_pairs={{0,16},{4,20},{8,24},{12,28},{16,0},{20,4},{24,8},{28,12},{32,48},... | collective-permute-start | bytes 786440 | tf_op jit(solution)/shard_map/ppermute | solution.py:643
  39.0 5.7 %inner_0.1 = (f32[256,1024]{1,0:T(8,128)S(1)}, f32[256,256]{1,0:T(8,128)S(1)}, f32[256,128]{1,0:T(8,128)S(1)}, f32[256,128]{1,0:T(8,128)S(1)}) custom-call(bf16[256,2048]{1,0:T(8,128)(2,1)S(1)} %get-tuple-element.120.x, bf16[256,2048]{1,0:T(8,128)(2,1)S(1)} %get-tuple-element.136.dy, bf16[256,512]{1,0:T(8,128)(2,1)S(1)} %get-tuple-element.115.bc, ...), custom_call_target="tpu_custom_call" | custom-call | bytes 18000000 | tf_op jit(solution)/shard_map/inner_0/pallas_call | solution.py:617
  44.7 4.0 %collective-permute-done.10.d2 = bf16[256,512]{1,0:T(8,128)(2,1)S(1)} collective-permute-done((bf16[256,512]{1,0:T(8,128)(2,1)S(1)}, bf16[256,512]{1,0:T(8,128)(2,1)S(1)}, u32[]{:S(2)}, u32[]{:S(2)}) %collective-permute-start.10) | collective-permute-done | bytes 262176 | tf_op jit(solution)/shard_map/ppermute | solution.py:643
  49.0 1.5 %collective-permute-start.12 = (bf16[256,512]{1,0:T(8,128)(2,1)S(1)}, bf16[256,512]{1,0:T(8,128)(2,1)S(1)}, u32[]{:S(2)}, u32[]{:S(2)}) collective-permute-start(bf16[256,512]{1,0:T(8,128)(2,1)S(1)} %edge_back.1), channel_id=1, source_target_pairs={{32,0},{36,4},{40,8},{44,12},{48,16},{52,20},{56,24},{60,28},{33,1... | collective-permute-start | bytes 786440 | tf_op jit(solution)/shard_map/ppermute | solution.py:643
  51.5 3.5 %collective-permute-start.17 = (bf16[256,512]{1,0:T(8,128)(2,1)S(1)}, bf16[256,512]{1,0:T(8,128)(2,1)S(1)}, u32[]{:S(2)}, u32[]{:S(2)}) collective-permute-start(bf16[256,512]{1,0:T(8,128)(2,1)S(1)} %get-tuple-element.145), channel_id=1, source_target_pairs={{0,24},{4,28},{8,0},{12,4},{16,8},{20,12},{24,16},{28,20},{32,56},... | collective-permute-start | bytes 786440 | tf_op jit(solution)/shard_map/ppermute | solution.py:643
  56.6 3.7 %collective-permute-start.13 = (bf16[256,512]{1,0:T(8,128)(2,1)S(1)}, bf16[256,512]{1,0:T(8,128)(2,1)S(1)}, u32[]{:S(2)}, u32[]{:S(2)}) collective-permute-start(bf16[256,512]{1,0:T(8,128)(2,1)S(1)} %get-tuple-element.131), channel_id=1, source_target_pairs={{0,24},{4,28},{8,0},{12,4},{16,8},{20,12},{24,16},{28,20},{32,56},... | collective-permute-start | bytes 786440 | tf_op jit(solution)/shard_map/ppermute | solution.py:643
  60.6 3.2 %collective-permute-done.17.c1 = bf16[256,512]{1,0:T(8,128)(2,1)S(1)} collective-permute-done((bf16[256,512]{1,0:T(8,128)(2,1)S(1)}, bf16[256,512]{1,0:T(8,128)(2,1)S(1)}, u32[]{:S(2)}, u32[]{:S(2)}) %collective-permute-start.17) | collective-permute-done | bytes 262176 | tf_op jit(solution)/shard_map/ppermute | solution.py:643
  63.8 5.9 %inner_1.1 = (f32[256,1024]{1,0:T(8,128)S(1)}, f32[256,512]{1,0:T(8,128)S(1)}, f32[256,128]{1,0:T(8,128)S(1)}, f32[256,128]{1,0:T(8,128)S(1)}, f32[8,2048]{1,0:T(8,128)S(1)}) custom-call(bf16[256,2048]{1,0:T(8,128)(2,1)S(1)} %get-tuple-element.120.x, bf16[256,2048]{1,0:T(8,128)(2,1)S(1)} %get-tuple-element.136.dy, ...), custom_call_target="tpu_custom_call" | custom-call | bytes 18000000 | tf_op jit(solution)/shard_map/inner_1/pallas_call | solution.py:617
  70.4 2.1 %carry.1 = (f32[256,128]{1,0:T(8,128)S(1)}, f32[256,256]{1,0:T(8,128)S(1)}, bf16[256,2048]{1,0:T(8,128)(2,1)S(1)}) custom-call(bf16[256,512]{1,0:T(8,128)(2,1)S(1)} %get-tuple-element.144.c0, bf16[256,512]{1,0:T(8,128)(2,1)S(1)} %collective-permute-done.17.c1, bf16[256,512]{1,0:T(8,128)(2,1)S(1)} %collective-permute-done.18.c2, ...), custom_call_target="tpu_custom_call" | custom-call | bytes 12000000 | tf_op jit(solution)/shard_map/carry/pallas_call | solution.py:617
  72.5 4.3 %collective-permute-done.13.g1 = bf16[256,512]{1,0:T(8,128)(2,1)S(1)} collective-permute-done((bf16[256,512]{1,0:T(8,128)(2,1)S(1)}, bf16[256,512]{1,0:T(8,128)(2,1)S(1)}, u32[]{:S(2)}, u32[]{:S(2)}) %collective-permute-start.13) | collective-permute-done | bytes 262176 | tf_op jit(solution)/shard_map/ppermute | solution.py:643
  76.9 4.0 %collective-permute-done.15.g3 = bf16[256,512]{1,0:T(8,128)(2,1)S(1)} collective-permute-done((bf16[256,512]{1,0:T(8,128)(2,1)S(1)}, bf16[256,512]{1,0:T(8,128)(2,1)S(1)}, u32[]{:S(2)}, u32[]{:S(2)}) %collective-permute-start.15) | collective-permute-done | bytes 262176 | tf_op jit(solution)/shard_map/ppermute | solution.py:643
  81.4 1.9 %collective-permute-start.20 = (bf16[8,2560]{1,0:T(8,128)(2,1)S(1)}, bf16[8,2560]{1,0:T(8,128)(2,1)S(1)}, u32[]{:S(2)}, u32[]{:S(2)}) collective-permute-start(bf16[8,2560]{1,0:T(8,128)(2,1)S(1)} %head.1), channel_id=1, source_target_pairs={{8,0},{12,4},{16,8},{20,12},{24,16},{28,20},{32,24},{36,28},{40,32... | collective-permute-start | bytes 122888 | tf_op jit(solution)/shard_map/ppermute | solution.py:643
  83.4 2.9 %last.1 = (f32[256,2048]{1,0:T(8,128)S(1)}, f32[256,512]{1,0:T(8,128)S(1)}, f32[256,128]{1,0:T(8,128)S(1)}) custom-call(bf16[256,512]{1,0:T(8,128)(2,1)S(1)} %get-tuple-element.152.g0, bf16[256,512]{1,0:T(8,128)(2,1)S(1)} %collective-permute-done.13.g1, bf16[256,512]{1,0:T(8,128)(2,1)S(1)} %collective-permute-done.14.g2, ...), custom_call_target="tpu_custom_call" | custom-call | bytes 15000000 | tf_op jit(solution)/shard_map/last/pallas_call | solution.py:617
  86.2 1.5 %back.1 = (bf16[128,2048]{1,0:T(8,128)(2,1)S(1)}, bf16[128,512]{1,0:T(8,128)(2,1)S(1)}, bf16[128,128]{1,0:T(8,128)(2,1)S(1)}, bf16[128,2688]{1,0:T(8,128)(2,1)S(1)}) custom-call(f32[256,2048]{1,0:T(8,128)S(1)} %get-tuple-element.158.e, f32[256,512]{1,0:T(8,128)S(1)} %get-tuple-element.159.es, f32[256,128]{1,0:T(8,128)S(1)} %get-tuple-element.160.steps, ...), custom_call_target="tpu_custom_call" | custom-call | bytes 9000000 | tf_op jit(solution)/shard_map/back/pallas_call | solution.py:617
  87.8 2.0 %collective-permute-start.21 = (bf16[128,2688]{1,0:T(8,128)(2,1)S(1)}, bf16[128,2688]{1,0:T(8,128)(2,1)S(1)}, u32[]{:S(2)}, u32[]{:S(2)}) collective-permute-start(bf16[128,2688]{1,0:T(8,128)(2,1)S(1)} %get-tuple-element.165), channel_id=1, source_target_pairs={{0,4},{4,0},{8,12},{12,8},{16,20},{20,16},{24,28},{28,24},{32,36},... | collective-permute-start | bytes 2064392 | tf_op jit(solution)/shard_map/ppermute | solution.py:643
  89.7 1.8 %collective-permute-done.21.message = bf16[128,2688]{1,0:T(8,128)(2,1)S(1)} collective-permute-done((bf16[128,2688]{1,0:T(8,128)(2,1)S(1)}, bf16[128,2688]{1,0:T(8,128)(2,1)S(1)}, u32[]{:S(2)}, u32[]{:S(2)}) %collective-permute-start.21) | collective-permute-done | bytes 688160 | tf_op jit(solution)/shard_map/ppermute | solution.py:643
  (59 shorter events, 17.0 us)
Async XLA Ops:
  0.6 10.8 %copy-start.5 = (bf16[1,128,64]{1,2,0:T(8,128)(2,1)S(1)}, bf16[1,128,64]{1,2,0:T(8,128)(2,1)}, u32[]{:S(2)}) copy-start(bf16[1,128,64]{1,2,0:T(8,128)(2,1)} %param.13) | copy-start | bytes 49156
  0.6 10.8 %copy-start.1 = (bf16[1,128,1024]{2,1,0:T(8,128)(2,1)S(1)}, bf16[1,128,1024]{2,1,0:T(8,128)(2,1)}, u32[]{:S(2)}) copy-start(bf16[1,128,1024]{2,1,0:T(8,128)(2,1)} %param.12) | copy-start | bytes 786436
  2.1 9.3 %collective-permute-start.3 = (bf16[128,2688]{1,0:T(8,128)(2,1)S(1)}, bf16[128,2688]{1,0:T(8,128)(2,1)S(1)}, u32[]{:S(2)}, u32[]{:S(2)}) collective-permute-start(bf16[128,2688]{1,0:T(8,128)(2,1)S(1)} %get-tuple-element.95), channel_id=1, source_target_pairs={{0,4},{4,0},{8,12},{12,8},{16,20},{20,16},{24,28},{28,24},{32,36},... | collective-permute-start | bytes 2064392 | tf_op jit(solution)/shard_map/ppermute | solution.py:643
  2.8 1.9 %collective-permute-start = (bf16[16,2560]{1,0:T(8,128)(2,1)S(1)}, bf16[16,2560]{1,0:T(8,128)(2,1)S(1)}, u32[]{:S(2)}, u32[]{:S(2)}) collective-permute-start(bf16[16,2560]{1,0:T(8,128)(2,1)S(1)} %get-tuple-element.90), channel_id=1, source_target_pairs={{28,92},{92,28},{29,93},{93,29},{30,94},{94,30},{31,95},{95,31}} | collective-permute-start | bytes 245768 | tf_op jit(solution)/shard_map/ppermute | solution.py:674
  4.8 19.6 %collective-permute-start.7 = (bf16[128,2048]{1,0:T(8,128)(2,1)S(1)}, bf16[128,2048]{1,0:T(8,128)(2,1)S(1)}, u32[]{:S(2)}, u32[]{:S(2)}) collective-permute-start(bf16[128,2048]{1,0:T(8,128)(2,1)S(1)} %get-tuple-element.109), channel_id=1, source_target_pairs={{0,64},{64,0},{1,65},{65,1},{2,66},{66,2},{3,67},{67,3},{4,68},{68... | collective-permute-start | bytes 1572872 | tf_op jit(solution)/shard_map/ppermute | solution.py:698
  5.4 24.6 %collective-permute-start.8 = (bf16[128,2048]{1,0:T(8,128)(2,1)S(1)}, bf16[128,2048]{1,0:T(8,128)(2,1)S(1)}, u32[]{:S(2)}, u32[]{:S(2)}) collective-permute-start(bf16[128,2048]{1,0:T(8,128)(2,1)S(1)} %get-tuple-element.114), channel_id=1, source_target_pairs={{0,68},{4,64},{8,76},{12,72},{16,84},{20,80},{24,92},{28,88},{32,1... | collective-permute-start | bytes 1572872 | tf_op jit(solution)/shard_map/ppermute | solution.py:699
  6.5 10.4 %collective-permute-start.1 = (bf16[8,2560]{1,0:T(8,128)(2,1)S(1)}, bf16[8,2560]{1,0:T(8,128)(2,1)S(1)}, u32[]{:S(2)}, u32[]{:S(2)}) collective-permute-start(bf16[8,2560]{1,0:T(8,128)(2,1)S(1)} %get-tuple-element.93), channel_id=1, source_target_pairs={{4,12},{12,20},{20,28},{92,36},{36,44},{44,52},{52,60},{68,76},{76... | collective-permute-start | bytes 122888 | tf_op jit(solution)/shard_map/ppermute | solution.py:690
  10.1 6.8 %collective-permute-start.2 = (bf16[8,2560]{1,0:T(8,128)(2,1)S(1)}, bf16[8,2560]{1,0:T(8,128)(2,1)S(1)}, u32[]{:S(2)}, u32[]{:S(2)}) collective-permute-start(bf16[8,2560]{1,0:T(8,128)(2,1)S(1)} %get-tuple-element.94), channel_id=1, source_target_pairs={{4,8},{12,16},{20,24},{92,32},{36,40},{44,48},{52,56},{68,72},{76,... | collective-permute-start | bytes 122888 | tf_op jit(solution)/shard_map/ppermute | solution.py:690
  17.7 18.9 %collective-permute-start.4 = (bf16[272,512]{1,0:T(8,128)(2,1)S(1)}, bf16[272,512]{1,0:T(8,128)(2,1)S(1)}, u32[]{:S(2)}, u32[]{:S(2)}) collective-permute-start(bf16[272,512]{1,0:T(8,128)(2,1)S(1)} %get-tuple-element.106), channel_id=1, source_target_pairs={{0,8},{4,12},{8,16},{12,20},{16,24},{20,28},{24,0},{28,4},{32,40},... | collective-permute-start | bytes 835592 | tf_op jit(solution)/shard_map/ppermute | solution.py:643
  19.5 17.9 %collective-permute-start.5 = (bf16[272,512]{1,0:T(8,128)(2,1)S(1)}, bf16[272,512]{1,0:T(8,128)(2,1)S(1)}, u32[]{:S(2)}, u32[]{:S(2)}) collective-permute-start(bf16[272,512]{1,0:T(8,128)(2,1)S(1)} %get-tuple-element.107), channel_id=1, source_target_pairs={{0,16},{4,20},{8,24},{12,28},{16,0},{20,4},{24,8},{28,12},{32,48},... | collective-permute-start | bytes 835592 | tf_op jit(solution)/shard_map/ppermute | solution.py:643
  21.2 16.2 %collective-permute-start.6 = (bf16[272,512]{1,0:T(8,128)(2,1)S(1)}, bf16[272,512]{1,0:T(8,128)(2,1)S(1)}, u32[]{:S(2)}, u32[]{:S(2)}) collective-permute-start(bf16[272,512]{1,0:T(8,128)(2,1)S(1)} %get-tuple-element.108), channel_id=1, source_target_pairs={{0,24},{4,28},{8,0},{12,4},{16,8},{20,12},{24,16},{28,20},{32,56},... | collective-permute-start | bytes 835592 | tf_op jit(solution)/shard_map/ppermute | solution.py:643
  31.6 13.1 %collective-permute-start.9 = (bf16[256,512]{1,0:T(8,128)(2,1)S(1)}, bf16[256,512]{1,0:T(8,128)(2,1)S(1)}, u32[]{:S(2)}, u32[]{:S(2)}) collective-permute-start(bf16[256,512]{1,0:T(8,128)(2,1)S(1)} %get-tuple-element.117), channel_id=1, source_target_pairs={{0,8},{4,12},{8,16},{12,20},{16,24},{20,28},{24,0},{28,4},{32,40},... | collective-permute-start | bytes 786440 | tf_op jit(solution)/shard_map/ppermute | solution.py:643
  33.3 15.4 %collective-permute-start.10 = (bf16[256,512]{1,0:T(8,128)(2,1)S(1)}, bf16[256,512]{1,0:T(8,128)(2,1)S(1)}, u32[]{:S(2)}, u32[]{:S(2)}) collective-permute-start(bf16[256,512]{1,0:T(8,128)(2,1)S(1)} %get-tuple-element.118), channel_id=1, source_target_pairs={{0,16},{4,20},{8,24},{12,28},{16,0},{20,4},{24,8},{28,12},{32,48},... | collective-permute-start | bytes 786440 | tf_op jit(solution)/shard_map/ppermute | solution.py:643
  36.6 12.1 %collective-permute-start.11 = (bf16[256,512]{1,0:T(8,128)(2,1)S(1)}, bf16[256,512]{1,0:T(8,128)(2,1)S(1)}, u32[]{:S(2)}, u32[]{:S(2)}) collective-permute-start(bf16[256,512]{1,0:T(8,128)(2,1)S(1)} %get-tuple-element.119), channel_id=1, source_target_pairs={{0,24},{4,28},{8,0},{12,4},{16,8},{20,12},{24,16},{28,20},{32,56},... | collective-permute-start | bytes 786440 | tf_op jit(solution)/shard_map/ppermute | solution.py:643
  37.7 12.9 %collective-permute-start.16 = (bf16[256,512]{1,0:T(8,128)(2,1)S(1)}, bf16[256,512]{1,0:T(8,128)(2,1)S(1)}, u32[]{:S(2)}, u32[]{:S(2)}) collective-permute-start(bf16[256,512]{1,0:T(8,128)(2,1)S(1)} %edge_forward.1), channel_id=1, source_target_pairs={{0,32},{4,36},{8,40},{12,44},{16,48},{20,52},{24,56},{28,60},{1,33... | collective-permute-start | bytes 786440 | tf_op jit(solution)/shard_map/ppermute | solution.py:643
  49.0 6.6 %collective-permute-start.12 = (bf16[256,512]{1,0:T(8,128)(2,1)S(1)}, bf16[256,512]{1,0:T(8,128)(2,1)S(1)}, u32[]{:S(2)}, u32[]{:S(2)}) collective-permute-start(bf16[256,512]{1,0:T(8,128)(2,1)S(1)} %edge_back.1), channel_id=1, source_target_pairs={{32,0},{36,4},{40,8},{44,12},{48,16},{52,20},{56,24},{60,28},{33,1... | collective-permute-start | bytes 786440 | tf_op jit(solution)/shard_map/ppermute | solution.py:643
  51.5 12.3 %collective-permute-start.17 = (bf16[256,512]{1,0:T(8,128)(2,1)S(1)}, bf16[256,512]{1,0:T(8,128)(2,1)S(1)}, u32[]{:S(2)}, u32[]{:S(2)}) collective-permute-start(bf16[256,512]{1,0:T(8,128)(2,1)S(1)} %get-tuple-element.145), channel_id=1, source_target_pairs={{0,24},{4,28},{8,0},{12,4},{16,8},{20,12},{24,16},{28,20},{32,56},... | collective-permute-start | bytes 786440 | tf_op jit(solution)/shard_map/ppermute | solution.py:643
  55.0 14.7 %collective-permute-start.18 = (bf16[256,512]{1,0:T(8,128)(2,1)S(1)}, bf16[256,512]{1,0:T(8,128)(2,1)S(1)}, u32[]{:S(2)}, u32[]{:S(2)}) collective-permute-start(bf16[256,512]{1,0:T(8,128)(2,1)S(1)} %get-tuple-element.146), channel_id=1, source_target_pairs={{0,16},{4,20},{8,24},{12,28},{16,0},{20,4},{24,8},{28,12},{32,48},... | collective-permute-start | bytes 786440 | tf_op jit(solution)/shard_map/ppermute | solution.py:643
  55.0 15.4 %collective-permute-start.19 = (bf16[256,512]{1,0:T(8,128)(2,1)S(1)}, bf16[256,512]{1,0:T(8,128)(2,1)S(1)}, u32[]{:S(2)}, u32[]{:S(2)}) collective-permute-start(bf16[256,512]{1,0:T(8,128)(2,1)S(1)} %get-tuple-element.147), channel_id=1, source_target_pairs={{0,8},{4,12},{8,16},{12,20},{16,24},{20,28},{24,0},{28,4},{32,40},... | collective-permute-start | bytes 786440 | tf_op jit(solution)/shard_map/ppermute | solution.py:643
  56.6 20.3 %collective-permute-start.13 = (bf16[256,512]{1,0:T(8,128)(2,1)S(1)}, bf16[256,512]{1,0:T(8,128)(2,1)S(1)}, u32[]{:S(2)}, u32[]{:S(2)}) collective-permute-start(bf16[256,512]{1,0:T(8,128)(2,1)S(1)} %get-tuple-element.131), channel_id=1, source_target_pairs={{0,24},{4,28},{8,0},{12,4},{16,8},{20,12},{24,16},{28,20},{32,56},... | collective-permute-start | bytes 786440 | tf_op jit(solution)/shard_map/ppermute | solution.py:643
  60.3 16.6 %collective-permute-start.14 = (bf16[256,512]{1,0:T(8,128)(2,1)S(1)}, bf16[256,512]{1,0:T(8,128)(2,1)S(1)}, u32[]{:S(2)}, u32[]{:S(2)}) collective-permute-start(bf16[256,512]{1,0:T(8,128)(2,1)S(1)} %get-tuple-element.132), channel_id=1, source_target_pairs={{0,16},{4,20},{8,24},{12,28},{16,0},{20,4},{24,8},{28,12},{32,48},... | collective-permute-start | bytes 786440 | tf_op jit(solution)/shard_map/ppermute | solution.py:643
  63.8 17.2 %collective-permute-start.15 = (bf16[256,512]{1,0:T(8,128)(2,1)S(1)}, bf16[256,512]{1,0:T(8,128)(2,1)S(1)}, u32[]{:S(2)}, u32[]{:S(2)}) collective-permute-start(bf16[256,512]{1,0:T(8,128)(2,1)S(1)} %get-tuple-element.133), channel_id=1, source_target_pairs={{0,8},{4,12},{8,16},{12,20},{16,24},{20,28},{24,0},{28,4},{32,40},... | collective-permute-start | bytes 786440 | tf_op jit(solution)/shard_map/ppermute | solution.py:643
  81.4 4.8 %collective-permute-start.20 = (bf16[8,2560]{1,0:T(8,128)(2,1)S(1)}, bf16[8,2560]{1,0:T(8,128)(2,1)S(1)}, u32[]{:S(2)}, u32[]{:S(2)}) collective-permute-start(bf16[8,2560]{1,0:T(8,128)(2,1)S(1)} %head.1), channel_id=1, source_target_pairs={{8,0},{12,4},{16,8},{20,12},{24,16},{28,20},{32,24},{36,28},{40,32... | collective-permute-start | bytes 122888 | tf_op jit(solution)/shard_map/ppermute | solution.py:643
  87.8 3.8 %collective-permute-start.21 = (bf16[128,2688]{1,0:T(8,128)(2,1)S(1)}, bf16[128,2688]{1,0:T(8,128)(2,1)S(1)}, u32[]{:S(2)}, u32[]{:S(2)}) collective-permute-start(bf16[128,2688]{1,0:T(8,128)(2,1)S(1)} %get-tuple-element.165), channel_id=1, source_target_pairs={{0,4},{4,0},{8,12},{12,8},{16,20},{20,16},{24,28},{28,24},{32,36},... | collective-permute-start | bytes 2064392 | tf_op jit(solution)/shard_map/ppermute | solution.py:643
  (8 other events, 84.4 us)

commit v6 on v5

--- a/solution.py
+++ b/solution.py
@@ -499,7 +499,8 @@
         cols = slice(b * PART, (b + 1) * PART)
         part = nn(read, carried_out[:, cols]) * dye[:, cols].astype(f32)
         outer = outer + head_sum(part, ones[:, cols])
-    diff_out[...] = outer
+    later = jnp.where(iota((ROWS, ROWS), 1) >= iota((ROWS, ROWS), 0), 1.0, 0.0).astype(f32)
+    diff_out[...] = nn(later, outer, HIGH)
 
 
 def last_kernel(
@@ -528,9 +529,8 @@
     total = within[ROWS - 1 : ROWS, :]
     dtotal = tsum[0:1, :] * jnp.exp(total)
     ra, rb = iota((ROWS, ROWS), 0), iota((ROWS, ROWS), 1)
-    later = jnp.where(rb >= ra, 1.0, 0.0).astype(f32)
     earlier = jnp.where(rb < ra, 1.0, 0.0).astype(f32)
-    da = nn(later, diff[...], HIGH) + nn(earlier, rsum, HIGH) + dtotal
+    da = diff[...] + nn(earlier, rsum, HIGH) + dtotal
     rate = -jnp.exp(tiled_heads(decay_log[...], core))
     steps_out[...] = (vsum[...] + rsum / delta[...] + rate * da) * sig[...]
     dwrite = dbc[:, :STATE] + nt(xs[...], gbuf[...])

time: 92.9 us -> 92.9 us (level)
  transfers between devices with their start and end apart: 22 -> 22, of which waited for: 7 -> 8; matrix products, arithmetic and copies ran while one was open for 0% -> 0% of each run, Pallas kernels for 32% -> 31%
where the time goes in v6:
time: 92.9 us; the launch traced here: 92.6 us
  starting transfers between devices  34.1 us (37%)
  Pallas kernels  33.5 us (36%)
  waiting for transfers between devices  23.9 us (26%)
  between operations  1.02 us (1%)
    pallas_call x19, Pallas kernels, call(): pl.pallas_call(kernel, in_specs=[pl.BlockSpec(memory_space=pltpu.HBM) if...  33.5 us
    ppermute x17, starting transfers between devices, send(): return lax.ppermute(x, 'ctx', pairs)  26.9 us
    ppermute x17, waiting for transfers between devices, send(): return lax.ppermute(x, 'ctx', pairs)  18.2 us
    ppermute x1, waiting for transfers between devices, local(): lax.ppermute(g_in, ('pipe', 'ctx'), [(p * count + i, (1 - p) * count + (i...  5.67 us
    ppermute x2, starting transfers between devices, onward(): return lax.ppermute(x, ('pipe', 'ctx'), pairs)  4.83 us
  transfers between devices with their start and end apart: 22, of which 8 were waited for; matrix products, arithmetic and copies ran while one was open for 0% of the time, Pallas kernels for 31%

profile of v6, /device:TPU:15, one launch (start us, length us, event | category | flops | bytes accessed | tf_op | source)
XLA Modules:
  0.0 92.6 jit_solution(10527818023984434764)
XLA Ops:
  6.5 3.5 %collective-permute-start.1 = (bf16[8,2560]{1,0:T(8,128)(2,1)S(1)}, bf16[8,2560]{1,0:T(8,128)(2,1)S(1)}, u32[]{:S(2)}, u32[]{:S(2)}) collective-permute-start(bf16[8,2560]{1,0:T(8,128)(2,1)S(1)} %get-tuple-element.93), channel_id=1, source_target_pairs={{4,12},{12,20},{20,28},{92,36},{36,44},{44,52},{52,60},{68,76},{76... | collective-permute-start | bytes 122888 | tf_op jit(solution)/shard_map/ppermute | solution.py:690
  11.5 5.4 %first.1 = (bf16[256,2048]{1,0:T(8,128)(2,1)S(1)}, bf16[256,2048]{1,0:T(8,128)(2,1)S(1)}, bf16[256,512]{1,0:T(8,128)(2,1)S(1)}, f32[256,2048]{1,0:T(8,128)S(1)},...) custom-call(bf16[128,4096]{1,0:T(8,128)(2,1)S(1)} %bitcast.17, ...), custom_call_target="tpu_custom_call" | custom-call | bytes 24000000 | tf_op jit(solution)/shard_map/first/pallas_call | solution.py:617
  17.7 1.7 %collective-permute-start.4 = (bf16[272,512]{1,0:T(8,128)(2,1)S(1)}, bf16[272,512]{1,0:T(8,128)(2,1)S(1)}, u32[]{:S(2)}, u32[]{:S(2)}) collective-permute-start(bf16[272,512]{1,0:T(8,128)(2,1)S(1)} %get-tuple-element.106), channel_id=1, source_target_pairs={{0,8},{4,12},{8,16},{12,20},{16,24},{20,28},{24,0},{28,4},{32,40},... | collective-permute-start | bytes 835592 | tf_op jit(solution)/shard_map/ppermute | solution.py:643
  19.5 1.8 %collective-permute-start.5 = (bf16[272,512]{1,0:T(8,128)(2,1)S(1)}, bf16[272,512]{1,0:T(8,128)(2,1)S(1)}, u32[]{:S(2)}, u32[]{:S(2)}) collective-permute-start(bf16[272,512]{1,0:T(8,128)(2,1)S(1)} %get-tuple-element.107), channel_id=1, source_target_pairs={{0,16},{4,20},{8,24},{12,28},{16,0},{20,4},{24,8},{28,12},{32,48},... | collective-permute-start | bytes 835592 | tf_op jit(solution)/shard_map/ppermute | solution.py:643
  21.2 2.0 %collective-permute-start.6 = (bf16[272,512]{1,0:T(8,128)(2,1)S(1)}, bf16[272,512]{1,0:T(8,128)(2,1)S(1)}, u32[]{:S(2)}, u32[]{:S(2)}) collective-permute-start(bf16[272,512]{1,0:T(8,128)(2,1)S(1)} %get-tuple-element.108), channel_id=1, source_target_pairs={{0,24},{4,28},{8,0},{12,4},{16,8},{20,12},{24,16},{28,20},{32,56},... | collective-permute-start | bytes 835592 | tf_op jit(solution)/shard_map/ppermute | solution.py:643
  24.4 5.7 %collective-permute-done.8.g_in = bf16[128,2048]{1,0:T(8,128)(2,1)S(1)} collective-permute-done((bf16[128,2048]{1,0:T(8,128)(2,1)S(1)}, bf16[128,2048]{1,0:T(8,128)(2,1)S(1)}, u32[]{:S(2)}, u32[]{:S(2)}) %collective-permute-start.8) | collective-permute-done | bytes 524320 | tf_op jit(solution)/shard_map/ppermute | solution.py:699
  30.0 1.6 %second.1 = (bf16[256,512]{1,0:T(8,128)(2,1)S(1)}, bf16[256,512]{1,0:T(8,128)(2,1)S(1)}, bf16[256,512]{1,0:T(8,128)(2,1)S(1)}, bf16[256,512]{1,0:T(8,128)(2,1)S(...) custom-call(bf16[128,2048]{1,0:T(8,128)(2,1)S(1)} %collective-permute-done.7.g_own, ...), custom_call_target="tpu_custom_call" | custom-call | bytes 12000000 | tf_op jit(solution)/shard_map/second/pallas_call | solution.py:617
  31.6 1.7 %collective-permute-start.9 = (bf16[256,512]{1,0:T(8,128)(2,1)S(1)}, bf16[256,512]{1,0:T(8,128)(2,1)S(1)}, u32[]{:S(2)}, u32[]{:S(2)}) collective-permute-start(bf16[256,512]{1,0:T(8,128)(2,1)S(1)} %get-tuple-element.117), channel_id=1, source_target_pairs={{0,8},{4,12},{8,16},{12,20},{16,24},{20,28},{24,0},{28,4},{32,40},... | collective-permute-start | bytes 786440 | tf_op jit(solution)/shard_map/ppermute | solution.py:643
  33.3 3.3 %collective-permute-start.10 = (bf16[256,512]{1,0:T(8,128)(2,1)S(1)}, bf16[256,512]{1,0:T(8,128)(2,1)S(1)}, u32[]{:S(2)}, u32[]{:S(2)}) collective-permute-start(bf16[256,512]{1,0:T(8,128)(2,1)S(1)} %get-tuple-element.118), channel_id=1, source_target_pairs={{0,16},{4,20},{8,24},{12,28},{16,0},{20,4},{24,8},{28,12},{32,48},... | collective-permute-start | bytes 786440 | tf_op jit(solution)/shard_map/ppermute | solution.py:643
  39.0 5.7 %inner_0.1 = (f32[256,1024]{1,0:T(8,128)S(1)}, f32[256,256]{1,0:T(8,128)S(1)}, f32[256,128]{1,0:T(8,128)S(1)}, f32[256,128]{1,0:T(8,128)S(1)}) custom-call(bf16[256,2048]{1,0:T(8,128)(2,1)S(1)} %get-tuple-element.120.x, bf16[256,2048]{1,0:T(8,128)(2,1)S(1)} %get-tuple-element.136.dy, bf16[256,512]{1,0:T(8,128)(2,1)S(1)} %get-tuple-element.115.bc, ...), custom_call_target="tpu_custom_call" | custom-call | bytes 18000000 | tf_op jit(solution)/shard_map/inner_0/pallas_call | solution.py:617
  44.7 4.0 %collective-permute-done.10.d2 = bf16[256,512]{1,0:T(8,128)(2,1)S(1)} collective-permute-done((bf16[256,512]{1,0:T(8,128)(2,1)S(1)}, bf16[256,512]{1,0:T(8,128)(2,1)S(1)}, u32[]{:S(2)}, u32[]{:S(2)}) %collective-permute-start.10) | collective-permute-done | bytes 262176 | tf_op jit(solution)/shard_map/ppermute | solution.py:643
  49.0 1.5 %collective-permute-start.12 = (bf16[256,512]{1,0:T(8,128)(2,1)S(1)}, bf16[256,512]{1,0:T(8,128)(2,1)S(1)}, u32[]{:S(2)}, u32[]{:S(2)}) collective-permute-start(bf16[256,512]{1,0:T(8,128)(2,1)S(1)} %edge_back.1), channel_id=1, source_target_pairs={{32,0},{36,4},{40,8},{44,12},{48,16},{52,20},{56,24},{60,28},{33,1... | collective-permute-start | bytes 786440 | tf_op jit(solution)/shard_map/ppermute | solution.py:643
  51.5 3.5 %collective-permute-start.17 = (bf16[256,512]{1,0:T(8,128)(2,1)S(1)}, bf16[256,512]{1,0:T(8,128)(2,1)S(1)}, u32[]{:S(2)}, u32[]{:S(2)}) collective-permute-start(bf16[256,512]{1,0:T(8,128)(2,1)S(1)} %get-tuple-element.145), channel_id=1, source_target_pairs={{0,24},{4,28},{8,0},{12,4},{16,8},{20,12},{24,16},{28,20},{32,56},... | collective-permute-start | bytes 786440 | tf_op jit(solution)/shard_map/ppermute | solution.py:643
  56.6 3.7 %collective-permute-start.13 = (bf16[256,512]{1,0:T(8,128)(2,1)S(1)}, bf16[256,512]{1,0:T(8,128)(2,1)S(1)}, u32[]{:S(2)}, u32[]{:S(2)}) collective-permute-start(bf16[256,512]{1,0:T(8,128)(2,1)S(1)} %get-tuple-element.131), channel_id=1, source_target_pairs={{0,24},{4,28},{8,0},{12,4},{16,8},{20,12},{24,16},{28,20},{32,56},... | collective-permute-start | bytes 786440 | tf_op jit(solution)/shard_map/ppermute | solution.py:643
  60.6 3.2 %collective-permute-done.17.c1 = bf16[256,512]{1,0:T(8,128)(2,1)S(1)} collective-permute-done((bf16[256,512]{1,0:T(8,128)(2,1)S(1)}, bf16[256,512]{1,0:T(8,128)(2,1)S(1)}, u32[]{:S(2)}, u32[]{:S(2)}) %collective-permute-start.17) | collective-permute-done | bytes 262176 | tf_op jit(solution)/shard_map/ppermute | solution.py:643
  63.8 5.9 %inner_1.1 = (f32[256,1024]{1,0:T(8,128)S(1)}, f32[256,512]{1,0:T(8,128)S(1)}, f32[256,128]{1,0:T(8,128)S(1)}, f32[256,128]{1,0:T(8,128)S(1)}, f32[8,2048]{1,0:T(8,128)S(1)}) custom-call(bf16[256,2048]{1,0:T(8,128)(2,1)S(1)} %get-tuple-element.120.x, bf16[256,2048]{1,0:T(8,128)(2,1)S(1)} %get-tuple-element.136.dy, ...), custom_call_target="tpu_custom_call" | custom-call | bytes 18000000 | tf_op jit(solution)/shard_map/inner_1/pallas_call | solution.py:617
  70.4 2.1 %carry.1 = (f32[256,128]{1,0:T(8,128)S(1)}, f32[256,256]{1,0:T(8,128)S(1)}, bf16[256,2048]{1,0:T(8,128)(2,1)S(1)}) custom-call(bf16[256,512]{1,0:T(8,128)(2,1)S(1)} %get-tuple-element.144.c0, bf16[256,512]{1,0:T(8,128)(2,1)S(1)} %collective-permute-done.17.c1, bf16[256,512]{1,0:T(8,128)(2,1)S(1)} %collective-permute-done.18.c2, ...), custom_call_target="tpu_custom_call" | custom-call | bytes 12000000 | tf_op jit(solution)/shard_map/carry/pallas_call | solution.py:617
  72.6 4.3 %collective-permute-done.13.g1 = bf16[256,512]{1,0:T(8,128)(2,1)S(1)} collective-permute-done((bf16[256,512]{1,0:T(8,128)(2,1)S(1)}, bf16[256,512]{1,0:T(8,128)(2,1)S(1)}, u32[]{:S(2)}, u32[]{:S(2)}) %collective-permute-start.13) | collective-permute-done | bytes 262176 | tf_op jit(solution)/shard_map/ppermute | solution.py:643
  76.9 4.0 %collective-permute-done.15.g3 = bf16[256,512]{1,0:T(8,128)(2,1)S(1)} collective-permute-done((bf16[256,512]{1,0:T(8,128)(2,1)S(1)}, bf16[256,512]{1,0:T(8,128)(2,1)S(1)}, u32[]{:S(2)}, u32[]{:S(2)}) %collective-permute-start.15) | collective-permute-done | bytes 262176 | tf_op jit(solution)/shard_map/ppermute | solution.py:643
  81.4 1.9 %collective-permute-start.20 = (bf16[8,2560]{1,0:T(8,128)(2,1)S(1)}, bf16[8,2560]{1,0:T(8,128)(2,1)S(1)}, u32[]{:S(2)}, u32[]{:S(2)}) collective-permute-start(bf16[8,2560]{1,0:T(8,128)(2,1)S(1)} %head.1), channel_id=1, source_target_pairs={{8,0},{12,4},{16,8},{20,12},{24,16},{28,20},{32,24},{36,28},{40,32... | collective-permute-start | bytes 122888 | tf_op jit(solution)/shard_map/ppermute | solution.py:643
  83.4 2.7 %last.1 = (f32[256,2048]{1,0:T(8,128)S(1)}, f32[256,512]{1,0:T(8,128)S(1)}, f32[256,128]{1,0:T(8,128)S(1)}) custom-call(bf16[256,512]{1,0:T(8,128)(2,1)S(1)} %get-tuple-element.152.g0, bf16[256,512]{1,0:T(8,128)(2,1)S(1)} %collective-permute-done.13.g1, bf16[256,512]{1,0:T(8,128)(2,1)S(1)} %collective-permute-done.14.g2, ...), custom_call_target="tpu_custom_call" | custom-call | bytes 15000000 | tf_op jit(solution)/shard_map/last/pallas_call | solution.py:617
  86.2 1.5 %back.1 = (bf16[128,2048]{1,0:T(8,128)(2,1)S(1)}, bf16[128,512]{1,0:T(8,128)(2,1)S(1)}, bf16[128,128]{1,0:T(8,128)(2,1)S(1)}, bf16[128,2688]{1,0:T(8,128)(2,1)S(1)}) custom-call(f32[256,2048]{1,0:T(8,128)S(1)} %get-tuple-element.158.e, f32[256,512]{1,0:T(8,128)S(1)} %get-tuple-element.159.es, f32[256,128]{1,0:T(8,128)S(1)} %get-tuple-element.160.steps, ...), custom_call_target="tpu_custom_call" | custom-call | bytes 9000000 | tf_op jit(solution)/shard_map/back/pallas_call | solution.py:617
  87.7 2.1 %collective-permute-start.21 = (bf16[128,2688]{1,0:T(8,128)(2,1)S(1)}, bf16[128,2688]{1,0:T(8,128)(2,1)S(1)}, u32[]{:S(2)}, u32[]{:S(2)}) collective-permute-start(bf16[128,2688]{1,0:T(8,128)(2,1)S(1)} %get-tuple-element.165), channel_id=1, source_target_pairs={{0,4},{4,0},{8,12},{12,8},{16,20},{20,16},{24,28},{28,24},{32,36},... | collective-permute-start | bytes 2064392 | tf_op jit(solution)/shard_map/ppermute | solution.py:643
  89.7 1.8 %collective-permute-done.21.message = bf16[128,2688]{1,0:T(8,128)(2,1)S(1)} collective-permute-done((bf16[128,2688]{1,0:T(8,128)(2,1)S(1)}, bf16[128,2688]{1,0:T(8,128)(2,1)S(1)}, u32[]{:S(2)}, u32[]{:S(2)}) %collective-permute-start.21) | collective-permute-done | bytes 688160 | tf_op jit(solution)/shard_map/ppermute | solution.py:643
  (59 shorter events, 17.1 us)
Async XLA Ops:
  0.6 10.8 %copy-start.5 = (bf16[1,128,64]{1,2,0:T(8,128)(2,1)S(1)}, bf16[1,128,64]{1,2,0:T(8,128)(2,1)}, u32[]{:S(2)}) copy-start(bf16[1,128,64]{1,2,0:T(8,128)(2,1)} %param.13) | copy-start | bytes 49156
  0.6 10.8 %copy-start.1 = (bf16[1,128,1024]{2,1,0:T(8,128)(2,1)S(1)}, bf16[1,128,1024]{2,1,0:T(8,128)(2,1)}, u32[]{:S(2)}) copy-start(bf16[1,128,1024]{2,1,0:T(8,128)(2,1)} %param.12) | copy-start | bytes 786436
  2.1 9.3 %collective-permute-start.3 = (bf16[128,2688]{1,0:T(8,128)(2,1)S(1)}, bf16[128,2688]{1,0:T(8,128)(2,1)S(1)}, u32[]{:S(2)}, u32[]{:S(2)}) collective-permute-start(bf16[128,2688]{1,0:T(8,128)(2,1)S(1)} %get-tuple-element.95), channel_id=1, source_target_pairs={{0,4},{4,0},{8,12},{12,8},{16,20},{20,16},{24,28},{28,24},{32,36},... | collective-permute-start | bytes 2064392 | tf_op jit(solution)/shard_map/ppermute | solution.py:643
  2.8 1.9 %collective-permute-start = (bf16[16,2560]{1,0:T(8,128)(2,1)S(1)}, bf16[16,2560]{1,0:T(8,128)(2,1)S(1)}, u32[]{:S(2)}, u32[]{:S(2)}) collective-permute-start(bf16[16,2560]{1,0:T(8,128)(2,1)S(1)} %get-tuple-element.90), channel_id=1, source_target_pairs={{28,92},{92,28},{29,93},{93,29},{30,94},{94,30},{31,95},{95,31}} | collective-permute-start | bytes 245768 | tf_op jit(solution)/shard_map/ppermute | solution.py:674
  4.8 19.6 %collective-permute-start.7 = (bf16[128,2048]{1,0:T(8,128)(2,1)S(1)}, bf16[128,2048]{1,0:T(8,128)(2,1)S(1)}, u32[]{:S(2)}, u32[]{:S(2)}) collective-permute-start(bf16[128,2048]{1,0:T(8,128)(2,1)S(1)} %get-tuple-element.109), channel_id=1, source_target_pairs={{0,64},{64,0},{1,65},{65,1},{2,66},{66,2},{3,67},{67,3},{4,68},{68... | collective-permute-start | bytes 1572872 | tf_op jit(solution)/shard_map/ppermute | solution.py:698
  5.4 24.6 %collective-permute-start.8 = (bf16[128,2048]{1,0:T(8,128)(2,1)S(1)}, bf16[128,2048]{1,0:T(8,128)(2,1)S(1)}, u32[]{:S(2)}, u32[]{:S(2)}) collective-permute-start(bf16[128,2048]{1,0:T(8,128)(2,1)S(1)} %get-tuple-element.114), channel_id=1, source_target_pairs={{0,68},{4,64},{8,76},{12,72},{16,84},{20,80},{24,92},{28,88},{32,1... | collective-permute-start | bytes 1572872 | tf_op jit(solution)/shard_map/ppermute | solution.py:699
  6.5 10.4 %collective-permute-start.1 = (bf16[8,2560]{1,0:T(8,128)(2,1)S(1)}, bf16[8,2560]{1,0:T(8,128)(2,1)S(1)}, u32[]{:S(2)}, u32[]{:S(2)}) collective-permute-start(bf16[8,2560]{1,0:T(8,128)(2,1)S(1)} %get-tuple-element.93), channel_id=1, source_target_pairs={{4,12},{12,20},{20,28},{92,36},{36,44},{44,52},{52,60},{68,76},{76... | collective-permute-start | bytes 122888 | tf_op jit(solution)/shard_map/ppermute | solution.py:690
  10.1 6.8 %collective-permute-start.2 = (bf16[8,2560]{1,0:T(8,128)(2,1)S(1)}, bf16[8,2560]{1,0:T(8,128)(2,1)S(1)}, u32[]{:S(2)}, u32[]{:S(2)}) collective-permute-start(bf16[8,2560]{1,0:T(8,128)(2,1)S(1)} %get-tuple-element.94), channel_id=1, source_target_pairs={{4,8},{12,16},{20,24},{92,32},{36,40},{44,48},{52,56},{68,72},{76,... | collective-permute-start | bytes 122888 | tf_op jit(solution)/shard_map/ppermute | solution.py:690
  17.7 18.9 %collective-permute-start.4 = (bf16[272,512]{1,0:T(8,128)(2,1)S(1)}, bf16[272,512]{1,0:T(8,128)(2,1)S(1)}, u32[]{:S(2)}, u32[]{:S(2)}) collective-permute-start(bf16[272,512]{1,0:T(8,128)(2,1)S(1)} %get-tuple-element.106), channel_id=1, source_target_pairs={{0,8},{4,12},{8,16},{12,20},{16,24},{20,28},{24,0},{28,4},{32,40},... | collective-permute-start | bytes 835592 | tf_op jit(solution)/shard_map/ppermute | solution.py:643
  19.5 17.9 %collective-permute-start.5 = (bf16[272,512]{1,0:T(8,128)(2,1)S(1)}, bf16[272,512]{1,0:T(8,128)(2,1)S(1)}, u32[]{:S(2)}, u32[]{:S(2)}) collective-permute-start(bf16[272,512]{1,0:T(8,128)(2,1)S(1)} %get-tuple-element.107), channel_id=1, source_target_pairs={{0,16},{4,20},{8,24},{12,28},{16,0},{20,4},{24,8},{28,12},{32,48},... | collective-permute-start | bytes 835592 | tf_op jit(solution)/shard_map/ppermute | solution.py:643
  21.2 16.2 %collective-permute-start.6 = (bf16[272,512]{1,0:T(8,128)(2,1)S(1)}, bf16[272,512]{1,0:T(8,128)(2,1)S(1)}, u32[]{:S(2)}, u32[]{:S(2)}) collective-permute-start(bf16[272,512]{1,0:T(8,128)(2,1)S(1)} %get-tuple-element.108), channel_id=1, source_target_pairs={{0,24},{4,28},{8,0},{12,4},{16,8},{20,12},{24,16},{28,20},{32,56},... | collective-permute-start | bytes 835592 | tf_op jit(solution)/shard_map/ppermute | solution.py:643
  31.6 13.1 %collective-permute-start.9 = (bf16[256,512]{1,0:T(8,128)(2,1)S(1)}, bf16[256,512]{1,0:T(8,128)(2,1)S(1)}, u32[]{:S(2)}, u32[]{:S(2)}) collective-permute-start(bf16[256,512]{1,0:T(8,128)(2,1)S(1)} %get-tuple-element.117), channel_id=1, source_target_pairs={{0,8},{4,12},{8,16},{12,20},{16,24},{20,28},{24,0},{28,4},{32,40},... | collective-permute-start | bytes 786440 | tf_op jit(solution)/shard_map/ppermute | solution.py:643
  33.3 15.4 %collective-permute-start.10 = (bf16[256,512]{1,0:T(8,128)(2,1)S(1)}, bf16[256,512]{1,0:T(8,128)(2,1)S(1)}, u32[]{:S(2)}, u32[]{:S(2)}) collective-permute-start(bf16[256,512]{1,0:T(8,128)(2,1)S(1)} %get-tuple-element.118), channel_id=1, source_target_pairs={{0,16},{4,20},{8,24},{12,28},{16,0},{20,4},{24,8},{28,12},{32,48},... | collective-permute-start | bytes 786440 | tf_op jit(solution)/shard_map/ppermute | solution.py:643
  36.6 12.1 %collective-permute-start.11 = (bf16[256,512]{1,0:T(8,128)(2,1)S(1)}, bf16[256,512]{1,0:T(8,128)(2,1)S(1)}, u32[]{:S(2)}, u32[]{:S(2)}) collective-permute-start(bf16[256,512]{1,0:T(8,128)(2,1)S(1)} %get-tuple-element.119), channel_id=1, source_target_pairs={{0,24},{4,28},{8,0},{12,4},{16,8},{20,12},{24,16},{28,20},{32,56},... | collective-permute-start | bytes 786440 | tf_op jit(solution)/shard_map/ppermute | solution.py:643
  37.7 12.9 %collective-permute-start.16 = (bf16[256,512]{1,0:T(8,128)(2,1)S(1)}, bf16[256,512]{1,0:T(8,128)(2,1)S(1)}, u32[]{:S(2)}, u32[]{:S(2)}) collective-permute-start(bf16[256,512]{1,0:T(8,128)(2,1)S(1)} %edge_forward.1), channel_id=1, source_target_pairs={{0,32},{4,36},{8,40},{12,44},{16,48},{20,52},{24,56},{28,60},{1,33... | collective-permute-start | bytes 786440 | tf_op jit(solution)/shard_map/ppermute | solution.py:643
  49.0 6.6 %collective-permute-start.12 = (bf16[256,512]{1,0:T(8,128)(2,1)S(1)}, bf16[256,512]{1,0:T(8,128)(2,1)S(1)}, u32[]{:S(2)}, u32[]{:S(2)}) collective-permute-start(bf16[256,512]{1,0:T(8,128)(2,1)S(1)} %edge_back.1), channel_id=1, source_target_pairs={{32,0},{36,4},{40,8},{44,12},{48,16},{52,20},{56,24},{60,28},{33,1... | collective-permute-start | bytes 786440 | tf_op jit(solution)/shard_map/ppermute | solution.py:643
  51.5 12.3 %collective-permute-start.17 = (bf16[256,512]{1,0:T(8,128)(2,1)S(1)}, bf16[256,512]{1,0:T(8,128)(2,1)S(1)}, u32[]{:S(2)}, u32[]{:S(2)}) collective-permute-start(bf16[256,512]{1,0:T(8,128)(2,1)S(1)} %get-tuple-element.145), channel_id=1, source_target_pairs={{0,24},{4,28},{8,0},{12,4},{16,8},{20,12},{24,16},{28,20},{32,56},... | collective-permute-start | bytes 786440 | tf_op jit(solution)/shard_map/ppermute | solution.py:643
  55.0 14.7 %collective-permute-start.18 = (bf16[256,512]{1,0:T(8,128)(2,1)S(1)}, bf16[256,512]{1,0:T(8,128)(2,1)S(1)}, u32[]{:S(2)}, u32[]{:S(2)}) collective-permute-start(bf16[256,512]{1,0:T(8,128)(2,1)S(1)} %get-tuple-element.146), channel_id=1, source_target_pairs={{0,16},{4,20},{8,24},{12,28},{16,0},{20,4},{24,8},{28,12},{32,48},... | collective-permute-start | bytes 786440 | tf_op jit(solution)/shard_map/ppermute | solution.py:643
  55.0 15.4 %collective-permute-start.19 = (bf16[256,512]{1,0:T(8,128)(2,1)S(1)}, bf16[256,512]{1,0:T(8,128)(2,1)S(1)}, u32[]{:S(2)}, u32[]{:S(2)}) collective-permute-start(bf16[256,512]{1,0:T(8,128)(2,1)S(1)} %get-tuple-element.147), channel_id=1, source_target_pairs={{0,8},{4,12},{8,16},{12,20},{16,24},{20,28},{24,0},{28,4},{32,40},... | collective-permute-start | bytes 786440 | tf_op jit(solution)/shard_map/ppermute | solution.py:643
  56.6 20.3 %collective-permute-start.13 = (bf16[256,512]{1,0:T(8,128)(2,1)S(1)}, bf16[256,512]{1,0:T(8,128)(2,1)S(1)}, u32[]{:S(2)}, u32[]{:S(2)}) collective-permute-start(bf16[256,512]{1,0:T(8,128)(2,1)S(1)} %get-tuple-element.131), channel_id=1, source_target_pairs={{0,24},{4,28},{8,0},{12,4},{16,8},{20,12},{24,16},{28,20},{32,56},... | collective-permute-start | bytes 786440 | tf_op jit(solution)/shard_map/ppermute | solution.py:643
  60.3 16.6 %collective-permute-start.14 = (bf16[256,512]{1,0:T(8,128)(2,1)S(1)}, bf16[256,512]{1,0:T(8,128)(2,1)S(1)}, u32[]{:S(2)}, u32[]{:S(2)}) collective-permute-start(bf16[256,512]{1,0:T(8,128)(2,1)S(1)} %get-tuple-element.132), channel_id=1, source_target_pairs={{0,16},{4,20},{8,24},{12,28},{16,0},{20,4},{24,8},{28,12},{32,48},... | collective-permute-start | bytes 786440 | tf_op jit(solution)/shard_map/ppermute | solution.py:643
  63.8 17.2 %collective-permute-start.15 = (bf16[256,512]{1,0:T(8,128)(2,1)S(1)}, bf16[256,512]{1,0:T(8,128)(2,1)S(1)}, u32[]{:S(2)}, u32[]{:S(2)}) collective-permute-start(bf16[256,512]{1,0:T(8,128)(2,1)S(1)} %get-tuple-element.133), channel_id=1, source_target_pairs={{0,8},{4,12},{8,16},{12,20},{16,24},{20,28},{24,0},{28,4},{32,40},... | collective-permute-start | bytes 786440 | tf_op jit(solution)/shard_map/ppermute | solution.py:643
  81.4 4.7 %collective-permute-start.20 = (bf16[8,2560]{1,0:T(8,128)(2,1)S(1)}, bf16[8,2560]{1,0:T(8,128)(2,1)S(1)}, u32[]{:S(2)}, u32[]{:S(2)}) collective-permute-start(bf16[8,2560]{1,0:T(8,128)(2,1)S(1)} %head.1), channel_id=1, source_target_pairs={{8,0},{12,4},{16,8},{20,12},{24,16},{28,20},{32,24},{36,28},{40,32... | collective-permute-start | bytes 122888 | tf_op jit(solution)/shard_map/ppermute | solution.py:643
  87.7 3.9 %collective-permute-start.21 = (bf16[128,2688]{1,0:T(8,128)(2,1)S(1)}, bf16[128,2688]{1,0:T(8,128)(2,1)S(1)}, u32[]{:S(2)}, u32[]{:S(2)}) collective-permute-start(bf16[128,2688]{1,0:T(8,128)(2,1)S(1)} %get-tuple-element.165), channel_id=1, source_target_pairs={{0,4},{4,0},{8,12},{12,8},{16,20},{20,16},{24,28},{28,24},{32,36},... | collective-permute-start | bytes 2064392 | tf_op jit(solution)/shard_map/ppermute | solution.py:643
  (8 other events, 84.4 us)

commit v7 on v6

--- a/solution.py
+++ b/solution.py
@@ -650,7 +650,7 @@
 
     def exchange(parts, sign):
         out = list(parts)
-        for k in (2, 1, 3):
+        for k in (1, 2, 3):
             out[k] = send(parts[k], [(i, around(i, sign * k)) for i in range(count)])
         return out
 

time: 92.9 us -> 92.9 us (level)
  no operation moved by 1% of the time
where the time goes in v7:
time: 92.9 us; the launch traced here: 92.6 us
  starting transfers between devices  34.1 us (37%)
  Pallas kernels  33.5 us (36%)
  waiting for transfers between devices  23.9 us (26%)
  between operations  1.02 us (1%)
    pallas_call x19, Pallas kernels, call(): pl.pallas_call(kernel, in_specs=[pl.BlockSpec(memory_space=pltpu.HBM) if...  33.5 us
    ppermute x17, starting transfers between devices, send(): return lax.ppermute(x, 'ctx', pairs)  26.9 us
    ppermute x17, waiting for transfers between devices, send(): return lax.ppermute(x, 'ctx', pairs)  18.2 us
    ppermute x1, waiting for transfers between devices, local(): lax.ppermute(g_in, ('pipe', 'ctx'), [(p * count + i, (1 - p) * count + (i...  5.67 us
    ppermute x2, starting transfers between devices, onward(): return lax.ppermute(x, ('pipe', 'ctx'), pairs)  4.83 us
  transfers between devices with their start and end apart: 22, of which 8 were waited for; matrix products, arithmetic and copies ran while one was open for 0% of the time, Pallas kernels for 31%

profile of v7, /device:TPU:15, one launch (start us, length us, event | category | flops | bytes accessed | tf_op | source)
XLA Modules:
  0.0 92.6 jit_solution(10527818023984434764)
XLA Ops:
  6.5 3.5 %collective-permute-start.1 = (bf16[8,2560]{1,0:T(8,128)(2,1)S(1)}, bf16[8,2560]{1,0:T(8,128)(2,1)S(1)}, u32[]{:S(2)}, u32[]{:S(2)}) collective-permute-start(bf16[8,2560]{1,0:T(8,128)(2,1)S(1)} %get-tuple-element.93), channel_id=1, source_target_pairs={{4,12},{12,20},{20,28},{92,36},{36,44},{44,52},{52,60},{68,76},{76... | collective-permute-start | bytes 122888 | tf_op jit(solution)/shard_map/ppermute | solution.py:690
  11.5 5.4 %first.1 = (bf16[256,2048]{1,0:T(8,128)(2,1)S(1)}, bf16[256,2048]{1,0:T(8,128)(2,1)S(1)}, bf16[256,512]{1,0:T(8,128)(2,1)S(1)}, f32[256,2048]{1,0:T(8,128)S(1)},...) custom-call(bf16[128,4096]{1,0:T(8,128)(2,1)S(1)} %bitcast.17, ...), custom_call_target="tpu_custom_call" | custom-call | bytes 24000000 | tf_op jit(solution)/shard_map/first/pallas_call | solution.py:617
  17.7 1.7 %collective-permute-start.4 = (bf16[272,512]{1,0:T(8,128)(2,1)S(1)}, bf16[272,512]{1,0:T(8,128)(2,1)S(1)}, u32[]{:S(2)}, u32[]{:S(2)}) collective-permute-start(bf16[272,512]{1,0:T(8,128)(2,1)S(1)} %get-tuple-element.106), channel_id=1, source_target_pairs={{0,8},{4,12},{8,16},{12,20},{16,24},{20,28},{24,0},{28,4},{32,40},... | collective-permute-start | bytes 835592 | tf_op jit(solution)/shard_map/ppermute | solution.py:643
  19.5 1.8 %collective-permute-start.5 = (bf16[272,512]{1,0:T(8,128)(2,1)S(1)}, bf16[272,512]{1,0:T(8,128)(2,1)S(1)}, u32[]{:S(2)}, u32[]{:S(2)}) collective-permute-start(bf16[272,512]{1,0:T(8,128)(2,1)S(1)} %get-tuple-element.107), channel_id=1, source_target_pairs={{0,16},{4,20},{8,24},{12,28},{16,0},{20,4},{24,8},{28,12},{32,48},... | collective-permute-start | bytes 835592 | tf_op jit(solution)/shard_map/ppermute | solution.py:643
  21.2 2.0 %collective-permute-start.6 = (bf16[272,512]{1,0:T(8,128)(2,1)S(1)}, bf16[272,512]{1,0:T(8,128)(2,1)S(1)}, u32[]{:S(2)}, u32[]{:S(2)}) collective-permute-start(bf16[272,512]{1,0:T(8,128)(2,1)S(1)} %get-tuple-element.108), channel_id=1, source_target_pairs={{0,24},{4,28},{8,0},{12,4},{16,8},{20,12},{24,16},{28,20},{32,56},... | collective-permute-start | bytes 835592 | tf_op jit(solution)/shard_map/ppermute | solution.py:643
  24.4 5.7 %collective-permute-done.8.g_in = bf16[128,2048]{1,0:T(8,128)(2,1)S(1)} collective-permute-done((bf16[128,2048]{1,0:T(8,128)(2,1)S(1)}, bf16[128,2048]{1,0:T(8,128)(2,1)S(1)}, u32[]{:S(2)}, u32[]{:S(2)}) %collective-permute-start.8) | collective-permute-done | bytes 524320 | tf_op jit(solution)/shard_map/ppermute | solution.py:699
  30.0 1.6 %second.1 = (bf16[256,512]{1,0:T(8,128)(2,1)S(1)}, bf16[256,512]{1,0:T(8,128)(2,1)S(1)}, bf16[256,512]{1,0:T(8,128)(2,1)S(1)}, bf16[256,512]{1,0:T(8,128)(2,1)S(...) custom-call(bf16[128,2048]{1,0:T(8,128)(2,1)S(1)} %collective-permute-done.7.g_own, ...), custom_call_target="tpu_custom_call" | custom-call | bytes 12000000 | tf_op jit(solution)/shard_map/second/pallas_call | solution.py:617
  31.6 1.7 %collective-permute-start.9 = (bf16[256,512]{1,0:T(8,128)(2,1)S(1)}, bf16[256,512]{1,0:T(8,128)(2,1)S(1)}, u32[]{:S(2)}, u32[]{:S(2)}) collective-permute-start(bf16[256,512]{1,0:T(8,128)(2,1)S(1)} %get-tuple-element.117), channel_id=1, source_target_pairs={{0,8},{4,12},{8,16},{12,20},{16,24},{20,28},{24,0},{28,4},{32,40},... | collective-permute-start | bytes 786440 | tf_op jit(solution)/shard_map/ppermute | solution.py:643
  33.3 3.3 %collective-permute-start.10 = (bf16[256,512]{1,0:T(8,128)(2,1)S(1)}, bf16[256,512]{1,0:T(8,128)(2,1)S(1)}, u32[]{:S(2)}, u32[]{:S(2)}) collective-permute-start(bf16[256,512]{1,0:T(8,128)(2,1)S(1)} %get-tuple-element.118), channel_id=1, source_target_pairs={{0,16},{4,20},{8,24},{12,28},{16,0},{20,4},{24,8},{28,12},{32,48},... | collective-permute-start | bytes 786440 | tf_op jit(solution)/shard_map/ppermute | solution.py:643
  39.0 5.7 %inner_0.1 = (f32[256,1024]{1,0:T(8,128)S(1)}, f32[256,256]{1,0:T(8,128)S(1)}, f32[256,128]{1,0:T(8,128)S(1)}, f32[256,128]{1,0:T(8,128)S(1)}) custom-call(bf16[256,2048]{1,0:T(8,128)(2,1)S(1)} %get-tuple-element.120.x, bf16[256,2048]{1,0:T(8,128)(2,1)S(1)} %get-tuple-element.136.dy, bf16[256,512]{1,0:T(8,128)(2,1)S(1)} %get-tuple-element.115.bc, ...), custom_call_target="tpu_custom_call" | custom-call | bytes 18000000 | tf_op jit(solution)/shard_map/inner_0/pallas_call | solution.py:617
  44.7 4.0 %collective-permute-done.10.d2 = bf16[256,512]{1,0:T(8,128)(2,1)S(1)} collective-permute-done((bf16[256,512]{1,0:T(8,128)(2,1)S(1)}, bf16[256,512]{1,0:T(8,128)(2,1)S(1)}, u32[]{:S(2)}, u32[]{:S(2)}) %collective-permute-start.10) | collective-permute-done | bytes 262176 | tf_op jit(solution)/shard_map/ppermute | solution.py:643
  49.0 1.5 %collective-permute-start.12 = (bf16[256,512]{1,0:T(8,128)(2,1)S(1)}, bf16[256,512]{1,0:T(8,128)(2,1)S(1)}, u32[]{:S(2)}, u32[]{:S(2)}) collective-permute-start(bf16[256,512]{1,0:T(8,128)(2,1)S(1)} %edge_back.1), channel_id=1, source_target_pairs={{32,0},{36,4},{40,8},{44,12},{48,16},{52,20},{56,24},{60,28},{33,1... | collective-permute-start | bytes 786440 | tf_op jit(solution)/shard_map/ppermute | solution.py:643
  51.5 3.5 %collective-permute-start.17 = (bf16[256,512]{1,0:T(8,128)(2,1)S(1)}, bf16[256,512]{1,0:T(8,128)(2,1)S(1)}, u32[]{:S(2)}, u32[]{:S(2)}) collective-permute-start(bf16[256,512]{1,0:T(8,128)(2,1)S(1)} %get-tuple-element.145), channel_id=1, source_target_pairs={{0,24},{4,28},{8,0},{12,4},{16,8},{20,12},{24,16},{28,20},{32,56},... | collective-permute-start | bytes 786440 | tf_op jit(solution)/shard_map/ppermute | solution.py:643
  56.6 3.7 %collective-permute-start.13 = (bf16[256,512]{1,0:T(8,128)(2,1)S(1)}, bf16[256,512]{1,0:T(8,128)(2,1)S(1)}, u32[]{:S(2)}, u32[]{:S(2)}) collective-permute-start(bf16[256,512]{1,0:T(8,128)(2,1)S(1)} %get-tuple-element.131), channel_id=1, source_target_pairs={{0,24},{4,28},{8,0},{12,4},{16,8},{20,12},{24,16},{28,20},{32,56},... | collective-permute-start | bytes 786440 | tf_op jit(solution)/shard_map/ppermute | solution.py:643
  60.6 3.2 %collective-permute-done.17.c1 = bf16[256,512]{1,0:T(8,128)(2,1)S(1)} collective-permute-done((bf16[256,512]{1,0:T(8,128)(2,1)S(1)}, bf16[256,512]{1,0:T(8,128)(2,1)S(1)}, u32[]{:S(2)}, u32[]{:S(2)}) %collective-permute-start.17) | collective-permute-done | bytes 262176 | tf_op jit(solution)/shard_map/ppermute | solution.py:643
  63.8 5.9 %inner_1.1 = (f32[256,1024]{1,0:T(8,128)S(1)}, f32[256,512]{1,0:T(8,128)S(1)}, f32[256,128]{1,0:T(8,128)S(1)}, f32[256,128]{1,0:T(8,128)S(1)}, f32[8,2048]{1,0:T(8,128)S(1)}) custom-call(bf16[256,2048]{1,0:T(8,128)(2,1)S(1)} %get-tuple-element.120.x, bf16[256,2048]{1,0:T(8,128)(2,1)S(1)} %get-tuple-element.136.dy, ...), custom_call_target="tpu_custom_call" | custom-call | bytes 18000000 | tf_op jit(solution)/shard_map/inner_1/pallas_call | solution.py:617
  70.4 2.1 %carry.1 = (f32[256,128]{1,0:T(8,128)S(1)}, f32[256,256]{1,0:T(8,128)S(1)}, bf16[256,2048]{1,0:T(8,128)(2,1)S(1)}) custom-call(bf16[256,512]{1,0:T(8,128)(2,1)S(1)} %get-tuple-element.144.c0, bf16[256,512]{1,0:T(8,128)(2,1)S(1)} %collective-permute-done.17.c1, bf16[256,512]{1,0:T(8,128)(2,1)S(1)} %collective-permute-done.18.c2, ...), custom_call_target="tpu_custom_call" | custom-call | bytes 12000000 | tf_op jit(solution)/shard_map/carry/pallas_call | solution.py:617
  72.6 4.3 %collective-permute-done.13.g1 = bf16[256,512]{1,0:T(8,128)(2,1)S(1)} collective-permute-done((bf16[256,512]{1,0:T(8,128)(2,1)S(1)}, bf16[256,512]{1,0:T(8,128)(2,1)S(1)}, u32[]{:S(2)}, u32[]{:S(2)}) %collective-permute-start.13) | collective-permute-done | bytes 262176 | tf_op jit(solution)/shard_map/ppermute | solution.py:643
  76.9 4.0 %collective-permute-done.15.g3 = bf16[256,512]{1,0:T(8,128)(2,1)S(1)} collective-permute-done((bf16[256,512]{1,0:T(8,128)(2,1)S(1)}, bf16[256,512]{1,0:T(8,128)(2,1)S(1)}, u32[]{:S(2)}, u32[]{:S(2)}) %collective-permute-start.15) | collective-permute-done | bytes 262176 | tf_op jit(solution)/shard_map/ppermute | solution.py:643
  81.4 1.9 %collective-permute-start.20 = (bf16[8,2560]{1,0:T(8,128)(2,1)S(1)}, bf16[8,2560]{1,0:T(8,128)(2,1)S(1)}, u32[]{:S(2)}, u32[]{:S(2)}) collective-permute-start(bf16[8,2560]{1,0:T(8,128)(2,1)S(1)} %head.1), channel_id=1, source_target_pairs={{8,0},{12,4},{16,8},{20,12},{24,16},{28,20},{32,24},{36,28},{40,32... | collective-permute-start | bytes 122888 | tf_op jit(solution)/shard_map/ppermute | solution.py:643
  83.4 2.7 %last.1 = (f32[256,2048]{1,0:T(8,128)S(1)}, f32[256,512]{1,0:T(8,128)S(1)}, f32[256,128]{1,0:T(8,128)S(1)}) custom-call(bf16[256,512]{1,0:T(8,128)(2,1)S(1)} %get-tuple-element.152.g0, bf16[256,512]{1,0:T(8,128)(2,1)S(1)} %collective-permute-done.13.g1, bf16[256,512]{1,0:T(8,128)(2,1)S(1)} %collective-permute-done.14.g2, ...), custom_call_target="tpu_custom_call" | custom-call | bytes 15000000 | tf_op jit(solution)/shard_map/last/pallas_call | solution.py:617
  86.2 1.5 %back.1 = (bf16[128,2048]{1,0:T(8,128)(2,1)S(1)}, bf16[128,512]{1,0:T(8,128)(2,1)S(1)}, bf16[128,128]{1,0:T(8,128)(2,1)S(1)}, bf16[128,2688]{1,0:T(8,128)(2,1)S(1)}) custom-call(f32[256,2048]{1,0:T(8,128)S(1)} %get-tuple-element.158.e, f32[256,512]{1,0:T(8,128)S(1)} %get-tuple-element.159.es, f32[256,128]{1,0:T(8,128)S(1)} %get-tuple-element.160.steps, ...), custom_call_target="tpu_custom_call" | custom-call | bytes 9000000 | tf_op jit(solution)/shard_map/back/pallas_call | solution.py:617
  87.7 2.1 %collective-permute-start.21 = (bf16[128,2688]{1,0:T(8,128)(2,1)S(1)}, bf16[128,2688]{1,0:T(8,128)(2,1)S(1)}, u32[]{:S(2)}, u32[]{:S(2)}) collective-permute-start(bf16[128,2688]{1,0:T(8,128)(2,1)S(1)} %get-tuple-element.165), channel_id=1, source_target_pairs={{0,4},{4,0},{8,12},{12,8},{16,20},{20,16},{24,28},{28,24},{32,36},... | collective-permute-start | bytes 2064392 | tf_op jit(solution)/shard_map/ppermute | solution.py:643
  89.7 1.8 %collective-permute-done.21.message = bf16[128,2688]{1,0:T(8,128)(2,1)S(1)} collective-permute-done((bf16[128,2688]{1,0:T(8,128)(2,1)S(1)}, bf16[128,2688]{1,0:T(8,128)(2,1)S(1)}, u32[]{:S(2)}, u32[]{:S(2)}) %collective-permute-start.21) | collective-permute-done | bytes 688160 | tf_op jit(solution)/shard_map/ppermute | solution.py:643
  (59 shorter events, 17.1 us)
Async XLA Ops:
  0.6 10.8 %copy-start.5 = (bf16[1,128,64]{1,2,0:T(8,128)(2,1)S(1)}, bf16[1,128,64]{1,2,0:T(8,128)(2,1)}, u32[]{:S(2)}) copy-start(bf16[1,128,64]{1,2,0:T(8,128)(2,1)} %param.13) | copy-start | bytes 49156
  0.6 10.8 %copy-start.1 = (bf16[1,128,1024]{2,1,0:T(8,128)(2,1)S(1)}, bf16[1,128,1024]{2,1,0:T(8,128)(2,1)}, u32[]{:S(2)}) copy-start(bf16[1,128,1024]{2,1,0:T(8,128)(2,1)} %param.12) | copy-start | bytes 786436
  2.1 9.3 %collective-permute-start.3 = (bf16[128,2688]{1,0:T(8,128)(2,1)S(1)}, bf16[128,2688]{1,0:T(8,128)(2,1)S(1)}, u32[]{:S(2)}, u32[]{:S(2)}) collective-permute-start(bf16[128,2688]{1,0:T(8,128)(2,1)S(1)} %get-tuple-element.95), channel_id=1, source_target_pairs={{0,4},{4,0},{8,12},{12,8},{16,20},{20,16},{24,28},{28,24},{32,36},... | collective-permute-start | bytes 2064392 | tf_op jit(solution)/shard_map/ppermute | solution.py:643
  2.8 1.9 %collective-permute-start = (bf16[16,2560]{1,0:T(8,128)(2,1)S(1)}, bf16[16,2560]{1,0:T(8,128)(2,1)S(1)}, u32[]{:S(2)}, u32[]{:S(2)}) collective-permute-start(bf16[16,2560]{1,0:T(8,128)(2,1)S(1)} %get-tuple-element.90), channel_id=1, source_target_pairs={{28,92},{92,28},{29,93},{93,29},{30,94},{94,30},{31,95},{95,31}} | collective-permute-start | bytes 245768 | tf_op jit(solution)/shard_map/ppermute | solution.py:674
  4.8 19.6 %collective-permute-start.7 = (bf16[128,2048]{1,0:T(8,128)(2,1)S(1)}, bf16[128,2048]{1,0:T(8,128)(2,1)S(1)}, u32[]{:S(2)}, u32[]{:S(2)}) collective-permute-start(bf16[128,2048]{1,0:T(8,128)(2,1)S(1)} %get-tuple-element.109), channel_id=1, source_target_pairs={{0,64},{64,0},{1,65},{65,1},{2,66},{66,2},{3,67},{67,3},{4,68},{68... | collective-permute-start | bytes 1572872 | tf_op jit(solution)/shard_map/ppermute | solution.py:698
  5.4 24.6 %collective-permute-start.8 = (bf16[128,2048]{1,0:T(8,128)(2,1)S(1)}, bf16[128,2048]{1,0:T(8,128)(2,1)S(1)}, u32[]{:S(2)}, u32[]{:S(2)}) collective-permute-start(bf16[128,2048]{1,0:T(8,128)(2,1)S(1)} %get-tuple-element.114), channel_id=1, source_target_pairs={{0,68},{4,64},{8,76},{12,72},{16,84},{20,80},{24,92},{28,88},{32,1... | collective-permute-start | bytes 1572872 | tf_op jit(solution)/shard_map/ppermute | solution.py:699
  6.5 10.4 %collective-permute-start.1 = (bf16[8,2560]{1,0:T(8,128)(2,1)S(1)}, bf16[8,2560]{1,0:T(8,128)(2,1)S(1)}, u32[]{:S(2)}, u32[]{:S(2)}) collective-permute-start(bf16[8,2560]{1,0:T(8,128)(2,1)S(1)} %get-tuple-element.93), channel_id=1, source_target_pairs={{4,12},{12,20},{20,28},{92,36},{36,44},{44,52},{52,60},{68,76},{76... | collective-permute-start | bytes 122888 | tf_op jit(solution)/shard_map/ppermute | solution.py:690
  10.1 6.8 %collective-permute-start.2 = (bf16[8,2560]{1,0:T(8,128)(2,1)S(1)}, bf16[8,2560]{1,0:T(8,128)(2,1)S(1)}, u32[]{:S(2)}, u32[]{:S(2)}) collective-permute-start(bf16[8,2560]{1,0:T(8,128)(2,1)S(1)} %get-tuple-element.94), channel_id=1, source_target_pairs={{4,8},{12,16},{20,24},{92,32},{36,40},{44,48},{52,56},{68,72},{76,... | collective-permute-start | bytes 122888 | tf_op jit(solution)/shard_map/ppermute | solution.py:690
  17.7 18.9 %collective-permute-start.4 = (bf16[272,512]{1,0:T(8,128)(2,1)S(1)}, bf16[272,512]{1,0:T(8,128)(2,1)S(1)}, u32[]{:S(2)}, u32[]{:S(2)}) collective-permute-start(bf16[272,512]{1,0:T(8,128)(2,1)S(1)} %get-tuple-element.106), channel_id=1, source_target_pairs={{0,8},{4,12},{8,16},{12,20},{16,24},{20,28},{24,0},{28,4},{32,40},... | collective-permute-start | bytes 835592 | tf_op jit(solution)/shard_map/ppermute | solution.py:643
  19.5 17.9 %collective-permute-start.5 = (bf16[272,512]{1,0:T(8,128)(2,1)S(1)}, bf16[272,512]{1,0:T(8,128)(2,1)S(1)}, u32[]{:S(2)}, u32[]{:S(2)}) collective-permute-start(bf16[272,512]{1,0:T(8,128)(2,1)S(1)} %get-tuple-element.107), channel_id=1, source_target_pairs={{0,16},{4,20},{8,24},{12,28},{16,0},{20,4},{24,8},{28,12},{32,48},... | collective-permute-start | bytes 835592 | tf_op jit(solution)/shard_map/ppermute | solution.py:643
  21.2 16.2 %collective-permute-start.6 = (bf16[272,512]{1,0:T(8,128)(2,1)S(1)}, bf16[272,512]{1,0:T(8,128)(2,1)S(1)}, u32[]{:S(2)}, u32[]{:S(2)}) collective-permute-start(bf16[272,512]{1,0:T(8,128)(2,1)S(1)} %get-tuple-element.108), channel_id=1, source_target_pairs={{0,24},{4,28},{8,0},{12,4},{16,8},{20,12},{24,16},{28,20},{32,56},... | collective-permute-start | bytes 835592 | tf_op jit(solution)/shard_map/ppermute | solution.py:643
  31.6 13.1 %collective-permute-start.9 = (bf16[256,512]{1,0:T(8,128)(2,1)S(1)}, bf16[256,512]{1,0:T(8,128)(2,1)S(1)}, u32[]{:S(2)}, u32[]{:S(2)}) collective-permute-start(bf16[256,512]{1,0:T(8,128)(2,1)S(1)} %get-tuple-element.117), channel_id=1, source_target_pairs={{0,8},{4,12},{8,16},{12,20},{16,24},{20,28},{24,0},{28,4},{32,40},... | collective-permute-start | bytes 786440 | tf_op jit(solution)/shard_map/ppermute | solution.py:643
  33.3 15.4 %collective-permute-start.10 = (bf16[256,512]{1,0:T(8,128)(2,1)S(1)}, bf16[256,512]{1,0:T(8,128)(2,1)S(1)}, u32[]{:S(2)}, u32[]{:S(2)}) collective-permute-start(bf16[256,512]{1,0:T(8,128)(2,1)S(1)} %get-tuple-element.118), channel_id=1, source_target_pairs={{0,16},{4,20},{8,24},{12,28},{16,0},{20,4},{24,8},{28,12},{32,48},... | collective-permute-start | bytes 786440 | tf_op jit(solution)/shard_map/ppermute | solution.py:643
  36.6 12.1 %collective-permute-start.11 = (bf16[256,512]{1,0:T(8,128)(2,1)S(1)}, bf16[256,512]{1,0:T(8,128)(2,1)S(1)}, u32[]{:S(2)}, u32[]{:S(2)}) collective-permute-start(bf16[256,512]{1,0:T(8,128)(2,1)S(1)} %get-tuple-element.119), channel_id=1, source_target_pairs={{0,24},{4,28},{8,0},{12,4},{16,8},{20,12},{24,16},{28,20},{32,56},... | collective-permute-start | bytes 786440 | tf_op jit(solution)/shard_map/ppermute | solution.py:643
  37.7 12.9 %collective-permute-start.16 = (bf16[256,512]{1,0:T(8,128)(2,1)S(1)}, bf16[256,512]{1,0:T(8,128)(2,1)S(1)}, u32[]{:S(2)}, u32[]{:S(2)}) collective-permute-start(bf16[256,512]{1,0:T(8,128)(2,1)S(1)} %edge_forward.1), channel_id=1, source_target_pairs={{0,32},{4,36},{8,40},{12,44},{16,48},{20,52},{24,56},{28,60},{1,33... | collective-permute-start | bytes 786440 | tf_op jit(solution)/shard_map/ppermute | solution.py:643
  49.0 6.6 %collective-permute-start.12 = (bf16[256,512]{1,0:T(8,128)(2,1)S(1)}, bf16[256,512]{1,0:T(8,128)(2,1)S(1)}, u32[]{:S(2)}, u32[]{:S(2)}) collective-permute-start(bf16[256,512]{1,0:T(8,128)(2,1)S(1)} %edge_back.1), channel_id=1, source_target_pairs={{32,0},{36,4},{40,8},{44,12},{48,16},{52,20},{56,24},{60,28},{33,1... | collective-permute-start | bytes 786440 | tf_op jit(solution)/shard_map/ppermute | solution.py:643
  51.5 12.3 %collective-permute-start.17 = (bf16[256,512]{1,0:T(8,128)(2,1)S(1)}, bf16[256,512]{1,0:T(8,128)(2,1)S(1)}, u32[]{:S(2)}, u32[]{:S(2)}) collective-permute-start(bf16[256,512]{1,0:T(8,128)(2,1)S(1)} %get-tuple-element.145), channel_id=1, source_target_pairs={{0,24},{4,28},{8,0},{12,4},{16,8},{20,12},{24,16},{28,20},{32,56},... | collective-permute-start | bytes 786440 | tf_op jit(solution)/shard_map/ppermute | solution.py:643
  55.0 14.7 %collective-permute-start.18 = (bf16[256,512]{1,0:T(8,128)(2,1)S(1)}, bf16[256,512]{1,0:T(8,128)(2,1)S(1)}, u32[]{:S(2)}, u32[]{:S(2)}) collective-permute-start(bf16[256,512]{1,0:T(8,128)(2,1)S(1)} %get-tuple-element.146), channel_id=1, source_target_pairs={{0,16},{4,20},{8,24},{12,28},{16,0},{20,4},{24,8},{28,12},{32,48},... | collective-permute-start | bytes 786440 | tf_op jit(solution)/shard_map/ppermute | solution.py:643
  55.0 15.4 %collective-permute-start.19 = (bf16[256,512]{1,0:T(8,128)(2,1)S(1)}, bf16[256,512]{1,0:T(8,128)(2,1)S(1)}, u32[]{:S(2)}, u32[]{:S(2)}) collective-permute-start(bf16[256,512]{1,0:T(8,128)(2,1)S(1)} %get-tuple-element.147), channel_id=1, source_target_pairs={{0,8},{4,12},{8,16},{12,20},{16,24},{20,28},{24,0},{28,4},{32,40},... | collective-permute-start | bytes 786440 | tf_op jit(solution)/shard_map/ppermute | solution.py:643
  56.6 20.3 %collective-permute-start.13 = (bf16[256,512]{1,0:T(8,128)(2,1)S(1)}, bf16[256,512]{1,0:T(8,128)(2,1)S(1)}, u32[]{:S(2)}, u32[]{:S(2)}) collective-permute-start(bf16[256,512]{1,0:T(8,128)(2,1)S(1)} %get-tuple-element.131), channel_id=1, source_target_pairs={{0,24},{4,28},{8,0},{12,4},{16,8},{20,12},{24,16},{28,20},{32,56},... | collective-permute-start | bytes 786440 | tf_op jit(solution)/shard_map/ppermute | solution.py:643
  60.3 16.6 %collective-permute-start.14 = (bf16[256,512]{1,0:T(8,128)(2,1)S(1)}, bf16[256,512]{1,0:T(8,128)(2,1)S(1)}, u32[]{:S(2)}, u32[]{:S(2)}) collective-permute-start(bf16[256,512]{1,0:T(8,128)(2,1)S(1)} %get-tuple-element.132), channel_id=1, source_target_pairs={{0,16},{4,20},{8,24},{12,28},{16,0},{20,4},{24,8},{28,12},{32,48},... | collective-permute-start | bytes 786440 | tf_op jit(solution)/shard_map/ppermute | solution.py:643
  63.8 17.2 %collective-permute-start.15 = (bf16[256,512]{1,0:T(8,128)(2,1)S(1)}, bf16[256,512]{1,0:T(8,128)(2,1)S(1)}, u32[]{:S(2)}, u32[]{:S(2)}) collective-permute-start(bf16[256,512]{1,0:T(8,128)(2,1)S(1)} %get-tuple-element.133), channel_id=1, source_target_pairs={{0,8},{4,12},{8,16},{12,20},{16,24},{20,28},{24,0},{28,4},{32,40},... | collective-permute-start | bytes 786440 | tf_op jit(solution)/shard_map/ppermute | solution.py:643
  81.4 4.7 %collective-permute-start.20 = (bf16[8,2560]{1,0:T(8,128)(2,1)S(1)}, bf16[8,2560]{1,0:T(8,128)(2,1)S(1)}, u32[]{:S(2)}, u32[]{:S(2)}) collective-permute-start(bf16[8,2560]{1,0:T(8,128)(2,1)S(1)} %head.1), channel_id=1, source_target_pairs={{8,0},{12,4},{16,8},{20,12},{24,16},{28,20},{32,24},{36,28},{40,32... | collective-permute-start | bytes 122888 | tf_op jit(solution)/shard_map/ppermute | solution.py:643
  87.7 3.9 %collective-permute-start.21 = (bf16[128,2688]{1,0:T(8,128)(2,1)S(1)}, bf16[128,2688]{1,0:T(8,128)(2,1)S(1)}, u32[]{:S(2)}, u32[]{:S(2)}) collective-permute-start(bf16[128,2688]{1,0:T(8,128)(2,1)S(1)} %get-tuple-element.165), channel_id=1, source_target_pairs={{0,4},{4,0},{8,12},{12,8},{16,20},{20,16},{24,28},{28,24},{32,36},... | collective-permute-start | bytes 2064392 | tf_op jit(solution)/shard_map/ppermute | solution.py:643
  (8 other events, 84.4 us)
